TPU v7x, 32 devices: a whole 2x2x4 slice. The times are simulated.
32 devices in a mesh: dp: 2 (over y), expert: 16 (over z, x, core).
Axes of the slice: x: 2, y: 2, z: 4, core: 2. Of those that a mesh axis runs over, the one named last changes fastest.
Arguments:
- tokens: bfloat16 [2, 2, 1024, 2048], P(None, 'dp', 'expert'), may hold values from -6 to 6
- grad_out: bfloat16 [2, 2, 1024, 2048], P(None, 'dp', 'expert'), may hold values from -6 to 6
- segments: int32 [2, 2, 1024], P(None, 'dp'), may hold values from 0 to 3, never falling along the last dimension, each value on 1 to 512 neighbouring positions
- routes: int32 [2, 2, 1024, 6], P(None, 'dp', 'expert'), may hold values from 0 to 15, all different within a row; in each aligned block of 64 rows (0 to 63, 64 to 127, ..., all dimensions but the last counted through in order) at most 32 rows name the same one
- gates: float32 [2, 2, 1024, 6], P(None, 'dp', 'expert'), may hold values from 0.05 to 0.45
- attn_gain: bfloat16 [2048], P('dp'), may hold values from 0.5 to 1.5
- w_query: bfloat16 [2048, 3072], P('dp'), may hold values from -0.125 to 0.125
- w_kv_down: bfloat16 [2048, 576], P('dp'), may hold values from -0.125 to 0.125
- kv_gain: bfloat16 [512], P('dp'), may hold values from 0.5 to 1.5
- w_kv_up: bfloat16 [512, 4096], P('dp'), may hold values from -0.25 to 0.25
- w_out: bfloat16 [2048, 2048], P('dp'), may hold values from -0.375 to 0.375
- ffn_gain: bfloat16 [2048], P('dp'), may hold values from 0.5 to 1.5
- w_shared_in: bfloat16 [2048, 5632], P('dp'), may hold values from -0.125 to 0.125
- w_shared_out: bfloat16 [2816, 2048], P('dp'), may hold values from -0.109375 to 0.109375
- w_expert_in: bfloat16 [16, 2048, 2816], P('expert', 'dp'), may hold values from -0.125 to 0.125
- w_expert_out: bfloat16 [16, 1408, 2048], P('expert', 'dp'), may hold values from -0.15625 to 0.15625
Outputs:
- mixed: bfloat16 [2, 2, 1024, 2048], P(None, 'dp', 'expert')
- input_grad: float32 [2, 2, 1024, 2048], P(None, 'dp', 'expert')
- attn_gain_grad: float32 [2048], P('dp')
- w_query_grad: float32 [2048, 3072], P('dp')
- w_kv_down_grad: float32 [2048, 576], P('dp')
- kv_gain_grad: float32 [512], P('dp')
- w_kv_up_grad: float32 [512, 4096], P('dp')
- w_out_grad: float32 [2048, 2048], P('dp')
- ffn_gain_grad: float32 [2048], P('dp')
- w_shared_in_grad: float32 [2048, 5632], P('dp')
- w_shared_out_grad: float32 [2816, 2048], P('dp')
- w_expert_in_grad: float32 [16, 2048, 2816], P('expert', 'dp')
- w_expert_out_grad: float32 [16, 1408, 2048], P('expert', 'dp')
Inputs may be any that keep to these rules, and one draw needn't show every extreme that they name: `routes`: within the tokens of one device in one micro-batch (aligned blocks of 64 rows in the order micro-batch, sequence, position) no expert is named more than 32 times, a bound that some block reaches. A token names 6 different experts. `segments`: document numbers never fall along a sequence; a document may cross the positions of several devices.
All inputs are finite; a program needn't handle non-finite values.
Results may differ from a plain program's by a relative error of at most 0.018.
Values may be sent and summed in bfloat16 or wider, within the bound.
No kernel may reach another device: no remote copies, remote signals or barrier semaphores. Data moves between devices by JAX's collectives and lax.ppermute only.
A program may use at most 576 MiB of HBM per device.

v0:
```python
import jax
import jax.numpy as jnp
from jax import lax
from jax.sharding import PartitionSpec as P

HEADS = 16
NOPE = 128
ROPE = 64
VDIM = 128
LATENT = 512


theta_base = 50000.0
eps_norm = 1e-06
highest = lax.Precision.HIGHEST


def rope_tables(length, width):
    half = width // 2
    freq = theta_base ** (-2.0 * jnp.arange(half, dtype=jnp.float32) / width)
    angle = jnp.arange(length, dtype=jnp.float32)[:, None] * freq[None, :]
    cosine = jnp.concatenate([jnp.cos(angle), jnp.cos(angle)], -1)
    sine = jnp.concatenate([jnp.sin(angle), jnp.sin(angle)], -1)
    return (cosine, sine)


def rotate(value, cosine, sine):
    half = value.shape[-1] // 2
    turned = jnp.concatenate([-value[..., half:], value[..., :half]], -1)
    return value * cosine + turned * sine


def normed(value, gain):
    return (
        value
        * lax.rsqrt(jnp.mean(value * value, -1, keepdims=True) + eps_norm)
        * gain.astype(jnp.float32)
    )


def swiglu(packed):
    half = packed.shape[-1] // 2
    return jax.nn.silu(packed[..., :half]) * packed[..., half:]


def matmul(left, right):
    return jnp.dot(left, right, preferred_element_type=jnp.float32)


def left_t_right(left, right):
    return lax.dot_general(
        left, right, (((0,), (0,)), ((), ())), preferred_element_type=jnp.float32
    )


def left_right_t(left, right):
    return lax.dot_general(
        left, right, (((1,), (1,)), ((), ())), preferred_element_type=jnp.float32
    )


def accumulate(total, term):
    if total is None:
        return term
    return total + term


def attention_scores(query_nope, query_rope, key_nope, rope_all, allowed, scale):
    raw = jnp.einsum("thd,shd->hts", query_nope, key_nope, preferred_element_type=jnp.float32)
    raw = raw + jnp.einsum("thr,sr->hts", query_rope, rope_all, preferred_element_type=jnp.float32)
    return jnp.where(allowed[None], raw * scale, -1e30)


def per_device(
    tokens,
    grad_out,
    segments,
    routes,
    gates,
    attn_gain,
    w_query,
    w_kv_down,
    kv_gain,
    w_kv_up,
    w_out,
    ffn_gain,
    w_shared_in,
    w_shared_out,
    w_expert_in,
    w_expert_out,
):
    micro_count = tokens.shape[0]
    local_rows = tokens.shape[2]
    model_width = tokens.shape[3]
    groups = lax.axis_size("expert")
    top_count = routes.shape[3]
    seq_length = local_rows * groups
    capacity = max(2, local_rows * top_count * 4 // (3 * groups))
    entries = local_rows * top_count
    first_row = lax.axis_index("expert") * local_rows
    key_cos, key_sin = rope_tables(seq_length, ROPE)
    query_cos = lax.dynamic_slice_in_dim(key_cos, first_row, local_rows, 0)
    query_sin = lax.dynamic_slice_in_dim(key_sin, first_row, local_rows, 0)
    key_places = jnp.arange(seq_length, dtype=jnp.int32)
    query_places = first_row + jnp.arange(local_rows, dtype=jnp.int32)
    scale = (NOPE + ROPE) ** (-0.5)
    owner_rows = jnp.arange(entries, dtype=jnp.int32) // top_count
    expert_ids = jnp.arange(groups, dtype=jnp.int32)

    def rotate_query(value):
        return rotate(value, query_cos[:, None, :], query_sin[:, None, :])

    def rotate_key(value):
        return rotate(value, query_cos, query_sin)

    grad_attn_gain = None
    grad_query = None
    grad_kv_down = None
    grad_kv_gain = None
    grad_kv_up = None
    grad_out_proj = None
    grad_ffn_gain = None
    grad_shared_in = None
    grad_shared_out = None
    grad_expert_in = None
    grad_expert_out = None
    outputs = []
    input_grads = []
    for micro_index in range(micro_count):
        attn_set = (
            lax.all_gather(attn_gain, "dp", axis=0, tiled=True),
            lax.all_gather(w_query, "dp", axis=0, tiled=True),
            lax.all_gather(w_kv_down, "dp", axis=0, tiled=True),
            lax.all_gather(kv_gain, "dp", axis=0, tiled=True),
            lax.all_gather(w_kv_up, "dp", axis=0, tiled=True),
            lax.all_gather(w_out, "dp", axis=0, tiled=True),
        )
        gain_attn, query_weight, down_weight, gain_kv, up_weight, out_weight = attn_set
        hidden_in = tokens[micro_index, 0].astype(jnp.float32)
        seg_all = segments[micro_index, 0]
        seg_query = lax.dynamic_slice_in_dim(seg_all, first_row, local_rows, 0)
        allowed = (seg_query[:, None] == seg_all[None, :]) & (
            key_places[None, :] <= query_places[:, None]
        )
        normed_in = normed(hidden_in, gain_attn).astype(jnp.bfloat16)
        query_full = matmul(normed_in, query_weight).reshape(local_rows, HEADS, NOPE + ROPE)
        query_nope = query_full[..., :NOPE].astype(jnp.bfloat16)
        query_rope_raw = query_full[..., NOPE:]
        query_rope = rotate_query(query_rope_raw).astype(jnp.bfloat16)
        kv_full = matmul(normed_in, down_weight)
        latent_raw = kv_full[:, :LATENT]
        key_rope_raw = kv_full[:, LATENT:]
        latent = normed(latent_raw, gain_kv).astype(jnp.bfloat16)
        key_rope = rotate_key(key_rope_raw).astype(jnp.bfloat16)
        expanded = matmul(latent, up_weight).astype(jnp.bfloat16)
        expanded_all, rope_all = (
            lax.all_gather(expanded, "expert", axis=0, tiled=True),
            lax.all_gather(key_rope, "expert", axis=0, tiled=True),
        )
        kv_heads = expanded_all.reshape(seq_length, HEADS, NOPE + VDIM)
        key_nope = kv_heads[..., :NOPE]
        values = kv_heads[..., NOPE:]
        score = attention_scores(query_nope, query_rope, key_nope, rope_all, allowed, scale)
        row_top = jnp.max(score, -1, keepdims=True)
        expo = jnp.exp(score - row_top)
        totals = jnp.sum(expo, -1, keepdims=True)
        log_total = row_top + jnp.log(totals)
        probs = (expo / totals).astype(jnp.bfloat16)
        attended = jnp.einsum("hts,shd->thd", probs, values, preferred_element_type=jnp.float32)
        attended = attended.reshape(local_rows, HEADS * VDIM).astype(jnp.bfloat16)
        first_sum = hidden_in + matmul(attended, out_weight)
        ffn_set = (
            lax.all_gather(ffn_gain, "dp", axis=0, tiled=True),
            lax.all_gather(w_shared_in, "dp", axis=0, tiled=True),
            lax.all_gather(w_shared_out, "dp", axis=0, tiled=True),
            lax.all_gather(w_expert_in, "dp", axis=1, tiled=True),
            lax.all_gather(w_expert_out, "dp", axis=1, tiled=True),
        )
        gain_ffn, shared_in, shared_down, expert_in, expert_down = ffn_set
        ffn_in = normed(first_sum, gain_ffn).astype(jnp.bfloat16)
        shared_pre = matmul(ffn_in, shared_in)
        shared_act = swiglu(shared_pre).astype(jnp.bfloat16)
        shared_out = matmul(shared_act, shared_down)
        chosen = routes[micro_index, 0].reshape(entries)
        gate_flat = gates[micro_index, 0].reshape(entries)
        one_hot = (chosen[:, None] == expert_ids[None, :]).astype(jnp.float32)
        earlier = jnp.cumsum(one_hot, 0) - one_hot
        slots = jnp.sum(earlier * one_hot, 1).astype(jnp.int32)
        places = chosen * capacity + slots
        sending = (
            jnp.zeros((groups * capacity, model_width), jnp.bfloat16)
            .at[places]
            .set(ffn_in[owner_rows])
        )
        arrived = lax.all_to_all(
            sending.reshape(groups, capacity, model_width),
            "expert",
            split_axis=0,
            concat_axis=0,
            tiled=True,
        )
        arrived = arrived.reshape(groups * capacity, model_width)
        expert_pre = matmul(arrived, expert_in[0])
        expert_act = swiglu(expert_pre).astype(jnp.bfloat16)
        expert_out = matmul(expert_act, expert_down[0]).astype(jnp.bfloat16)
        returned = lax.all_to_all(
            expert_out.reshape(groups, capacity, model_width),
            "expert",
            split_axis=0,
            concat_axis=0,
            tiled=True,
        )
        returned = returned.reshape(groups * capacity, model_width)
        picked = returned[places].astype(jnp.float32) * gate_flat[:, None]
        routed = jnp.sum(picked.reshape(local_rows, top_count, model_width), 1)
        outputs.append((first_sum + shared_out + routed).astype(jnp.bfloat16))
        ffn_set = (
            lax.all_gather(ffn_gain, "dp", axis=0, tiled=True),
            lax.all_gather(w_shared_in, "dp", axis=0, tiled=True),
            lax.all_gather(w_shared_out, "dp", axis=0, tiled=True),
            lax.all_gather(w_expert_in, "dp", axis=1, tiled=True),
            lax.all_gather(w_expert_out, "dp", axis=1, tiled=True),
        )
        gain_ffn, shared_in, shared_down, expert_in, expert_down = ffn_set
        grad_y = grad_out[micro_index, 0].astype(jnp.float32)
        grad_rows = (grad_y[owner_rows] * gate_flat[:, None]).astype(jnp.bfloat16)
        grad_send = (
            jnp.zeros((groups * capacity, model_width), jnp.bfloat16).at[places].set(grad_rows)
        )
        grad_arrived = lax.all_to_all(
            grad_send.reshape(groups, capacity, model_width),
            "expert",
            split_axis=0,
            concat_axis=0,
            tiled=True,
        )
        grad_arrived = grad_arrived.reshape(groups * capacity, model_width)
        grad_expert_out = accumulate(grad_expert_out, left_t_right(expert_act, grad_arrived)[None])
        grad_eact = left_right_t(grad_arrived, expert_down[0])
        _, expert_pull = jax.vjp(swiglu, expert_pre)
        grad_epre = expert_pull(grad_eact)[0].astype(jnp.bfloat16)
        grad_expert_in = accumulate(grad_expert_in, left_t_right(arrived, grad_epre)[None])
        grad_einput = left_right_t(grad_epre, expert_in[0]).astype(jnp.bfloat16)
        grad_back = lax.all_to_all(
            grad_einput.reshape(groups, capacity, model_width),
            "expert",
            split_axis=0,
            concat_axis=0,
            tiled=True,
        )
        grad_back = grad_back.reshape(groups * capacity, model_width)
        grad_ffn_in = jnp.sum(
            grad_back[places].astype(jnp.float32).reshape(local_rows, top_count, model_width), 1
        )
        grad_low = grad_y.astype(jnp.bfloat16)
        grad_shared_out = accumulate(grad_shared_out, left_t_right(shared_act, grad_low))
        grad_sact = left_right_t(grad_low, shared_down)
        _, shared_pull = jax.vjp(swiglu, shared_pre)
        grad_spre = shared_pull(grad_sact)[0].astype(jnp.bfloat16)
        grad_shared_in = accumulate(grad_shared_in, left_t_right(ffn_in, grad_spre))
        grad_ffn_in = grad_ffn_in + left_right_t(grad_spre, shared_in)
        _, ffn_norm_pull = jax.vjp(normed, first_sum, gain_ffn.astype(jnp.float32))
        grad_first_norm, grad_gain_ffn = ffn_norm_pull(grad_ffn_in)
        grad_ffn_gain = accumulate(grad_ffn_gain, grad_gain_ffn)
        grad_first = grad_y + grad_first_norm
        attn_set = (
            lax.all_gather(attn_gain, "dp", axis=0, tiled=True),
            lax.all_gather(w_query, "dp", axis=0, tiled=True),
            lax.all_gather(w_kv_down, "dp", axis=0, tiled=True),
            lax.all_gather(kv_gain, "dp", axis=0, tiled=True),
            lax.all_gather(w_kv_up, "dp", axis=0, tiled=True),
            lax.all_gather(w_out, "dp", axis=0, tiled=True),
        )
        gain_attn, query_weight, down_weight, gain_kv, up_weight, out_weight = attn_set
        grad_attn_low = grad_first.astype(jnp.bfloat16)
        grad_out_proj = accumulate(grad_out_proj, left_t_right(attended, grad_attn_low))
        grad_attended = (
            left_right_t(grad_attn_low, out_weight)
            .astype(jnp.bfloat16)
            .reshape(local_rows, HEADS, VDIM)
        )
        score = attention_scores(query_nope, query_rope, key_nope, rope_all, allowed, scale)
        probs_full = jnp.exp(score - log_total)
        probs_low = probs_full.astype(jnp.bfloat16)
        grad_values = jnp.einsum(
            "hts,thd->shd", probs_low, grad_attended, preferred_element_type=jnp.float32
        )
        grad_probs = jnp.einsum(
            "thd,shd->hts", grad_attended, values, preferred_element_type=jnp.float32
        )
        row_delta = jnp.sum(probs_full * grad_probs, -1, keepdims=True)
        grad_score = (probs_full * (grad_probs - row_delta) * scale).astype(jnp.bfloat16)
        grad_qnope = jnp.einsum(
            "hts,shd->thd", grad_score, key_nope, preferred_element_type=jnp.float32
        )
        grad_qrope = jnp.einsum(
            "hts,sr->thr", grad_score, rope_all, preferred_element_type=jnp.float32
        )
        grad_knope = jnp.einsum(
            "hts,thd->shd", grad_score, query_nope, preferred_element_type=jnp.float32
        )
        grad_krope = jnp.einsum(
            "hts,thr->sr", grad_score, query_rope, preferred_element_type=jnp.float32
        )
        grad_partial = (
            jnp.concatenate([grad_knope, grad_values], -1)
            .reshape(seq_length, HEADS * (NOPE + VDIM))
            .astype(jnp.bfloat16)
        )
        grad_partial = lax.optimization_barrier(grad_partial)
        own_expanded, own_krope = (
            lax.psum_scatter(
                grad_partial.astype(jnp.float32).astype(jnp.bfloat16),
                "expert",
                scatter_dimension=0,
                tiled=True,
            ).astype(jnp.float32),
            lax.psum_scatter(
                grad_krope.astype(jnp.bfloat16), "expert", scatter_dimension=0, tiled=True
            ).astype(jnp.float32),
        )
        grad_kv_up = accumulate(
            grad_kv_up,
            lax.dot_general(
                latent.astype(jnp.float32),
                own_expanded,
                (((0,), (0,)), ((), ())),
                precision=highest,
            ),
        )
        grad_latent = lax.dot_general(
            own_expanded, up_weight.astype(jnp.float32), (((1,), (1,)), ((), ())), precision=highest
        )
        _, latent_pull = jax.vjp(normed, latent_raw, gain_kv.astype(jnp.float32))
        grad_latent_raw, grad_gain_kv = latent_pull(grad_latent)
        grad_kv_gain = accumulate(grad_kv_gain, grad_gain_kv)
        _, krope_pull = jax.vjp(rotate_key, key_rope_raw)
        grad_krope_raw = krope_pull(own_krope)[0]
        grad_kv_full = jnp.concatenate([grad_latent_raw, grad_krope_raw], -1).astype(jnp.bfloat16)
        grad_kv_down = accumulate(grad_kv_down, left_t_right(normed_in, grad_kv_full))
        grad_normed = left_right_t(grad_kv_full, down_weight)
        _, qrope_pull = jax.vjp(rotate_query, query_rope_raw)
        grad_qrope_raw = qrope_pull(grad_qrope)[0]
        grad_query_full = (
            jnp.concatenate([grad_qnope, grad_qrope_raw], -1)
            .reshape(local_rows, HEADS * (NOPE + ROPE))
            .astype(jnp.bfloat16)
        )
        grad_query = accumulate(grad_query, left_t_right(normed_in, grad_query_full))
        grad_normed = grad_normed + left_right_t(grad_query_full, query_weight)
        _, input_pull = jax.vjp(normed, hidden_in, gain_attn.astype(jnp.float32))
        grad_input_norm, grad_gain_attn = input_pull(grad_normed)
        grad_attn_gain = accumulate(grad_attn_gain, grad_gain_attn)
        input_grads.append(grad_first + grad_input_norm)
    shards = (
        lax.psum_scatter(grad_attn_gain, "dp", scatter_dimension=0, tiled=True),
        lax.psum_scatter(grad_query, "dp", scatter_dimension=0, tiled=True),
        lax.psum_scatter(grad_kv_down, "dp", scatter_dimension=0, tiled=True),
        lax.psum_scatter(grad_kv_gain, "dp", scatter_dimension=0, tiled=True),
        lax.psum_scatter(grad_kv_up, "dp", scatter_dimension=0, tiled=True),
        lax.psum_scatter(grad_out_proj, "dp", scatter_dimension=0, tiled=True),
        lax.psum_scatter(grad_ffn_gain, "dp", scatter_dimension=0, tiled=True),
        lax.psum_scatter(grad_shared_in, "dp", scatter_dimension=0, tiled=True),
        lax.psum_scatter(grad_shared_out, "dp", scatter_dimension=0, tiled=True),
        lax.psum_scatter(grad_expert_in, "dp", scatter_dimension=1, tiled=True),
        lax.psum_scatter(grad_expert_out, "dp", scatter_dimension=1, tiled=True),
    )
    dense = lax.psum(
        (
            shards[0],
            shards[1],
            shards[2],
            shards[3],
            shards[4],
            shards[5],
            shards[6],
            shards[7],
            shards[8],
        ),
        "expert",
    )
    mixed = jnp.stack(outputs)[:, None]
    input_grad = jnp.stack(input_grads)[:, None]
    return (
        mixed,
        input_grad,
        dense[0],
        dense[1],
        dense[2],
        dense[3],
        dense[4],
        dense[5],
        dense[6],
        dense[7],
        dense[8],
        shards[9],
        shards[10],
    )


def solution(mesh):
    in_specs = (
        P(None, "dp", "expert", None),
        P(None, "dp", "expert", None),
        P(None, "dp", None),
        P(None, "dp", "expert", None),
        P(None, "dp", "expert", None),
        P("dp"),
        P("dp", None),
        P("dp", None),
        P("dp"),
        P("dp", None),
        P("dp", None),
        P("dp"),
        P("dp", None),
        P("dp", None),
        P("expert", "dp", None),
        P("expert", "dp", None),
    )
    out_specs = (
        P(None, "dp", "expert", None),
        P(None, "dp", "expert", None),
        P("dp"),
        P("dp", None),
        P("dp", None),
        P("dp"),
        P("dp", None),
        P("dp", None),
        P("dp"),
        P("dp", None),
        P("dp", None),
        P("expert", "dp", None),
        P("expert", "dp", None),
    )
    return jax.shard_map(
        per_device, mesh=mesh, in_specs=in_specs, out_specs=out_specs, check_vma=False
    )
```

profile of v0, /device:TPU:1, one launch (start us, length us, event | category | flops | bytes accessed | tf_op | source)
XLA Modules:
  0.0 4699.2 jit_solution(5950649930636337833)
XLA Ops:
  16.6 30.9 all-gather.12.cloned.1.call-done
  50.2 55.7 %all-gather.14.cloned.1.call-done = bf16[512,4096]{1,0:T(8,128)(2,1)} async-done(((bf16[256,4096]{1,0:T(8,128)(2,1)}), bf16[512,4096]{1,0:T(8,128)(2,1)}) %all-gather.14.cloned.1.call-update) | async-done | bytes 4194320 | tf_op jit(solution)/shard_map/all_gather | solution.py:135
  127.3 25.6 all_gather.36
  152.9 107.1 %all-gather.18.cloned.1.call-done = bf16[2048,3072]{1,0:T(8,128)(2,1)} async-done(((bf16[1024,3072]{1,0:T(8,128)(2,1)}), bf16[2048,3072]{1,0:T(8,128)(2,1)}) %all-gather.18.cloned.1.call-update) | async-done | bytes 12582928 | tf_op jit(solution)/shard_map/all_gather | solution.py:132
  260.0 16.7 copy.78
  290.6 46.9 all-gather.16.cloned.1.call-done
  337.5 10.9 copy.130
  362.6 78.3 %all-gather.20.cloned.1.call-done = bf16[2048,2048]{1,0:T(8,128)(2,1)} async-done(((bf16[1024,2048]{1,0:T(8,128)(2,1)}), bf16[2048,2048]{1,0:T(8,128)(2,1)}) %all-gather.20.cloned.1.call-update) | async-done | bytes 8388624 | tf_op jit(solution)/shard_map/all_gather | solution.py:136
  472.7 55.2 %all-to-all-done = bf16[16,32,2048]{2,1,0:T(8,128)(2,1)} async-done(((bf16[16,32,2048]{2,1,0:T(8,128)(2,1)}), bf16[16,32,2048]{2,1,0:T(8,128)(2,1)}, u32[]{:S(2)}, u32[]{:S(2)}) %all-to-all-start) | async-done | bytes 2097184 | tf_op jit(solution)/shard_map/all_to_all | solution.py:195
  527.9 26.3 all-to-all-start.4
  556.5 52.7 %all_gather.44 = bf16[1024,64]{1,0:T(8,128)(2,1)S(1)} all-gather(bf16[64,64]{1,0:T(8,128)(2,1)S(1)} %fusion.271), channel_id=1, replica_groups=mesh['dp'=2,'expert'=16] {'expert'}, dimensions={0}, use_global_device_ids=true | all-gather | bytes 139264 | tf_op jit(solution)/shard_map/all_gather | solution.py:158
  609.2 10.0 copy.131
  630.5 64.1 %all-gather.26.cloned.1.call-done = bf16[1,2048,2816]{2,1,0:T(8,128)(2,1)} async-done(((bf16[1,1024,2816]{2,1,0:T(8,128)(2,1)}), bf16[1,2048,2816]{2,1,0:T(8,128)(2,1)}) %all-gather.26.cloned.1.call-update) | async-done | bytes 11534352 | tf_op jit(solution)/shard_map/all_gather | solution.py:176
  694.6 12.5 fusion.8
  707.1 63.5 %all-gather.28.cloned.1.call-done = bf16[1,1408,2048]{2,1,0:T(8,128)(2,1)} async-done(((bf16[1,704,2048]{2,1,0:T(8,128)(2,1)}), bf16[1,1408,2048]{2,1,0:T(8,128)(2,1)}) %all-gather.28.cloned.1.call-update) | async-done | bytes 5767184 | tf_op jit(solution)/shard_map/all_gather | solution.py:177
  770.6 12.4 fusion.197
  783.1 10.2 fusion.48
  812.2 230.4 %all-gather.22.cloned.1.call-done = bf16[2048,5632]{1,0:T(8,128)(2,1)} async-done(((bf16[1024,5632]{1,0:T(8,128)(2,1)}), bf16[2048,5632]{1,0:T(8,128)(2,1)}) %all-gather.22.cloned.1.call-update) | async-done | bytes 23068688 | tf_op jit(solution)/shard_map/all_gather | solution.py:174
  1042.6 12.8 fusion.339
  1055.4 129.6 %all-gather.24.cloned.1.call-done = bf16[2816,2048]{1,0:T(8,128)(2,1)} async-done(((bf16[1408,2048]{1,0:T(8,128)(2,1)}), bf16[2816,2048]{1,0:T(8,128)(2,1)}) %all-gather.24.cloned.1.call-update) | async-done | bytes 11534352 | tf_op jit(solution)/shard_map/all_gather | solution.py:175
  1205.4 13.1 multiply_reduce_fusion.5
  1242.1 33.9 all-to-all-done.2
  1276.0 11.2 all-to-all-start.6
  1287.2 11.1 fusion.6
  1298.3 30.4 all-to-all-done.6
  1328.7 10.4 fusion.198
  1339.0 12.1 fusion.51
  1351.2 10.9 all-to-all-start.7
  1362.4 10.0 fusion.340
  1377.3 26.5 all-to-all-done.7
  1419.1 12.7 multiply_reduce_fusion.4
  1443.3 10.6 fusion.133
  1453.9 13.9 convert_bitcast_fusion.1
  1484.2 10.2 fusion.130
  1502.8 12.1 copy.118
  1516.1 14.1 convert_bitcast_fusion.3
  1544.0 11.9 copy.116
  1556.0 45.5 reduce-scatter.19.cloned.1.call-done
  1603.3 106.9 %reduce-scatter.39.cloned.1.call-done = bf16[64,4096]{1,0:T(8,128)(2,1)} async-done(((bf16[1024,4096]{1,0:T(8,128)(2,1)}), bf16[64,4096]{1,0:T(8,128)(2,1)}) %reduce-scatter.39.cloned.1.call-update) | async-done | bytes 524304
  1714.0 103.9 %reduce-scatter.37.cloned.1.call-done = bf16[64,4096]{1,0:T(8,128)(2,1)} async-done(((bf16[1024,4096]{1,0:T(8,128)(2,1)}), bf16[64,4096]{1,0:T(8,128)(2,1)}) %reduce-scatter.37.cloned.1.call-update) | async-done | bytes 524304
  1846.9 9.9 fusion.215
  1856.8 16.2 convolution_add_fusion.1
  1891.2 14.1 fusion.120
  1906.3 13.8 fusion.125
  1921.1 10.7 fusion.224
  1931.8 17.4 convolution_add_fusion.2
  1950.6 18.8 fusion.246
  1969.4 29.7 convolution_add_fusion
  2005.4 9.7 add_bitcast_fusion.1
  2015.4 14.5 fusion.196
  2030.0 17.3 add_bitcast_fusion
  2047.4 132.6 %reduce-scatter.29.cloned.1.call-done = f32[1024,2048]{1,0:T(8,128)} async-done(((f32[2048,2048]{1,0:T(8,128)}), f32[1024,2048]{1,0:T(8,128)}) %reduce-scatter.29.cloned.1.call-update) | async-done | bytes 8388624 | tf_op jit(solution)/shard_map/reduce_scatter | solution.py:361
  2180.0 259.6 %reduce-scatter.31.cloned.1.call-done = f32[1408,2048]{1,0:T(8,128)} async-done(((f32[2816,2048]{1,0:T(8,128)}), f32[1408,2048]{1,0:T(8,128)}) %reduce-scatter.31.cloned.1.call-update) | async-done | bytes 11534352 | tf_op jit(solution)/shard_map/reduce_scatter | solution.py:364
  2439.6 281.7 %reduce-scatter.23.cloned.1.call-done = f32[1024,3072]{1,0:T(8,128)} async-done(((f32[2048,3072]{1,0:T(8,128)}), f32[1024,3072]{1,0:T(8,128)}) %reduce-scatter.23.cloned.1.call-update) | async-done | bytes 12582928 | tf_op jit(solution)/shard_map/reduce_scatter | solution.py:357
  2721.3 506.2 %reduce-scatter.41.cloned.1.call-done = f32[1024,5632]{1,0:T(8,128)} async-done(((f32[2048,5632]{1,0:T(8,128)}), f32[1024,5632]{1,0:T(8,128)}) %reduce-scatter.41.cloned.1.call-update) | async-done | bytes 23068688
  3249.6 34.3 all-to-all-done.1
  3285.3 11.2 all-to-all-start.3
  3319.6 18.2 all-to-all-done.3
  3375.9 37.7 all-reduce.20
  3416.1 207.5 %reduce-scatter.33.cloned.1.call-done = f32[1,1024,2816]{2,1,0:T(8,128)} async-done(((f32[1,2048,2816]{2,1,0:T(8,128)}), f32[1,1024,2816]{2,1,0:T(8,128)}) %reduce-scatter.33.cloned.1.call-update) | async-done | bytes 11534352 | tf_op jit(solution)/shard_map/reduce_scatter | solution.py:365
  3623.7 1019.6 %all-reduce.25.cloned.1.call-done = (f32[1024,3072]{1,0:T(8,128)}, f32[1024,576]{0,1:T(8,128)}, f32[256,4096]{1,0:T(8,128)}, f32[1024,2048]{1,0:T(8,128)}, f32[1024,5632]{1,0:T(8,128)}, /*index=5*/f32[1408,2048]{1,0:T(8,128)}) async-done(((f32[1024,3072]{1,0:T(8,128)}, f32[1024,576]{0,1:T(8,128)}, f32[256,4096]{1,0:T(8,128)}, f32[1024,2048]{1,0:T(8,128)}, f32[1024,5632]{1,0:T(8,128)}, ...) | async-done | bytes 62128144 | tf_op jit(solution)/shard_map/psum | solution.py:368
  4643.3 11.1 copy.204
  4665.8 16.0 copy.208
  4681.8 10.6 copy.209
  (571 shorter events, 399.6 us)
Async XLA Ops:
  7.2 40.3 all-gather.12.cloned.1.call-start
  7.9 97.9 %all-gather.14.cloned.1.call-start = ((), (), s32[]{:S(2)}) async-start(), calls=%async_computation.21 | async-start | bytes 6291456 | tf_op jit(solution)/shard_map/all_gather | solution.py:135
  8.7 251.3 %all-gather.18.cloned.1.call-start = ((), (), s32[]{:S(2)}) async-start(), calls=%async_computation.23 | async-start | bytes 18874368 | tf_op jit(solution)/shard_map/all_gather | solution.py:132
  9.4 328.0 %all-gather.16.cloned.1.call-start = ((), (), s32[]{:S(2)}) async-start(), calls=%async_computation.22 | async-start | bytes 8912896 | tf_op jit(solution)/shard_map/all_gather | solution.py:157
  13.2 98.4 %copy-start.99 = (f32[2,1,256]{2,1,0:T(1,128)}, f32[2,1,256]{2,1,0:T(1,128)S(1)}, u32[]{:S(2)}) copy-start(f32[2,1,256]{2,1,0:T(1,128)S(1)} %convert_element_type.409) | copy-start | bytes 6148
  16.4 269.4 %copy-start.73 = (f32[2048]{0:T(1024)}, f32[2048]{0:T(1024)S(1)}, u32[]{:S(2)}) copy-start(f32[2048]{0:T(1024)S(1)} %convert_element_type.320) | copy-start | bytes 24580
  16.6 94.0 %copy-start.149 = (f32[64]{0:T(128)}, f32[64]{0:T(128)S(1)}, u32[]{:S(2)}) copy-start(f32[64]{0:T(128)S(1)} %get-tuple-element.63) | copy-start | bytes 772
  16.6 260.0 %copy-start.118 = (f32[64]{0:T(128)}, f32[64]{0:T(128)S(1)}, u32[]{:S(2)}) copy-start(f32[64]{0:T(128)S(1)} %fusion.303) | copy-start | bytes 772
  109.9 330.9 %all-gather.20.cloned.1.call-start = ((), (), s32[]{:S(2)}) async-start(), calls=%async_computation.24 | async-start | bytes 12582912 | tf_op jit(solution)/shard_map/all_gather | solution.py:136
  110.5 498.7 %all-gather.30.cloned.1.call-start = ((), (), s32[]{:S(2)}) async-start(), calls=%async_computation.29 | async-start | bytes 8912896 | tf_op jit(solution)/shard_map/all_gather | solution.py:157
  110.6 175.2 %copy-start.115 = (f32[64]{0:T(128)}, f32[64]{0:T(128)S(1)}, u32[]{:S(2)}) copy-start(f32[64]{0:T(128)S(1)} %fusion.306) | copy-start | bytes 772
  111.5 444.9 %copy-start.48 = (f32[64,576]{1,0:T(8,128)}, f32[64,576]{1,0:T(8,128)S(1)}, u32[]{:S(2)}) copy-start(f32[64,576]{1,0:T(8,128)S(1)} %fusion.260) | copy-start | bytes 442372
  115.5 579.1 %all-gather.26.cloned.1.call-start = ((), (), s32[]{:S(2)}) async-start(), calls=%async_computation.27 | async-start | bytes 17301504 | tf_op jit(solution)/shard_map/all_gather | solution.py:176
  116.3 654.3 %all-gather.28.cloned.1.call-start = ((), (), s32[]{:S(2)}) async-start(), calls=%async_computation.28 | async-start | bytes 8650752 | tf_op jit(solution)/shard_map/all_gather | solution.py:177
  117.1 925.5 %all-gather.22.cloned.1.call-start = ((), (), s32[]{:S(2)}) async-start(), calls=%async_computation.25 | async-start | bytes 34603008 | tf_op jit(solution)/shard_map/all_gather | solution.py:174
  127.2 429.1 %copy-start.84 = (f32[64,64]{1,0:T(8,128)}, f32[64,64]{1,0:T(8,128)S(1)}, u32[]{:S(2)}) copy-start(f32[64,64]{1,0:T(8,128)S(1)} %get-tuple-element.81) | copy-start | bytes 49156
  127.2 429.1 %copy-start.90 = (f32[64,64]{1,0:T(8,128)}, f32[64,64]{1,0:T(8,128)S(1)}, u32[]{:S(2)}) copy-start(f32[64,64]{1,0:T(8,128)S(1)} %get-tuple-element.82) | copy-start | bytes 49156
  289.9 335.0 %copy-start.25 = (f32[64,16,192]{2,0,1:T(8,128)}, f32[64,16,192]{2,0,1:T(8,128)S(1)}, u32[]{:S(2)}) copy-start(f32[64,16,192]{2,0,1:T(8,128)S(1)} %fusion.208) | copy-start | bytes 2359300
  290.6 337.0 %copy-start.78 = (bf16[64,16,64]{2,0,1:T(8,128)(2,1)}, bf16[64,16,64]{2,0,1:T(8,128)(2,1)S(1)}, u32[]{:S(2)}) copy-start(bf16[64,16,64]{2,0,1:T(8,128)(2,1)S(1)} %get-tuple-element.118) | copy-start | bytes 393220
  456.3 71.6 %all-to-all-start = ((bf16[16,32,2048]{2,1,0:T(8,128)(2,1)}), bf16[16,32,2048]{2,1,0:T(8,128)(2,1)}, u32[]{:S(2)}, u32[]{:S(2)}) async-start(bf16[16,32,2048]{2,1,0:T(8,128)(2,1)} %bitcast.409), calls=%async_computation | async-start | bytes 4194304 | tf_op jit(solution)/shard_map/all_to_all | solution.py:195
  462.8 722.2 %all-gather.24.cloned.1.call-start = ((), (), s32[]{:S(2)}) async-start(), calls=%async_computation.26 | async-start | bytes 17301504 | tf_op jit(solution)/shard_map/all_gather | solution.py:175
  527.9 179.3 %all-to-all-start.4 = ((bf16[16,32,2048]{2,1,0:T(8,128)(2,1)}), bf16[16,32,2048]{2,1,0:T(8,128)(2,1)}, u32[]{:S(2)}, u32[]{:S(2)}) async-start(bf16[16,32,2048]{2,1,0:T(8,128)(2,1)} %bitcast.408), calls=%async_computation.4 | async-start | bytes 4194304 | tf_op jit(solution)/shard_map/all_to_all | solution.py:230
  555.7 638.8 %copy-start.122 = (s32[1024]{0:T(1024)}, s32[1024]{0:T(1024)S(1)}, u32[]{:S(2)}) copy-start(s32[1024]{0:T(1024)S(1)} %pad_clamp_fusion.1) | copy-start | bytes 12292
  793.2 401.3 %all-to-all-start.5 = ((bf16[16,32,2048]{2,1,0:T(8,128)(2,1)}), bf16[16,32,2048]{2,1,0:T(8,128)(2,1)S(1)}, u32[]{:S(2)}, u32[]{:S(2)}) async-start(bf16[16,32,2048]{2,1,0:T(8,128)(2,1)} %bitcast.413), calls=%async_computation.5 | async-start | bytes 4194304 | tf_op jit(solution)/shard_map/all_to_all | solution.py:244
  812.1 243.3 %copy-start.153 = (f32[64]{0:T(128)}, f32[64]{0:T(128)S(1)}, u32[]{:S(2)}) copy-start(f32[64]{0:T(128)S(1)} %get-tuple-element.154) | copy-start | bytes 772
  812.1 393.2 %copy-start.14 = (f32[64,2048]{1,0:T(8,128)}, f32[64,2048]{1,0:T(8,128)S(1)}, u32[]{:S(2)}) copy-start(f32[64,2048]{1,0:T(8,128)S(1)} %get-tuple-element.155) | copy-start | bytes 1572868
  812.1 393.2 %copy-start.141 = (f32[64]{0:T(128)}, f32[64]{0:T(128)S(1)}, u32[]{:S(2)}) copy-start(f32[64]{0:T(128)S(1)} %fusion.308) | copy-start | bytes 772
  812.1 372.9 %copy-start.33 = (bf16[2,1,64,2048]{3,2,1,0:T(8,128)(2,1)S(1)}, bf16[2,1,64,2048]{3,2,1,0:T(8,128)(2,1)}, u32[]{:S(2)}) copy-start(bf16[2,1,64,2048]{3,2,1,0:T(8,128)(2,1)} %param.17) | copy-start | bytes 1572868
  1227.9 48.1 %all-to-all-start.2 = ((bf16[16,32,2048]{2,1,0:T(8,128)(2,1)}), bf16[16,32,2048]{2,1,0:T(8,128)(2,1)S(1)}, u32[]{:S(2)}, u32[]{:S(2)}) async-start(bf16[16,32,2048]{2,1,0:T(8,128)(2,1)} %bitcast.410), calls=%async_computation.2 | async-start | bytes 4194304 | tf_op jit(solution)/shard_map/all_to_all | solution.py:195
  1276.0 52.7 %all-to-all-start.6 = ((bf16[16,32,2048]{2,1,0:T(8,128)(2,1)}), bf16[16,32,2048]{2,1,0:T(8,128)(2,1)}, u32[]{:S(2)}, u32[]{:S(2)}) async-start(bf16[16,32,2048]{2,1,0:T(8,128)(2,1)} %bitcast.411), calls=%async_computation.7 | async-start | bytes 4194304 | tf_op jit(solution)/shard_map/all_to_all | solution.py:230
  1351.2 52.6 %all-to-all-start.7 = ((bf16[16,32,2048]{2,1,0:T(8,128)(2,1)}), bf16[16,32,2048]{2,1,0:T(8,128)(2,1)}, u32[]{:S(2)}, u32[]{:S(2)}) async-start(bf16[16,32,2048]{2,1,0:T(8,128)(2,1)} %bitcast.414), calls=%async_computation.8 | async-start | bytes 4194304 | tf_op jit(solution)/shard_map/all_to_all | solution.py:244
  1362.1 193.9 %reduce-scatter.21.cloned.1.call-start = ((), (), s32[]{:S(2)}) async-start(), calls=%async_computation.31 | async-start | bytes 278528 | tf_op jit(solution)/shard_map/reduce_scatter | solution.py:318
  1362.2 168.0 %copy-start.111 = (f32[16,64]{1,0:T(8,128)}, f32[16,64]{1,0:T(8,128)S(1)}, u32[]{:S(2)}) copy-start(f32[16,64]{1,0:T(8,128)S(1)} %log_add_fusion.1) | copy-start | bytes 12292
  1362.3 105.5 %copy-start.109 = (f32[16,64]{1,0:T(8,128)}, f32[16,64]{1,0:T(8,128)S(1)}, u32[]{:S(2)}) copy-start(f32[16,64]{1,0:T(8,128)S(1)} %log_add_fusion) | copy-start | bytes 12292
  1377.3 479.6 %copy-start.36 = (bf16[64,2816]{1,0:T(8,128)(2,1)}, bf16[64,2816]{1,0:T(8,128)(2,1)S(1)}, u32[]{:S(2)}) copy-start(bf16[64,2816]{1,0:T(8,128)(2,1)S(1)} %get-tuple-element.98) | copy-start | bytes 1081348
  1432.1 402.3 %copy-start.29 = (f32[64,2048]{1,0:T(8,128)}, f32[64,2048]{1,0:T(8,128)S(1)}, u32[]{:S(2)}) copy-start(f32[64,2048]{1,0:T(8,128)S(1)} %get-tuple-element.105) | copy-start | bytes 1572868
  1432.2 405.5 %copy-start.27 = (f32[64,2048]{1,0:T(8,128)}, f32[64,2048]{1,0:T(8,128)S(1)}, u32[]{:S(2)}) copy-start(f32[64,2048]{1,0:T(8,128)S(1)} %get-tuple-element.106) | copy-start | bytes 1572868
  1484.2 117.3 %reduce-scatter.19.cloned.1.call-start = ((), (), s32[]{:S(2)}) async-start(), calls=%async_computation.30 | async-start | bytes 278528 | tf_op jit(solution)/shard_map/reduce_scatter | solution.py:318
  1494.5 215.8 %reduce-scatter.39.cloned.1.call-start = ((), (), s32[]{:S(2)}) async-start(), calls=%async_computation.40 | async-start | bytes 8912896
  1514.9 303.0 %reduce-scatter.37.cloned.1.call-start = ((), (), s32[]{:S(2)}) async-start(), calls=%async_computation.39 | async-start | bytes 8912896
  1555.9 262.0 %copy-start.47 = (f32[64,576]{1,0:T(8,128)S(1)}, f32[64,576]{1,0:T(8,128)}, u32[]{:S(2)}) copy-start(f32[64,576]{1,0:T(8,128)} %copy-done.46) | copy-start | bytes 442372
  1555.9 262.0 %copy-start.49 = (f32[64,576]{1,0:T(8,128)S(1)}, f32[64,576]{1,0:T(8,128)}, u32[]{:S(2)}) copy-start(f32[64,576]{1,0:T(8,128)} %copy-done.48) | copy-start | bytes 442372
  1555.9 262.0 %copy-start.100 = (f32[2,1,256]{2,1,0:T(1,128)S(1)}, f32[2,1,256]{2,1,0:T(1,128)}, u32[]{:S(2)}) copy-start(f32[2,1,256]{2,1,0:T(1,128)} %copy-done.99) | copy-start | bytes 6148
  1555.9 261.9 %copy-start.127 = (f32[64]{0:T(128)S(1)}, f32[64]{0:T(128)}, u32[]{:S(2)}) copy-start(f32[64]{0:T(128)} %copy-done.126) | copy-start | bytes 772
  1555.9 261.9 %copy-start.134 = (f32[64]{0:T(128)S(1)}, f32[64]{0:T(128)}, u32[]{:S(2)}) copy-start(f32[64]{0:T(128)} %copy-done.133) | copy-start | bytes 772
  1556.0 491.4 %reduce-scatter.25.cloned.1.call-start = ((), (), s32[]{:S(2)}) async-start(), calls=%async_computation.33 | async-start | bytes 7077888 | tf_op jit(solution)/shard_map/reduce_scatter | solution.py:358
  1603.3 219.2 %copy-start.103 = (bf16[64,64]{1,0:T(8,128)(2,1)}, bf16[64,64]{1,0:T(8,128)(2,1)S(1)}, u32[]{:S(2)}) copy-start(bf16[64,64]{1,0:T(8,128)(2,1)S(1)} %get-tuple-element.123) | copy-start | bytes 24580
  1603.3 220.1 %copy-start.101 = (bf16[64,64]{1,0:T(8,128)(2,1)}, bf16[64,64]{1,0:T(8,128)(2,1)S(1)}, u32[]{:S(2)}) copy-start(bf16[64,64]{1,0:T(8,128)(2,1)S(1)} %get-tuple-element.124) | copy-start | bytes 24580
  1603.3 219.0 %copy-start.158 = (f32[64]{0:T(128)S(1)}, f32[64]{0:T(128)}, u32[]{:S(2)}) copy-start(f32[64]{0:T(128)} %copy-done.157) | copy-start | bytes 772
  1603.3 219.0 %copy-start.156 = (f32[64]{0:T(128)S(1)}, f32[64]{0:T(128)}, u32[]{:S(2)}) copy-start(f32[64]{0:T(128)} %copy-done.155) | copy-start | bytes 772
  1603.3 219.2 %copy-start.7 = (bf16[2,1,64,2048]{3,2,1,0:T(8,128)(2,1)S(1)}, bf16[2,1,64,2048]{3,2,1,0:T(8,128)(2,1)}, u32[]{:S(2)}) copy-start(bf16[2,1,64,2048]{3,2,1,0:T(8,128)(2,1)} %param.16) | copy-start | bytes 1572868
  1603.3 219.2 %copy-start.74 = (f32[2048]{0:T(1024)S(1)}, f32[2048]{0:T(1024)}, u32[]{:S(2)}) copy-start(f32[2048]{0:T(1024)} %copy-done.73) | copy-start | bytes 24580
  1603.3 219.2 %copy-start.119 = (f32[64]{0:T(128)S(1)}, f32[64]{0:T(128)}, u32[]{:S(2)}) copy-start(f32[64]{0:T(128)} %copy-done.118) | copy-start | bytes 772
  1714.0 109.3 %copy-start.116 = (f32[64]{0:T(128)S(1)}, f32[64]{0:T(128)}, u32[]{:S(2)}) copy-start(f32[64]{0:T(128)} %copy-done.115) | copy-start | bytes 772
  1826.5 220.9 %reduce-scatter.27.cloned.1.call-start = ((), (), s32[]{:S(2)}) async-start(), calls=%async_computation.34 | async-start | bytes 12582912 | tf_op jit(solution)/shard_map/reduce_scatter | solution.py:360
  1834.4 345.6 %reduce-scatter.29.cloned.1.call-start = ((), (), s32[]{:S(2)}) async-start(), calls=%async_computation.35 | async-start | bytes 25165824 | tf_op jit(solution)/shard_map/reduce_scatter | solution.py:361
  1846.0 593.6 %reduce-scatter.31.cloned.1.call-start = ((), (), s32[]{:S(2)}) async-start(), calls=%async_computation.36 | async-start | bytes 34603008 | tf_op jit(solution)/shard_map/reduce_scatter | solution.py:364
  1873.1 848.2 %reduce-scatter.23.cloned.1.call-start = ((), (), s32[]{:S(2)}) async-start(), calls=%async_computation.32 | async-start | bytes 37748736 | tf_op jit(solution)/shard_map/reduce_scatter | solution.py:357
  1949.2 1278.2 %reduce-scatter.41.cloned.1.call-start = ((), (), s32[]{:S(2)}) async-start(), calls=%async_computation.41 | async-start | bytes 69206016
  1999.1 1417.0 %reduce-scatter.35.cloned.1.call-start = ((), (), s32[]{:S(2)}) async-start(), calls=%async_computation.38 | async-start | bytes 17301504 | tf_op jit(solution)/shard_map/reduce_scatter | solution.py:366
  2015.1 1608.5 %reduce-scatter.33.cloned.1.call-start = ((), (), s32[]{:S(2)}) async-start(), calls=%async_computation.37 | async-start | bytes 34603008 | tf_op jit(solution)/shard_map/reduce_scatter | solution.py:365
  2047.3 2596.0 %all-reduce.25.cloned.1.call-start = ((), (), s32[]{:S(2)}) async-start(), calls=%async_computation.42 | async-start | bytes 124256256 | tf_op jit(solution)/shard_map/psum | solution.py:368
  3236.0 47.9 %all-to-all-start.1 = ((bf16[16,32,2048]{2,1,0:T(8,128)(2,1)}), bf16[16,32,2048]{2,1,0:T(8,128)(2,1)S(1)}, u32[]{:S(2)}, u32[]{:S(2)}) async-start(bf16[16,32,2048]{2,1,0:T(8,128)(2,1)} %bitcast.415), calls=%async_computation.1 | async-start | bytes 4194304 | tf_op jit(solution)/shard_map/all_to_all | solution.py:206
  3285.3 52.6 %all-to-all-start.3 = ((bf16[16,32,2048]{2,1,0:T(8,128)(2,1)}), bf16[16,32,2048]{2,1,0:T(8,128)(2,1)S(1)}, u32[]{:S(2)}, u32[]{:S(2)}) async-start(bf16[16,32,2048]{2,1,0:T(8,128)(2,1)} %bitcast.412), calls=%async_computation.3 | async-start | bytes 4194304 | tf_op jit(solution)/shard_map/all_to_all | solution.py:206
  (140 other events, 2034.4 us)
Sparse Core Ops, SparseCore 0:
  9.5 37.9 all-gather.11
  49.1 56.7 all-gather.13
  107.4 152.4 all-gather.17
  262.6 74.8 all-gather.15
  338.8 101.9 all-gather.19
  443.5 110.2 all-gather.29
  555.3 139.2 all-gather.25
  696.1 74.4 all-gather.27
  772.2 270.3 all-gather.21
  1044.0 140.9 all-gather.23
  1484.3 58.3 reduce-scatter.20
  1546.7 54.8 reduce-scatter.18
  1606.2 104.0 reduce-scatter.38
  1714.7 103.0 reduce-scatter.36
  1826.6 59.8 reduce-scatter.24
  1889.2 99.3 reduce-scatter.26
  1990.7 189.2 reduce-scatter.28
  2182.7 256.7 reduce-scatter.30
  2441.9 279.3 reduce-scatter.22
  2723.4 504.0 reduce-scatter.40
  3230.4 133.2 reduce-scatter.34
  3366.5 257.0 reduce-scatter.32
  3629.2 1014.0 all-reduce.24
where the time goes:
time: 4710 us; the launch traced here: 4700 us
  waiting for transfers between devices  3670 us (78%)
  matrix products  526 us (11%)
  local copies, waits for them, and re-layouts  195 us (4%)
  blocking collectives  132 us (3%)
  starting transfers between devices  87.5 us (2%)
  other arithmetic  67 us (1%)
    psum x1, waiting for transfers between devices, per_device(): lax.psum((shards[0], shards[1], shards[2], shards[3], shards[4], shards[5...  1020 us
    unnamed x26, waiting for transfers between devices  722 us
    reduce_scatter x1, waiting for transfers between devices, per_device(): lax.psum_scatter(grad_query, 'dp', scatter_dimension=0, tiled=True)  282 us
    reduce_scatter x1, waiting for transfers between devices, per_device(): lax.psum_scatter(grad_shared_out, 'dp', scatter_dimension=0, tiled=True)  260 us
    all_gather x1, waiting for transfers between devices, per_device(): lax.all_gather(w_shared_in, 'dp', axis=0, tiled=True)  230 us
    reduce_scatter x1, waiting for transfers between devices, per_device(): lax.psum_scatter(grad_expert_in, 'dp', scatter_dimension=1, tiled=True)  208 us
    dot_general x14, matrix products, left_t_right(): lax.dot_general(left, right, (((0,), (0,)), ((), ())), preferred_element_...  164 us
    reduce_scatter x1, waiting for transfers between devices, per_device(): lax.psum_scatter(grad_out_proj, 'dp', scatter_dimension=0, tiled=True)  133 us
  transfers between devices with their start and end apart: 31, of which 24 were waited for; matrix products, arithmetic and copies ran while one was open for 12% of the time, Pallas kernels for 0%

commit v1 on v0

v1 whole, which is shorter than its diff:
```python
import functools

import jax
import jax.numpy as jnp
from jax import lax
from jax.experimental import pallas as pl
from jax.experimental.layout import Layout, with_layout_constraint
from jax.experimental.pallas import tpu as pltpu
from jax.sharding import PartitionSpec as P

HEADS = 16
NOPE = 128
ROPE = 64
VDIM = 128
LATENT = 512
DOC_MAX = 512

theta_base = 50000.0
eps_norm = 1e-06
bf16 = jnp.bfloat16
f32 = jnp.float32


def rope_tables(length, width):
    half = width // 2
    freq = theta_base ** (-2.0 * jnp.arange(half, dtype=f32) / width)
    angle = jnp.arange(length, dtype=f32)[:, None] * freq[None, :]
    cosine = jnp.concatenate([jnp.cos(angle), jnp.cos(angle)], -1)
    sine = jnp.concatenate([jnp.sin(angle), jnp.sin(angle)], -1)
    return (cosine, sine)


def rotate_back(value, cosine, sine):
    half = value.shape[-1] // 2
    scaled = value * sine
    turned = jnp.concatenate([scaled[..., half:], -scaled[..., :half]], -1)
    return value * cosine + turned


def normed(value, gain):
    return (
        value
        * lax.rsqrt(jnp.mean(value * value, -1, keepdims=True) + eps_norm)
        * gain.astype(f32)
    )


def normed_back(value, gain, grad):
    inv = lax.rsqrt(jnp.mean(value * value, -1, keepdims=True) + eps_norm)
    hat = value * inv
    scaled = grad * gain.astype(f32)
    inner = jnp.mean(scaled * hat, -1, keepdims=True)
    return inv * (scaled - hat * inner), jnp.sum(grad * hat, 0)


def swiglu_parts(packed):
    half = packed.shape[-1] // 2
    return packed[..., :half], packed[..., half:]


def swiglu(packed):
    gate, up = swiglu_parts(packed)
    return gate * jax.nn.sigmoid(gate) * up


def swiglu_back(packed, grad):
    gate, up = swiglu_parts(packed)
    sig = jax.nn.sigmoid(gate)
    d_gate = grad * up * sig * (1.0 + gate * (1.0 - sig))
    d_up = grad * gate * sig
    return jnp.concatenate([d_gate, d_up], -1)


def dot(left, right):
    return jnp.dot(left, right, preferred_element_type=f32)


def dot_tn(left, right):
    return lax.dot_general(left, right, (((0,), (0,)), ((), ())), preferred_element_type=f32)


def dot_nt(left, right):
    return lax.dot_general(left, right, (((1,), (1,)), ((), ())), preferred_element_type=f32)


def row_major(x):
    return with_layout_constraint(x, Layout(major_to_minor=tuple(range(x.ndim))))


def after(value, *first):
    return lax.optimization_barrier((value,) + first)[0]


def block_of_keys(refs, start, stop, low):
    qn_ref, rope_ref, kv_ref, seg_col, seg_row = refs
    rows = qn_ref.shape[2]

    def take(ref, first, last):
        return ref[first // rows : last // rows, 0].reshape(last - first, ref.shape[3])

    query = jnp.concatenate([take(qn_ref, start, stop), take(rope_ref, start, stop)[:, :ROPE]], 1)
    kv = take(kv_ref, low, stop)
    key = jnp.concatenate([kv[:, :NOPE], take(rope_ref, low, stop)[:, ROPE:]], 1)
    value = kv[:, NOPE:]
    score = dot_nt(query, key) * ((NOPE + ROPE) ** (-0.5))
    size = (stop - start, stop - low)
    q_at = lax.broadcasted_iota(jnp.int32, size, 0) + (start - low)
    k_at = lax.broadcasted_iota(jnp.int32, size, 1)
    allowed = (seg_col[0, start:stop] == seg_row[0, :, low:stop]) & (k_at <= q_at)
    return query, key, value, jnp.where(allowed, score, -1e30)


def query_blocks(seq, rows, size=256):
    for start in range(0, seq, size):
        low = max(0, start - DOC_MAX + 1) // rows * rows
        yield start, start + size, low


def attend_kernel(qn_ref, rope_ref, kv_ref, seg_col, seg_row, out_ref, lse_ref):
    owners, _, rows, _ = qn_ref.shape
    refs = (qn_ref, rope_ref, kv_ref, seg_col, seg_row)
    for start, stop, low in query_blocks(owners * rows, rows):
        _, _, value, score = block_of_keys(refs, start, stop, low)
        top = jnp.max(score, -1, keepdims=True)
        expo = jnp.exp(score - top)
        total = jnp.sum(expo, -1, keepdims=True)
        out = dot((expo / total).astype(bf16), value).astype(bf16)
        at = slice(start // rows, stop // rows)
        out_ref[at, 0] = out.reshape((stop - start) // rows, rows, VDIM)
        lse_ref[0, start:stop] = top + jnp.log(total)


def attend_back_kernel(
    qn_ref, rope_ref, kv_ref, seg_col, seg_row, lse_ref, dout_ref, cos_ref, sin_ref, back_ref, acc
):
    owners, _, rows, _ = qn_ref.shape
    seq = owners * rows
    refs = (qn_ref, rope_ref, kv_ref, seg_col, seg_row)
    acc[...] = jnp.zeros_like(acc)
    for start, stop, low in query_blocks(seq, rows):
        at = slice(start // rows, stop // rows)
        query, key, value, score = block_of_keys(refs, start, stop, low)
        prob = jnp.exp(score - lse_ref[0, start:stop])
        dout = dout_ref[at, 0].reshape(stop - start, VDIM)
        dprob = dot_nt(dout, value)
        delta = jnp.sum(prob * dprob, -1, keepdims=True)
        dscore = (prob * (dprob - delta) * ((NOPE + ROPE) ** (-0.5))).astype(bf16)
        dquery = dot(dscore, key)
        acc[low:stop, : NOPE + ROPE] += dot_tn(dscore, query)
        acc[low:stop, 256:] += dot_tn(prob.astype(bf16), dout)
        rope = rotate_back(dquery[:, NOPE:], cos_ref[start:stop], sin_ref[start:stop])
        whole = jnp.concatenate([dquery[:, :NOPE], rope, rope, dquery, rope], 1)
        back_ref[at, 0] = whole.astype(bf16).reshape((stop - start) // rows, rows, 512)
    dkey = acc[...]
    tail = jnp.concatenate([dkey[:, NOPE : NOPE + ROPE], dkey[:, :NOPE], dkey[:, 256:]], 1)
    back_ref[:, 0, :, NOPE + ROPE :] = tail.astype(bf16).reshape(owners, rows, 320)


def attend(q_nope, roped, kvup, segs):
    owners, micro, rows, _ = q_nope.shape
    seq = owners * rows
    spec = lambda c: pl.BlockSpec((owners, 1, rows, c), lambda m: (0, m, 0, 0))
    return pl.pallas_call(
        attend_kernel,
        out_shape=(
            jax.ShapeDtypeStruct((owners, micro, rows, VDIM), bf16),
            jax.ShapeDtypeStruct((micro, seq, 1), f32),
        ),
        grid=(micro,),
        in_specs=[
            spec(NOPE),
            spec(2 * ROPE),
            spec(2 * NOPE),
            pl.BlockSpec((1, seq, 1), lambda m: (m, 0, 0)),
            pl.BlockSpec((1, 1, seq), lambda m: (m, 0, 0)),
        ],
        out_specs=(spec(VDIM), pl.BlockSpec((1, seq, 1), lambda m: (m, 0, 0))),
        cost_estimate=pl.CostEstimate(
            flops=2 * micro * seq * 640 * 320,
            transcendentals=micro * seq * 640,
            bytes_accessed=micro * seq * 1400,
        ),
    )(q_nope, roped, kvup, segs[:, :, None], segs[:, None, :])


def attend_back(q_nope, roped, kvup, segs, lse, dout, cosine, sine):
    owners, micro, rows, _ = q_nope.shape
    seq = owners * rows
    spec = lambda c: pl.BlockSpec((owners, 1, rows, c), lambda m: (0, m, 0, 0))
    flat = pl.BlockSpec((seq, ROPE), lambda m: (0, 0))
    return pl.pallas_call(
        attend_back_kernel,
        out_shape=jax.ShapeDtypeStruct((owners, micro, rows, 512), bf16),
        grid=(micro,),
        in_specs=[
            spec(NOPE),
            spec(2 * ROPE),
            spec(2 * NOPE),
            pl.BlockSpec((1, seq, 1), lambda m: (m, 0, 0)),
            pl.BlockSpec((1, 1, seq), lambda m: (m, 0, 0)),
            pl.BlockSpec((1, seq, 1), lambda m: (m, 0, 0)),
            spec(VDIM),
            flat,
            flat,
        ],
        out_specs=spec(512),
        scratch_shapes=[pltpu.VMEM((seq, 384), f32)],
        cost_estimate=pl.CostEstimate(
            flops=2 * micro * seq * 640 * 832,
            transcendentals=micro * seq * 640,
            bytes_accessed=micro * seq * 2600,
        ),
    )(q_nope, roped, kvup, segs[:, :, None], segs[:, None, :], lse, dout, cosine, sine)


def put_back_kernel(place_ref, rows_ref, units_ref, weight_ref, out_ref, *, product):
    blocks, size, capacity = place_ref.shape
    shared = product(units_ref[...], weight_ref[...])
    for b in range(blocks):
        placed = dot(place_ref[b], rows_ref[b * capacity : (b + 1) * capacity])
        at = slice(b * size, (b + 1) * size)
        out_ref[at] = (placed + shared[at]).astype(bf16)


def put_back(place, rows, units, weight, product):
    blocks, size, capacity = place.shape
    total, count = units.shape
    width = rows.shape[1]
    many = 4
    return pl.pallas_call(
        functools.partial(put_back_kernel, product=product),
        out_shape=jax.ShapeDtypeStruct((total, width), bf16),
        grid=(blocks // many,),
        in_specs=[
            pl.BlockSpec((many, size, capacity), lambda i: (i, 0, 0)),
            pl.BlockSpec((many * capacity, width), lambda i: (i, 0)),
            pl.BlockSpec((many * size, count), lambda i: (i, 0)),
            pl.BlockSpec(weight.shape, lambda i: (0, 0)),
        ],
        out_specs=pl.BlockSpec((many * size, width), lambda i: (i, 0)),
        cost_estimate=pl.CostEstimate(
            flops=2 * total * width * (capacity + count),
            transcendentals=0,
            bytes_accessed=2 * (total * width + rows.size + units.size + weight.size),
        ),
    )(place, rows, units, weight)


def columns_kernel(x_ref, out_ref, *, runs, piece):
    groups = x_ref.shape[0]
    length = groups * piece
    parts = []
    for c in range(runs):
        parts += [x_ref[e, :, c * piece : (c + 1) * piece].astype(f32) for e in range(groups)]
        if length % 128 == 0:
            out_ref[:, c * length : (c + 1) * length] = jnp.concatenate(parts, 1)
            parts = []
    if parts:
        out_ref[...] = jnp.concatenate(parts, 1)


def run_columns(stacked, runs):
    groups, rows, count = stacked.shape
    size = min(128, rows)
    return pl.pallas_call(
        functools.partial(columns_kernel, runs=runs, piece=count // runs),
        out_shape=jax.ShapeDtypeStruct((rows, groups * count), f32),
        grid=(rows // size,),
        in_specs=[pl.BlockSpec((groups, size, count), lambda i: (0, i, 0))],
        out_specs=pl.BlockSpec((size, groups * count), lambda i: (i, 0)),
        cost_estimate=pl.CostEstimate(
            flops=0, transcendentals=0, bytes_accessed=6 * stacked.size
        ),
    )(stacked)


def attn_columns_kernel(x_ref, out_ref, query_ref, *, a, b):
    for e in range(0, x_ref.shape[0], 2):
        one, two = x_ref[e].astype(f32), x_ref[e + 1].astype(f32)
        out_ref[:, e * a : (e + 2) * a] = jnp.concatenate([one[:, :a], two[:, :a]], 1)
        query_ref[:, e * b : (e + 2) * b] = jnp.concatenate(
            [one[:, a : a + b], two[:, a : a + b]], 1
        )


def attn_columns(stacked, a, b):
    groups, rows, count = stacked.shape
    size = min(128, rows)
    return pl.pallas_call(
        functools.partial(attn_columns_kernel, a=a, b=b),
        out_shape=(
            jax.ShapeDtypeStruct((rows, groups * a), f32),
            jax.ShapeDtypeStruct((rows, groups * b), f32),
        ),
        grid=(rows // size,),
        in_specs=[pl.BlockSpec((groups, size, count), lambda i: (0, i, 0))],
        out_specs=(
            pl.BlockSpec((size, groups * a), lambda i: (i, 0)),
            pl.BlockSpec((size, groups * b), lambda i: (i, 0)),
        ),
        cost_estimate=pl.CostEstimate(
            flops=0, transcendentals=0, bytes_accessed=6 * stacked.size
        ),
    )(stacked)


def per_device(
    tokens,
    grad_out,
    segments,
    routes,
    gates,
    attn_gain,
    w_query,
    w_kv_down,
    kv_gain,
    w_kv_up,
    w_out,
    ffn_gain,
    w_shared_in,
    w_shared_out,
    w_expert_in,
    w_expert_out,
):
    micro, _, rows, width = tokens.shape
    groups = lax.axis_size("expert")
    parts = lax.axis_size("dp")
    me = lax.axis_index("expert")
    part = lax.axis_index("dp")
    own = micro * rows
    total = groups * own
    seq = rows * groups
    top = routes.shape[3]
    capacity = max(2, rows * top * 4 // (3 * groups))
    qk = NOPE + ROPE
    assert HEADS == groups

    def shift(x, step):
        return lax.ppermute(x, "dp", [((i + step) % parts, i) for i in range(parts)])

    def send(x, step):
        return lax.ppermute(x, "dp", [(i, (i + step) % parts) for i in range(parts)])

    def others(x):
        return [shift(x, r) for r in range(1, parts)]

    def turn(x, axis, amount):
        size = x.shape[axis]
        return lax.dynamic_slice_in_dim(
            jnp.concatenate([x, x], axis), amount * (size // parts), size, axis
        )

    def own_first(x, axis):
        return turn(x, axis, part)

    def natural(x, axis):
        return turn(x, axis, (parts - part) % parts)

    def lay_out(x, rest):
        size = x.shape[0]
        whole = jnp.zeros((parts * size,) + x.shape[1:], x.dtype)
        for r, piece in enumerate([x] + rest):
            at = ((part + r) % parts) * size
            whole = lax.dynamic_update_slice_in_dim(whole, piece, at, 0)
        return whole

    def block_of(full, index):
        size = full.shape[0] // parts
        return lax.dynamic_slice_in_dim(full, (index % parts) * size, size, 0)

    def exchanged(own_block, block_for):
        result = own_block.astype(f32)
        for r in range(1, parts):
            result = result + send(block_for(r), r).astype(f32)
        return result

    pairs = [(i, i ^ 1) for i in range(groups)]
    odd = me % 2

    def pieces(x, *first):
        size = x.shape[0]
        found = [(x, part * size)]
        if parts == 2:
            half = size // 2
            asked = lax.dynamic_slice_in_dim(x, odd * half, half, 0)
            if first:
                asked = after(asked, *first)
            got = shift(asked, 1)
            swapped = lax.ppermute(got, "expert", pairs)
            base = (1 - part) * size
            found += [(got, base + odd * half), (swapped, base + (1 - odd) * half)]
        else:
            asked = after(x, *first) if first else x
            found += [(y, ((part + r) % parts) * size) for r, y in enumerate(others(asked), 1)]
        return found

    def dot_pieces(x, blocks):
        return sum(
            dot(lax.dynamic_slice_in_dim(x, at, w.shape[0], 1), w) for w, at in blocks
        )

    def dot_pieces_t(x, blocks):
        whole = jnp.zeros((x.shape[0], sum(w.shape[0] for w, _ in blocks)), f32)
        for w, at in blocks:
            whole = lax.dynamic_update_slice_in_dim(whole, dot_nt(x, w), at, 1)
        return whole

    def spread(x):
        return lax.all_gather(x, "expert", axis=0, tiled=True)

    def stack(x):
        return lax.all_gather(x, "expert", axis=0, tiled=False)

    def swap(x):
        return lax.all_to_all(x, "expert", split_axis=0, concat_axis=0, tiled=True)

    def collect(x):
        return lax.psum_scatter(x, "expert", scatter_dimension=0, tiled=True)

    gain_sizes = (width // parts, LATENT // parts, width // parts)
    cuts = (gain_sizes[0], gain_sizes[0] + gain_sizes[1])
    own_gains = jnp.concatenate([attn_gain, kv_gain, ffn_gain])
    gain_rows = jnp.split(lay_out(own_gains[None], [y[None] for y in others(own_gains)]), cuts, 1)
    gain_attn, gain_kv, gain_ffn = (rows_of.reshape(-1) for rows_of in gain_rows)

    first_own = jnp.concatenate(
        [lax.dynamic_slice_in_dim(w_query, me * qk, qk, 1), w_kv_down], 1
    )
    first_all = jnp.concatenate([first_own] + others(first_own), 0)
    wkvup_own = lax.dynamic_slice_in_dim(w_kv_up, me * 2 * NOPE, 2 * NOPE, 1)
    wkvup_me = lay_out(wkvup_own, others(wkvup_own))
    wout = pieces(w_out)

    def turned(w):
        return jnp.concatenate([-w[:, ROPE // 2 :], w[:, : ROPE // 2]], 1)

    w_down = first_all[:, qk:]
    rope_q, rope_k = first_all[:, NOPE:qk], first_all[:, qk + LATENT :]
    w_first = jnp.concatenate(
        [
            first_all[:, :NOPE],
            first_all[:, qk : qk + LATENT],
            rope_q,
            rope_k,
            turned(rope_q),
            turned(rope_k),
        ],
        1,
    )

    x_own = tokens[:, 0].reshape(own, width)
    dy_own = grad_out[:, 0].reshape(own, width)
    act_own = normed(x_own.astype(f32), gain_attn).astype(bf16)
    act = spread(own_first(act_own, 1))
    dy_all = spread(after(dy_own, act))

    expert_ids = jnp.arange(groups, dtype=jnp.int32)
    routes_own = routes[:, 0].reshape(own, top)
    gates_own = gates[:, 0].reshape(own, top)
    table = jnp.sum(
        jnp.where(routes_own[None] == expert_ids[:, None, None], gates_own[None], 0.0), -1
    )
    gate_rows = swap(table).reshape(groups * micro, rows)
    hit = gate_rows > 0.0
    slot = jnp.cumsum(hit.astype(jnp.int32), 1) - 1
    pick = (slot[:, None, :] == jnp.arange(capacity, dtype=jnp.int32)[None, :, None]) & hit[
        :, None, :
    ]
    gate_slots = jnp.sum(jnp.where(pick, gate_rows[:, None, :], 0.0), -1).reshape(-1, 1)
    pick = pick.astype(bf16)
    place = pick.swapaxes(1, 2)

    def dispatch(x):
        picked = jnp.einsum(
            "bst,btd->bsd",
            pick,
            x.reshape(groups * micro, rows, width),
            preferred_element_type=f32,
        )
        return picked.reshape(groups * micro * capacity, width)

    ff = w_shared_in.shape[1] // 2
    run = ff // (parts * groups)
    wout_in = wout[1][0]
    wsi_own = jnp.concatenate(
        [
            lax.dynamic_slice_in_dim(w_shared_in, c * (ff // parts) + me * run, run, 1)
            for c in range(2 * parts)
        ],
        1,
    )
    wso_own = lax.dynamic_slice_in_dim(w_shared_out, me * run, run, 0)
    wsi_me = jnp.concatenate([wsi_own] + others(after(wsi_own, wout_in)), 0)
    wso_me = lay_out(wso_own, others(after(wso_own, wout_in)))
    wei_others = others(after(w_expert_in[0], wout_in))
    weo_others = others(after(w_expert_out[0], wout_in))
    wq = pieces(w_query, wei_others[0], weo_others[0])
    wkvup = pieces(w_kv_up, wei_others[0], weo_others[0])

    cosine, sine = rope_tables(seq, ROPE)

    def table_of(values):
        both = jnp.concatenate([values, values], 1).reshape(groups, 1, rows, 2 * ROPE)
        return jnp.broadcast_to(both, (groups, micro, rows, 2 * ROPE)).reshape(total, 2 * ROPE)

    first = dot(after(act, gate_rows), w_first)
    q_nope = first[:, :NOPE].astype(bf16)
    latent_raw = first[:, NOPE : NOPE + LATENT]
    latent = normed(latent_raw, gain_kv).astype(bf16)
    at = NOPE + LATENT
    roped = (
        first[:, at : at + 2 * ROPE] * table_of(cosine) + first[:, at + 2 * ROPE :] * table_of(sine)
    ).astype(bf16)
    kvup = dot(latent, wkvup_me).astype(bf16)

    def owners(x):
        return x.reshape(groups, micro, rows, x.shape[-1])

    segs = segments[:, 0]
    head = (owners(q_nope), owners(roped), owners(kvup), segs)
    attn, lse = attend(*head)
    attn_own = swap(attn.reshape(groups, own, VDIM))
    attn_own = attn_own.swapaxes(0, 1).reshape(own, groups * VDIM)
    x1 = x_own.astype(f32) + dot_pieces(attn_own, wout)
    hid_own = normed(x1, gain_ffn).astype(bf16)
    hid_all = spread(own_first(hid_own, 1))
    attn_all = spread(after(attn_own, hid_all))

    spre = dot(hid_all, wsi_me)
    sact = swiglu(spre).astype(bf16)
    dsact = dot_nt(dy_all, wso_me)
    dspre = swiglu_back(spre, dsact).astype(bf16)
    g_si = dot_tn(hid_all, dspre)
    size = width // parts
    g_si = exchanged(g_si[:size], lambda r: g_si[r * size : (r + 1) * size].astype(bf16))
    g_so = dot_tn(sact, dy_all)
    g_so = exchanged(block_of(g_so, part), lambda r: block_of(g_so, part + r).astype(bf16))
    g_si = stack(row_major(g_si.astype(bf16)))
    g_so = stack(row_major(g_so.astype(bf16)))

    arrived = dispatch(hid_all).astype(bf16)
    dyexp = (gate_slots * dispatch(dy_all)).astype(bf16)
    wei = jnp.concatenate([w_expert_in[0]] + wei_others, 0)
    weo = lay_out(w_expert_out[0], weo_others)
    epre = dot(arrived, wei)
    eact = swiglu(epre).astype(bf16)
    deact = dot_nt(dyexp, weo)
    depre = swiglu_back(epre, deact).astype(bf16)
    dhid_rows = dot_nt(depre, wei).astype(bf16)
    dhid_part = put_back(place, dhid_rows, dspre, wsi_me, dot_nt)
    dhid_sum = collect(after(dhid_part, g_si, g_so))

    arrived, depre, eact, dyexp = lax.optimization_barrier(
        (arrived, depre, eact, dyexp, dhid_part)
    )[:4]
    gated = (gate_slots * dot(eact, weo)).astype(bf16)
    out_part = put_back(place, gated, sact, wso_me, dot)

    def expert_in_grad(r):
        return dot_tn(arrived[:, r * size : (r + 1) * size], depre)

    def expert_out_grad(r):
        short = eact.shape[1] // parts
        some = lax.dynamic_slice_in_dim(eact, ((part + r) % parts) * short, short, 1)
        return dot_tn(some, dyexp)

    sent_in = [expert_in_grad(r).astype(bf16) for r in range(1, parts)]
    sent_out = [expert_out_grad(r).astype(bf16) for r in range(1, parts)]
    dhid_sum = after(dhid_sum, out_part, *sent_in, *sent_out)
    got_in = [send(x, r).astype(f32) for r, x in enumerate(sent_in, 1)]
    got_out = [send(x, r).astype(f32) for r, x in enumerate(sent_out, 1)]
    out_sum = collect(after(out_part, dhid_sum))
    dhid = natural(dhid_sum, 1).astype(f32)

    dy = dy_own.astype(f32)
    dx1_norm, g_ffn_gain = normed_back(x1, gain_ffn, dhid)
    dx1 = dy + dx1_norm
    dx1_low = dx1.astype(bf16)
    dattn_own = dot_pieces_t(dx1_low, wout).astype(bf16)
    dattn = swap(dattn_own.reshape(own, groups, VDIM).swapaxes(0, 1))
    dao = after(dx1_low, dattn).reshape(own, groups, width // groups).swapaxes(0, 1)
    dao = swap(dao)
    dattn = dattn.reshape(groups, micro, rows, VDIM)
    back = attend_back(*head, lse, dattn, cosine, sine)
    moved = swap(back.reshape(groups, own, 512))

    def back_of(x, first_column, last_column):
        piece = x[..., first_column:last_column]
        return piece.swapaxes(0, 1).reshape(own, groups * (last_column - first_column))

    flat = back.reshape(total, 512)
    g_query = dot_tn(act, flat[:, :qk])
    g_kvup = dot_tn(latent, flat[:, 256:])
    g_out = dot_tn(attn_all, dao.reshape(total, width // groups))

    def fold(x):
        many = size // x.shape[0]
        return jnp.concatenate(jnp.split(x, many, 1), 0)

    def unfold(x, height):
        return jnp.concatenate(jnp.split(x, x.shape[1] // height, 1), 2)

    def attn_grads(r):
        return jnp.concatenate(
            [
                block_of(g_out, part + r),
                g_query[r * size : (r + 1) * size],
                fold(block_of(g_kvup, part + r)),
            ],
            1,
        )

    g_attn = exchanged(attn_grads(0), lambda r: attn_grads(r).astype(bf16))
    g_attn = stack(row_major(g_attn.astype(bf16)))

    dq_own = back_of(moved, 0, qk)
    dkvup_own = back_of(moved, 256, 512)
    dkrope_own = jnp.sum(moved[..., qk:256].astype(f32), 0)
    dlatent = dot_pieces_t(dkvup_own, wkvup)
    latent_own = lax.dynamic_slice_in_dim(latent_raw, me * own, own, 0)
    cos_own = jnp.tile(lax.dynamic_slice_in_dim(cosine, me * rows, rows, 0), (micro, 1))
    sin_own = jnp.tile(lax.dynamic_slice_in_dim(sine, me * rows, rows, 0), (micro, 1))
    dlatent_raw, g_kv_gain = normed_back(latent_own, gain_kv, dlatent)
    dkvfull = jnp.concatenate([dlatent_raw, rotate_back(dkrope_own, cos_own, sin_own)], -1)
    dkvfull = dkvfull.astype(bf16)
    dkv_all = spread(dkvfull)
    dact = dot_pieces_t(dq_own, wq) + natural(dot_nt(dkvfull, w_down), 1)
    dx_norm, g_attn_gain = normed_back(x_own.astype(f32), gain_attn, dact)
    input_grad = dx1 + dx_norm

    step = width // (parts * groups)
    act_rows = jnp.concatenate(
        [
            lax.dynamic_slice_in_dim(act, c * size + me * step, step, 1)
            for c in range(parts)
        ],
        1,
    )
    g_down = dot_tn(act_rows, dkv_all)

    def last_grads(r):
        gains = [block_of(g, part + r) for g in (g_attn_gain, g_kv_gain, g_ffn_gain)]
        gains = jnp.concatenate(gains).reshape(-1, LATENT + ROPE)
        return jnp.concatenate([g_down[r * step : (r + 1) * step], gains], 0)

    last = exchanged(last_grads(0), lambda r: last_grads(r).astype(bf16))
    last = stack(last.astype(bf16))
    g_down = last[:, :step].astype(f32).reshape(size, LATENT + ROPE)
    gains = jnp.sum(last[:, step:].astype(f32), 0).reshape(-1)
    gains = jnp.split(gains, cuts)

    mixed = (x1 + out_sum.astype(f32)).astype(bf16)
    g_ein = sum(got_in, expert_in_grad(0))
    g_eout = sum(got_out, expert_out_grad(0))
    out_grad, query_grad = attn_columns(g_attn, width // groups, qk)
    kvup_grad = unfold(g_attn[..., width // groups + qk :], LATENT // parts)
    kvup_grad = kvup_grad.swapaxes(0, 1).reshape(LATENT // parts, -1).astype(f32)
    return (
        mixed.reshape(micro, 1, rows, width),
        input_grad.reshape(micro, 1, rows, width),
        gains[0],
        query_grad,
        g_down,
        gains[1],
        kvup_grad,
        out_grad,
        gains[2],
        run_columns(g_si, 2 * parts),
        g_so.astype(f32).reshape(ff // parts, width),
        g_ein[None],
        g_eout[None],
    )


def solution(mesh):
    tok = P(None, "dp", "expert", None)
    row = P("dp", None)
    exp = P("expert", "dp", None)
    in_specs = (
        tok, tok, P(None, "dp", None), tok, tok,
        P("dp"), row, row, P("dp"), row, row, P("dp"), row, row, exp, exp,
    )
    out_specs = (
        tok, tok, P("dp"), row, row, P("dp"), row, row, P("dp"), row, row, exp, exp,
    )

    return jax.shard_map(
        per_device, mesh=mesh, in_specs=in_specs, out_specs=out_specs, check_vma=False
    )
```

time: 4710 us -> 1300 us (0.28)
  waiting for transfers between devices: 3670 us -> 791 us
  matrix products: 526 us -> 199 us
  blocking collectives: 132 us -> 0 us
  local copies, waits for them, and re-layouts: 195 us -> 86.6 us
  Pallas kernels: 0 us -> 70.1 us
    psum x1 -> x0, waiting for transfers between devices: 1020 us -> none  [per_device(): lax.psum((shards[0], shards[1], shards[2], shards[3], shards[4], shards[5...]
    reduce_scatter x9 -> x2, waiting for transfers between devices: 927 us -> 57.3 us  [collect(): return lax.psum_scatter(x, 'expert', scatter_dimension=0, tiled=True)]
    unnamed x26 -> x11, waiting for transfers between devices: 722 us -> 2.04 us
    all_gather x10 -> x9, waiting for transfers between devices: 806 us -> 128 us  [the longest x5 109 us: spread(): return lax.all_gather(x, 'expert', axis=0, tiled=True)]
    ppermute x0 -> x19, waiting for transfers between devices: none -> 571 us  [the longest x10 343 us: shift(): lax.ppermute(x, 'dp', [((i + step) % parts, i) for i in range(parts)])]
    dot_general x66 -> x33, matrix products: 526 us -> 199 us  [the longest x10 65.5 us: dot_tn(): lax.dot_general(left, right, (((0,), (0,)), ((), ())), preferred_element_...]
    all_to_all x8 -> x5, waiting for transfers between devices: 199 us -> 32 us  [swap(): return lax.all_to_all(x, 'expert', split_axis=0, concat_axis=0, tiled=True)]
    all_gather x5 -> x0, blocking collectives: 88.4 us -> none  [the longest x2 78.3 us: per_device(): lax.all_gather(key_rope, 'expert', axis=0, tiled=True)]
  transfers between devices with their start and end apart: 31 -> 35, of which waited for: 24 -> 19; matrix products, arithmetic and copies ran while one was open for 12% -> 22% of each run, Pallas kernels for 0% -> 4%
where the time goes in v1:
time: 1300 us; the launch traced here: 1290 us
  waiting for transfers between devices  791 us (61%)
  matrix products  199 us (15%)
  local copies, waits for them, and re-layouts  86.6 us (7%)
  Pallas kernels  70.1 us (5%)
  starting transfers between devices  68.3 us (5%)
  other arithmetic  64.2 us (5%)
  between operations  15.5 us (1%)
    ppermute x10, waiting for transfers between devices, shift(): lax.ppermute(x, 'dp', [((i + step) % parts, i) for i in range(parts)])  343 us
    ppermute x6, waiting for transfers between devices, send(): lax.ppermute(x, 'dp', [(i, (i + step) % parts) for i in range(parts)])  228 us
    all_gather x5, waiting for transfers between devices, spread(): return lax.all_gather(x, 'expert', axis=0, tiled=True)  109 us
    dot_general x10, matrix products, dot_tn(): lax.dot_general(left, right, (((0,), (0,)), ((), ())), preferred_element_...  65.5 us
    dot_general x13, matrix products, dot_nt(): lax.dot_general(left, right, (((1,), (1,)), ((), ())), preferred_element_...  64.1 us
    dot_general x8, matrix products, dot(): return jnp.dot(left, right, preferred_element_type=f32)  58.5 us
    reduce_scatter x2, waiting for transfers between devices, collect(): return lax.psum_scatter(x, 'expert', scatter_dimension=0, tiled=True)  57.3 us
    all_to_all x5, starting transfers between devices, swap(): return lax.all_to_all(x, 'expert', split_axis=0, concat_axis=0, tiled=True)  35.3 us
  transfers between devices with their start and end apart: 35, of which 19 were waited for; matrix products, arithmetic and copies ran while one was open for 22% of the time, Pallas kernels for 4%

profile of v1, /device:TPU:1, one launch (start us, length us, event | category | flops | bytes accessed | tf_op | source)
XLA Modules:
  0.0 1294.3 jit_solution(16747225938847290353)
XLA Ops:
  21.5 8.4 all-to-all-start
  31.2 3.2 constant_dynamic-slice_fusion.11
  46.6 11.1 collective-permute-done.2
  62.5 40.2 %collective-permute-done.3 = bf16[512,2048]{1,0:T(8,128)(2,1)} collective-permute-done((bf16[512,2048]{1,0:T(8,128)(2,1)}, bf16[512,2048]{1,0:T(8,128)(2,1)}, u32[]{:S(2)}, u32[]{:S(2)}) %collective-permute-start.3) | collective-permute-done | bytes 2097184 | tf_op jit(solution)/shard_map/ppermute | solution.py:339
  104.6 12.4 fusion.81
  123.4 7.7 shard_map.255
  133.2 5.8 all-to-all-start.1
  139.0 11.4 all-gather.17.cloned.1.call-start
  153.0 3.1 fusion.50
  168.2 21.8 %collective-permute-done.7 = bf16[88,2048]{1,0:T(8,128)(2,1)} collective-permute-done((bf16[88,2048]{1,0:T(8,128)(2,1)}, bf16[88,2048]{1,0:T(8,128)(2,1)}, u32[]{:S(2)}, u32[]{:S(2)}) %collective-permute-start.7) | collective-permute-done | bytes 360480 | tf_op jit(solution)/shard_map/ppermute | solution.py:339
  193.1 42.0 %all-gather.17.cloned.1.call-done = bf16[2048,2048]{1,0:T(8,128)(2,1)} async-done(((bf16[128,2048]{1,0:T(8,128)(2,1)}), bf16[2048,2048]{1,0:T(8,128)(2,1)}) %all-gather.17.cloned.1.call-update) | async-done | bytes 8388624 | tf_op jit(solution)/shard_map/all_gather | solution.py:409
  235.1 8.6 fusion.82
  243.6 66.5 %all-gather.19.cloned.1.call-done = bf16[2048,2048]{1,0:T(8,128)(2,1)} async-done(((bf16[128,2048]{1,0:T(8,128)(2,1)}), bf16[2048,2048]{1,0:T(8,128)(2,1)}) %all-gather.19.cloned.1.call-update) | async-done | bytes 8388624 | tf_op jit(solution)/shard_map/all_gather | solution.py:409
  310.2 9.0 multiply_convert_fusion.7
  319.8 3.4 fusion.83
  326.0 16.0 %collective-permute-done.9 = bf16[1024,352]{0,1:T(8,128)(2,1)} collective-permute-done((bf16[1024,352]{0,1:T(8,128)(2,1)}, bf16[1024,352]{0,1:T(8,128)(2,1)}, u32[]{:S(2)}, u32[]{:S(2)}) %collective-permute-start.9) | collective-permute-done | bytes 720928 | tf_op jit(solution)/shard_map/ppermute | solution.py:342
  346.1 3.3 broadcast_in_dim.101
  353.5 178.0 %collective-permute-done.5 = bf16[704,2048]{1,0:T(8,128)(2,1)} collective-permute-done((bf16[704,2048]{1,0:T(8,128)(2,1)}, bf16[704,2048]{1,0:T(8,128)(2,1)}, u32[]{:S(2)}, u32[]{:S(2)}) %collective-permute-start.5) | collective-permute-done | bytes 2883616 | tf_op jit(solution)/shard_map/ppermute | solution.py:339
  531.5 3.8 constant_dynamic-update-slice_fusion.3
  535.2 4.6 fusion.44
  540.4 6.1 convolution_convert_fusion.1
  548.6 18.6 %fusion.2 = f32[1024,2816]{1,0:T(8,128)} fusion(bf16[1024,2048]{1,0:T(8,128)(2,1)S(1)} %bitcast.176, bf16[1024,2816]{1,0:T(8,128)(2,1)} %collective-permute-done.6, bf16[1024,2816]{1,0:T(8,128)(2,1)} %bitcast.213), kind=kOutput, calls=%fused_computation.6 | convolution fusion | flops 11834228736 | bytes 27262976 | tf_op jit(solution)/shard_map/dot_general | solution.py:75
  567.2 14.8 %multiply_convert_fusion.3 = (bf16[1024,1408]{1,0:T(8,128)(2,1)S(1)}, bf16[1024,1408]{1,0:T(8,128)(2,1)}, bf16[1024,1408]{1,0:T(8,128)(2,1)}) fusion(f32[1024,2816]{1,0:T(8,128)} %fusion.2, bf16[1024,2048]{1,0:T(8,128)(2,1)S(1)} %fusion, bf16[1408,2048]{1,0:T(8,128)(2,1)} %constant_dynamic-update-slice_fusion.3), kind=kOutput, calls=%fused_computation.11 | convolution fusion | flops 5928648704 | bytes 30146560 | tf_op jit(solution)/shard_map/dot_general | solution.py:83
  582.0 17.6 %fusion.3.rows_ref = bf16[1024,2048]{1,0:T(8,128)(2,1)} fusion(bf16[1024,2816]{1,0:T(8,128)(2,1)} %collective-permute-done.6, bf16[1024,2816]{1,0:T(8,128)(2,1)} %bitcast.214, bf16[1024,1408]{1,0:T(8,128)(2,1)} %get-tuple-element.148, bf16[1024,1408]{1,0:T(8,128)(2,1)S(1)} %get-tuple-element.147), kind=kOutput, calls=%fused_computation.17 | convolution fusion | flops 11847860224 | bytes 21495808 | tf_op jit(solution)/shard_map/dot_general | solution.py:83
  599.5 12.5 shard_map.256
  612.1 4.9 pad_maximum_fusion.3
  617.0 11.4 multiply_convert_fusion.rows_ref
  628.4 11.2 shard_map.257
  639.6 7.4 convolution_convert_fusion.2
  647.0 10.8 convolution_convert_fusion
  657.9 57.3 %reduce-scatter.3.cloned.1.call-done = bf16[128,2048]{1,0:T(8,128)(2,1)} async-done(((bf16[2048,2048]{1,0:T(8,128)(2,1)}), bf16[128,2048]{1,0:T(8,128)(2,1)}) %reduce-scatter.3.cloned.1.call-update) | async-done | bytes 524304 | tf_op jit(solution)/shard_map/reduce_scatter | solution.py:418
  723.6 5.8 all-to-all-start.2
  732.7 10.6 all-to-all-done.2
  744.1 9.8 shard_map.258
  753.9 3.9 copy.211
  757.8 4.5 all-to-all-start.3
  766.1 23.4 %collective-permute-done.13 = bf16[128,4096]{1,0:T(8,128)(2,1)} collective-permute-done((bf16[128,4096]{1,0:T(8,128)(2,1)}, bf16[128,4096]{1,0:T(8,128)(2,1)}, u32[]{:S(2)}, u32[]{:S(2)}) %collective-permute-start.13) | collective-permute-done | bytes 1048608 | tf_op jit(solution)/shard_map/ppermute | solution.py:339
  791.7 12.4 all-to-all-done.3
  816.5 5.1 fusion.84
  822.9 9.2 collective-permute-done.10
  836.6 68.2 %collective-permute-done.11 = bf16[512,3072]{1,0:T(8,128)(2,1)} collective-permute-done((bf16[512,3072]{1,0:T(8,128)(2,1)S(1)}, bf16[512,3072]{1,0:T(8,128)(2,1)}, u32[]{:S(2)}, u32[]{:S(2)}) %collective-permute-start.11) | collective-permute-done | bytes 3145760 | tf_op jit(solution)/shard_map/ppermute | solution.py:339
  909.8 5.1 convolution_dynamic-update-slice_fusion.1
  914.9 3.3 convolution_dynamic-update-slice_fusion.3
  923.7 3.2 fusion.37
  928.6 4.1 collective-permute-done.15
  935.1 10.7 all-to-all-start.4
  946.1 5.5 fusion.28
  952.9 3.6 fusion.26
  957.5 6.5 all-to-all-done.4
  964.0 5.8 fusion.85
  978.1 12.3 collective-permute-done.16
  994.3 186.7 %collective-permute-done.18 = bf16[704,2048]{1,0:T(8,128)(2,1)S(1)} collective-permute-done((bf16[704,2048]{1,0:T(8,128)(2,1)}, bf16[704,2048]{1,0:T(8,128)(2,1)S(1)}, u32[]{:S(2)}, u32[]{:S(2)}) %collective-permute-start.18) | collective-permute-done | bytes 2883616 | tf_op jit(solution)/shard_map/ppermute | solution.py:342
  1181.0 8.7 add_bitcast_fusion.1
  1189.7 12.1 add_bitcast_fusion
  1201.7 8.7 convert.81
  1210.4 15.7 %shard_map.260 = f32[1024,5632]{1,0:T(8,128)} custom-call(bf16[16,1024,352]{2,1,0:T(8,128)(2,1)} %bitcast.175), custom_call_target="tpu_custom_call" | custom-call | bytes 34603008 | tf_op jit(solution)/shard_map/pallas_call | solution.py:265
  1229.3 3.2 copy.232
  1233.7 3.1 multiply_add_fusion
  1236.7 19.8 %all-gather.29.cloned.1.call-done = bf16[16384,384]{1,0:T(8,128)(2,1)} async-done(((bf16[1024,384]{1,0:T(8,128)(2,1)}), bf16[16384,384]{1,0:T(8,128)(2,1)}) %all-gather.29.cloned.1.call-update) | async-done | bytes 12582928 | tf_op jit(solution)/shard_map/all_gather | solution.py:412
  1256.6 13.2 %shard_map.259 = (f32[1024,2048]{1,0:T(8,128)}, f32[1024,3072]{1,0:T(8,128)}) custom-call(bf16[16,1024,384]{2,1,0:T(8,128)(2,1)} %bitcast.165), custom_call_target="tpu_custom_call" | custom-call | bytes 37748736 | tf_op jit(solution)/shard_map/pallas_call | solution.py:289
  1269.7 3.5 fusion.76
  1273.2 3.3 convert_bitcast_fusion
  1276.5 5.4 copy.229
  1281.9 5.6 copy.233
  (324 shorter events, 144.2 us)
Async XLA Ops:
  7.2 11.3 copy-start
  7.2 97.4 %all-gather.15.cloned.1.call-start = ((), (), s32[]{:S(2)}) async-start(), calls=%async_computation.7 | async-start | bytes 8912896 | tf_op jit(solution)/shard_map/all_gather | solution.py:409
  9.7 3.5 collective-permute-start
  13.1 6.6 copy-start.52
  14.5 6.2 copy-start.50
  14.5 6.3 copy-start.51
  19.7 38.9 %collective-permute-start.1 = (bf16[1024,768]{0,1:T(8,128)(2,1)}, bf16[1024,768]{0,1:T(8,128)(2,1)S(1)}, u32[]{:S(2)}, u32[]{:S(2)}) collective-permute-start(bf16[1024,768]{0,1:T(8,128)(2,1)} %pad_maximum_fusion.7), channel_id=1, source_target_pairs={{16,0},{0,16},{17,1},{1,17},{18,2},{2,18},{19,3},{3,19},{20,4},{4,... | collective-permute-start | bytes 4718600 | tf_op jit(solution)/shard_map/ppermute | solution.py:339
  21.5 21.8 %all-to-all-start = ((f32[16,1,128]{2,1,0:T(1,128)}), f32[16,1,128]{2,1,0:T(1,128)}, u32[]{:S(2)}, u32[]{:S(2)}) async-start(f32[16,1,128]{2,1,0:T(1,128)} %bitcast.2), calls=%async_computation | async-start | bytes 16384 | tf_op jit(solution)/shard_map/all_to_all | solution.py:415
  31.0 26.8 %collective-permute-start.2 = (bf16[256,256]{1,0:T(8,128)(2,1)S(1)}, bf16[256,256]{1,0:T(8,128)(2,1)}, u32[]{:S(2)}, u32[]{:S(2)}) collective-permute-start(bf16[256,256]{1,0:T(8,128)(2,1)S(1)} %get-tuple-element.146), channel_id=1, source_target_pairs={{16,0},{0,16},{17,1},{1,17},{18,2},{2,18},{19,3},{3,19},{20,4},{4,... | collective-permute-start | bytes 393224 | tf_op jit(solution)/shard_map/ppermute | solution.py:339
  34.4 68.2 %collective-permute-start.3 = (bf16[512,2048]{1,0:T(8,128)(2,1)}, bf16[512,2048]{1,0:T(8,128)(2,1)}, u32[]{:S(2)}, u32[]{:S(2)}) collective-permute-start(bf16[512,2048]{1,0:T(8,128)(2,1)} %constant_dynamic-slice_fusion.11), channel_id=1, source_target_pairs={{16,0},{0,16},{17,1},{1,17},{18,2},{2,18},{19,3},{3,19},{20,4},{4,... | collective-permute-start | bytes 6291464 | tf_op jit(solution)/shard_map/ppermute | solution.py:339
  102.7 55.6 %collective-permute-start.4 = (bf16[512,2048]{1,0:T(8,128)(2,1)}, bf16[512,2048]{1,0:T(8,128)(2,1)S(1)}, u32[]{:S(2)}, u32[]{:S(2)}) collective-permute-start(bf16[512,2048]{1,0:T(8,128)(2,1)} %collective-permute-done.3), channel_id=1, source_target_pairs={{0,1},{1,0},{2,3},{3,2},{4,5},{5,4},{6,7},{7,6},{8,9},{9,8},{10,11... | collective-permute-start | bytes 6291464 | tf_op jit(solution)/shard_map/ppermute | solution.py:389
  123.4 27.0 %copy-start.47 = (f32[1,8,2,128]{3,2,1,0:T(2,128)S(1)}, f32[1,8,2,128]{3,2,1,0:T(2,128)}, u32[]{:S(2)}) copy-start(f32[1,8,2,128]{3,2,1,0:T(2,128)} %get-tuple-element.179) | copy-start | bytes 24580
  133.2 19.8 %all-to-all-start.1 = ((bf16[16,128,128]{1,2,0:T(8,128)(2,1)}), bf16[16,128,128]{1,2,0:T(8,128)(2,1)S(1)}, u32[]{:S(2)}, u32[]{:S(2)}) async-start(bf16[16,128,128]{1,2,0:T(8,128)(2,1)} %copy.200), calls=%async_computation.1 | async-start | bytes 1048576 | tf_op jit(solution)/shard_map/all_to_all | solution.py:415
  139.0 96.1 %all-gather.17.cloned.1.call-start = ((), (), s32[]{:S(2)}) async-start(), calls=%async_computation.8 | async-start | bytes 8912896 | tf_op jit(solution)/shard_map/all_gather | solution.py:409
  150.4 8.5 copy-start.38
  153.0 5.3 copy-start.8
  161.2 148.9 %all-gather.19.cloned.1.call-start = ((), (), s32[]{:S(2)}) async-start(), calls=%async_computation.9 | async-start | bytes 8912896 | tf_op jit(solution)/shard_map/all_gather | solution.py:409
  161.9 450.1 %all-gather.25.cloned.1.call-start = ((), (), s32[]{:S(2)}) async-start(), calls=%async_computation.14 | async-start | bytes 13369344 | tf_op jit(solution)/shard_map/all_gather | solution.py:412
  164.0 27.1 %copy-start.26 = (bf16[1024,88]{1,0:T(8,128)(2,1)}, bf16[1024,88]{1,0:T(8,128)(2,1)S(1)}, u32[]{:S(2)}) copy-start(bf16[1024,88]{1,0:T(8,128)(2,1)S(1)} %get-tuple-element.154) | copy-start | bytes 540676
  164.0 27.1 %copy-start.27 = (bf16[1024,88]{1,0:T(8,128)(2,1)}, bf16[1024,88]{1,0:T(8,128)(2,1)S(1)}, u32[]{:S(2)}) copy-start(bf16[1024,88]{1,0:T(8,128)(2,1)S(1)} %get-tuple-element.155) | copy-start | bytes 540676
  164.0 27.1 %copy-start.28 = (bf16[1024,88]{1,0:T(8,128)(2,1)}, bf16[1024,88]{1,0:T(8,128)(2,1)S(1)}, u32[]{:S(2)}) copy-start(bf16[1024,88]{1,0:T(8,128)(2,1)S(1)} %get-tuple-element.156) | copy-start | bytes 540676
  164.8 26.2 %collective-permute-start.8 = (bf16[1024,352]{0,1:T(8,128)(2,1)S(1)}, bf16[1024,352]{0,1:T(8,128)(2,1)S(1)}, u32[]{:S(2)}, u32[]{:S(2)}) collective-permute-start(bf16[1024,352]{0,1:T(8,128)(2,1)S(1)} %copy.201), channel_id=1, source_target_pairs={{16,0},{0,16},{17,1},{1,17},{18,2},{2,18},{19,3},{3,19},{20,4},{4,... | collective-permute-start | bytes 2162696 | tf_op jit(solution)/shard_map/ppermute | solution.py:339
  167.7 22.3 %collective-permute-start.7 = (bf16[88,2048]{1,0:T(8,128)(2,1)}, bf16[88,2048]{1,0:T(8,128)(2,1)}, u32[]{:S(2)}, u32[]{:S(2)}) collective-permute-start(bf16[88,2048]{1,0:T(8,128)(2,1)} %get-tuple-element.39), channel_id=1, source_target_pairs={{16,0},{0,16},{17,1},{1,17},{18,2},{2,18},{19,3},{3,19},{20,4},{4,... | collective-permute-start | bytes 1081352 | tf_op jit(solution)/shard_map/ppermute | solution.py:339
  191.0 119.1 %copy-start.24 = (bf16[176,2048]{1,0:T(8,128)(2,1)}, bf16[176,2048]{1,0:T(8,128)(2,1)S(1)}, u32[]{:S(2)}) copy-start(bf16[176,2048]{1,0:T(8,128)(2,1)S(1)} %constant_dynamic-update-slice_fusion.1.weight_ref) | copy-start | bytes 2162692
  193.1 50.6 %copy-start.18 = (bf16[2048,352]{1,0:T(8,128)(2,1)}, bf16[2048,352]{1,0:T(8,128)(2,1)S(1)}, u32[]{:S(2)}) copy-start(bf16[2048,352]{1,0:T(8,128)(2,1)S(1)} %pad_maximum_fusion.8.weight_ref) | copy-start | bytes 4325380
  310.1 9.6 copy-start.13
  324.2 17.7 %collective-permute-start.9 = (bf16[1024,352]{0,1:T(8,128)(2,1)}, bf16[1024,352]{0,1:T(8,128)(2,1)}, u32[]{:S(2)}, u32[]{:S(2)}) collective-permute-start(bf16[1024,352]{0,1:T(8,128)(2,1)} %slice.226), channel_id=1, source_target_pairs={{0,16},{16,0},{1,17},{17,1},{2,18},{18,2},{3,19},{19,3},{4,20},{20... | collective-permute-start | bytes 2162696 | tf_op jit(solution)/shard_map/ppermute | solution.py:342
  344.5 370.7 %reduce-scatter.3.cloned.1.call-start = ((), (), s32[]{:S(2)}) async-start(), calls=%async_computation.10 | async-start | bytes 8912896 | tf_op jit(solution)/shard_map/reduce_scatter | solution.py:418
  344.6 202.0 %collective-permute-start.6 = (bf16[1024,2816]{1,0:T(8,128)(2,1)}, bf16[1024,2816]{1,0:T(8,128)(2,1)}, u32[]{:S(2)}, u32[]{:S(2)}) collective-permute-start(bf16[1024,2816]{1,0:T(8,128)(2,1)} %bitcast.212), channel_id=1, source_target_pairs={{16,0},{0,16},{17,1},{1,17},{18,2},{2,18},{19,3},{3,19},{20,4},{4,... | collective-permute-start | bytes 17301512 | tf_op jit(solution)/shard_map/ppermute | solution.py:339
  345.8 185.6 %collective-permute-start.5 = (bf16[704,2048]{1,0:T(8,128)(2,1)}, bf16[704,2048]{1,0:T(8,128)(2,1)}, u32[]{:S(2)}, u32[]{:S(2)}) collective-permute-start(bf16[704,2048]{1,0:T(8,128)(2,1)} %bitcast.187), channel_id=1, source_target_pairs={{16,0},{0,16},{17,1},{1,17},{18,2},{2,18},{19,3},{3,19},{20,4},{4,... | collective-permute-start | bytes 8650760 | tf_op jit(solution)/shard_map/ppermute | solution.py:339
  540.4 26.8 %copy-start.6 = (bf16[1024,2048]{1,0:T(8,128)(2,1)}, bf16[1024,2048]{1,0:T(8,128)(2,1)S(1)}, u32[]{:S(2)}) copy-start(bf16[1024,2048]{1,0:T(8,128)(2,1)S(1)} %fusion) | copy-start | bytes 12582916
  628.4 11.2 copy-start.33
  639.6 7.4 copy-start.11
  647.0 68.2 %copy-start.3 = (f32[128,2048]{1,0:T(8,128)S(1)}, f32[128,2048]{1,0:T(8,128)}, u32[]{:S(2)}) copy-start(f32[128,2048]{1,0:T(8,128)} %copy-done.2) | copy-start | bytes 3145732
  647.0 68.2 %copy-start.39 = (f32[1,8,2,128]{3,1,2,0:T(8,128)S(1)}, f32[1,8,2,128]{3,1,2,0:T(8,128)}, u32[]{:S(2)}) copy-start(f32[1,8,2,128]{3,1,2,0:T(8,128)} %copy-done.38) | copy-start | bytes 24580
  647.0 68.2 %copy-start.49 = (f32[128]{0:T(128)S(1)}, f32[128]{0:T(128)}, u32[]{:S(2)}) copy-start(f32[128]{0:T(128)} %copy-done.48) | copy-start | bytes 1540
  647.0 69.9 %copy-start.19 = (bf16[2,1,64,2048]{3,2,1,0:T(8,128)(2,1)S(1)}, bf16[2,1,64,2048]{3,2,1,0:T(8,128)(2,1)}, u32[]{:S(2)}) copy-start(bf16[2,1,64,2048]{3,2,1,0:T(8,128)(2,1)} %param.17) | copy-start | bytes 1572868
  719.4 10.0 copy-start.55
  723.6 19.7 %all-to-all-start.2 = ((bf16[16,128,128]{2,1,0:T(8,128)(2,1)}), bf16[16,128,128]{2,1,0:T(8,128)(2,1)S(1)}, u32[]{:S(2)}, u32[]{:S(2)}) async-start(bf16[16,128,128]{2,1,0:T(8,128)(2,1)} %bitcast_bitcast_fusion.1), calls=%async_computation.4 | async-start | bytes 1048576 | tf_op jit(solution)/shard_map/all_to_all | solution.py:415
  757.8 46.2 %all-to-all-start.3 = ((bf16[16,128,512]{1,2,0:T(8,128)(2,1)}), bf16[16,128,512]{1,2,0:T(8,128)(2,1)}, u32[]{:S(2)}, u32[]{:S(2)}) async-start(bf16[16,128,512]{1,2,0:T(8,128)(2,1)} %copy.211), calls=%async_computation.5 | async-start | bytes 4194304 | tf_op jit(solution)/shard_map/all_to_all | solution.py:415
  762.4 161.3 %all-gather.21.cloned.1.call-start = ((), (), s32[]{:S(2)}) async-start(), calls=%async_computation.12 | async-start | bytes 2785280 | tf_op jit(solution)/shard_map/all_gather | solution.py:409
  764.7 24.7 %collective-permute-start.13 = (bf16[128,4096]{1,0:T(8,128)(2,1)}, bf16[128,4096]{1,0:T(8,128)(2,1)}, u32[]{:S(2)}, u32[]{:S(2)}) collective-permute-start(bf16[128,4096]{1,0:T(8,128)(2,1)} %constant_dynamic-slice_fusion.3), channel_id=1, source_target_pairs={{16,0},{0,16},{17,1},{1,17},{18,2},{2,18},{19,3},{3,19},{20,4},{4,... | collective-permute-start | bytes 3145736 | tf_op jit(solution)/shard_map/ppermute | solution.py:339
  789.5 21.4 %collective-permute-start.14 = (bf16[128,4096]{1,0:T(8,128)(2,1)}, bf16[128,4096]{1,0:T(8,128)(2,1)}, u32[]{:S(2)}, u32[]{:S(2)}) collective-permute-start(bf16[128,4096]{1,0:T(8,128)(2,1)} %collective-permute-done.13), channel_id=1, source_target_pairs={{0,1},{1,0},{2,3},{3,2},{4,5},{5,4},{6,7},{7,6},{8,9},{9,8},{10,11... | collective-permute-start | bytes 3145736 | tf_op jit(solution)/shard_map/ppermute | solution.py:389
  806.6 6.1 copy-start.44
  809.1 7.4 copy-start.16
  815.7 141.8 %all-gather.23.cloned.1.call-start = ((), (), s32[]{:S(2)}) async-start(), calls=%async_computation.13 | async-start | bytes 8912896 | tf_op jit(solution)/shard_map/all_gather | solution.py:409
  816.5 385.3 %all-gather.27.cloned.1.call-start = ((), (), s32[]{:S(2)}) async-start(), calls=%async_computation.15 | async-start | bytes 6127616 | tf_op jit(solution)/shard_map/all_gather | solution.py:412
  821.6 10.5 collective-permute-start.10
  833.0 393.1 %all-gather.31.cloned.1.call-start = ((), (), s32[]{:S(2)}) async-start(), calls=%async_computation.17 | async-start | bytes 1566720 | tf_op jit(solution)/shard_map/all_gather | solution.py:412
  835.3 69.4 %collective-permute-start.11 = (bf16[512,3072]{1,0:T(8,128)(2,1)S(1)}, bf16[512,3072]{1,0:T(8,128)(2,1)}, u32[]{:S(2)}, u32[]{:S(2)}) collective-permute-start(bf16[512,3072]{1,0:T(8,128)(2,1)S(1)} %constant_dynamic-slice_fusion.4), channel_id=1, source_target_pairs={{16,0},{0,16},{17,1},{1,17},{18,2},{2,18},{19,3},{3,19},{20,4},{4,... | collective-permute-start | bytes 9437192 | tf_op jit(solution)/shard_map/ppermute | solution.py:339
  904.8 13.4 %collective-permute-start.12 = (bf16[512,3072]{1,0:T(8,128)(2,1)}, bf16[512,3072]{1,0:T(8,128)(2,1)}, u32[]{:S(2)}, u32[]{:S(2)}) collective-permute-start(bf16[512,3072]{1,0:T(8,128)(2,1)} %collective-permute-done.11), channel_id=1, source_target_pairs={{0,1},{1,0},{2,3},{3,2},{4,5},{5,4},{6,7},{7,6},{8,9},{9,8},{10,11... | collective-permute-start | bytes 9437192 | tf_op jit(solution)/shard_map/ppermute | solution.py:389
  914.9 6.4 copy-start.9
  914.9 6.4 copy-start.41
  914.9 6.4 copy-start.53
  927.1 5.6 collective-permute-start.15
  933.6 300.1 %reduce-scatter.5.cloned.1.call-start = ((), (), s32[]{:S(2)}) async-start(), calls=%async_computation.11 | async-start | bytes 8912896 | tf_op jit(solution)/shard_map/reduce_scatter | solution.py:418
  935.1 28.9 %all-to-all-start.4 = ((bf16[16,128,128]{2,1,0:T(8,128)(2,1)}), bf16[16,128,128]{2,1,0:T(8,128)(2,1)S(1)}, u32[]{:S(2)}, u32[]{:S(2)}) async-start(bf16[16,128,128]{2,1,0:T(8,128)(2,1)} %bitcast_bitcast_fusion), calls=%async_computation.6 | async-start | bytes 1048576 | tf_op jit(solution)/shard_map/all_to_all | solution.py:415
  945.8 310.8 %all-gather.29.cloned.1.call-start = ((), (), s32[]{:S(2)}) async-start(), calls=%async_computation.16 | async-start | bytes 13369344 | tf_op jit(solution)/shard_map/all_gather | solution.py:412
  946.1 6.9 copy-start.46
  971.0 19.4 %collective-permute-start.16 = (bf16[1024,384]{1,0:T(8,128)(2,1)}, bf16[1024,384]{1,0:T(8,128)(2,1)}, u32[]{:S(2)}, u32[]{:S(2)}) collective-permute-start(bf16[1024,384]{1,0:T(8,128)(2,1)} %maximum_maximum_fusion), channel_id=1, source_target_pairs={{0,16},{16,0},{1,17},{17,1},{2,18},{18,2},{3,19},{19,3},{4,20},{20... | collective-permute-start | bytes 2359304 | tf_op jit(solution)/shard_map/ppermute | solution.py:342
  992.8 196.9 %copy-start.12 = (bf16[32,32,2048]{2,1,0:T(8,128)(2,1)S(1)}, bf16[32,32,2048]{2,1,0:T(8,128)(2,1)}, u32[]{:S(2)}) copy-start(bf16[32,32,2048]{2,1,0:T(8,128)(2,1)} %copy-done.10) | copy-start | bytes 12582916
  992.8 196.9 %collective-permute-start.17 = (bf16[1024,2816]{1,0:T(8,128)(2,1)}, bf16[1024,2816]{1,0:T(8,128)(2,1)S(1)}, u32[]{:S(2)}, u32[]{:S(2)}) collective-permute-start(bf16[1024,2816]{1,0:T(8,128)(2,1)} %convolution_convert_fusion), channel_id=1, source_target_pairs={{0,16},{16,0},{1,17},{17,1},{2,18},{18,2},{3,19},{19,3},{4,20},{20... | collective-permute-start | bytes 17301512 | tf_op jit(solution)/shard_map/ppermute | solution.py:342
  994.0 187.0 %collective-permute-start.18 = (bf16[704,2048]{1,0:T(8,128)(2,1)}, bf16[704,2048]{1,0:T(8,128)(2,1)S(1)}, u32[]{:S(2)}, u32[]{:S(2)}) collective-permute-start(bf16[704,2048]{1,0:T(8,128)(2,1)} %convolution_convert_fusion.2), channel_id=1, source_target_pairs={{0,16},{16,0},{1,17},{17,1},{2,18},{18,2},{3,19},{19,3},{4,20},{20... | collective-permute-start | bytes 8650760 | tf_op jit(solution)/shard_map/ppermute | solution.py:342
  1227.5 6.1 copy-start.20
  (28 other events, 73.0 us)
Sparse Core Ops, SparseCore 0:
  17.0 76.9 all-gather.14
  161.3 73.6 all-gather.16
  237.2 72.8 all-gather.18
  344.6 99.8 all-gather.24
  612.2 102.9 reduce-scatter.2
  815.8 48.7 all-gather.20
  866.8 76.5 all-gather.22
  945.7 61.0 all-gather.26
  1009.0 37.7 all-gather.30
  1051.3 101.5 reduce-scatter.4
  1155.7 100.8 all-gather.28

commit v2 on v1

--- a/solution.py
+++ b/solution.py
@@ -246,12 +246,13 @@
     )(place, rows, units, weight)
 
 
-def columns_kernel(x_ref, out_ref, *, runs, piece):
+def shared_in_kernel(x_ref, out_ref, *, runs, piece):
     groups = x_ref.shape[0]
+    turned = [x_ref[e].astype(f32).T for e in range(groups)]
     length = groups * piece
     parts = []
     for c in range(runs):
-        parts += [x_ref[e, :, c * piece : (c + 1) * piece].astype(f32) for e in range(groups)]
+        parts += [t[:, c * piece : (c + 1) * piece] for t in turned]
         if length % 128 == 0:
             out_ref[:, c * length : (c + 1) * length] = jnp.concatenate(parts, 1)
             parts = []
@@ -259,17 +260,64 @@
         out_ref[...] = jnp.concatenate(parts, 1)
 
 
-def run_columns(stacked, runs):
+def shared_out_kernel(x_ref, out_ref, *, piece):
+    rows = x_ref[0].astype(f32)
+    count = rows.shape[0] // piece
+    out_ref[0] = jnp.concatenate([rows[c * piece : (c + 1) * piece] for c in range(count)], 1)
+
+
+def shared_rows(stacked, runs, piece):
+    groups, count, size = stacked.shape
+    first = runs * piece
+    rest = count - first
+    step = 128
+    in_grad = pl.pallas_call(
+        functools.partial(shared_in_kernel, runs=runs, piece=piece),
+        out_shape=jax.ShapeDtypeStruct((size, groups * first), f32),
+        grid=(size // step,),
+        in_specs=[pl.BlockSpec((groups, first, step), lambda i: (0, 0, i))],
+        out_specs=pl.BlockSpec((step, groups * first), lambda i: (i, 0)),
+        cost_estimate=pl.CostEstimate(
+            flops=0, transcendentals=0, bytes_accessed=6 * groups * first * size
+        ),
+    )(stacked)
+    out_grad = pl.pallas_call(
+        functools.partial(shared_out_kernel, piece=piece),
+        out_shape=jax.ShapeDtypeStruct((groups, piece, rest // piece * size), f32),
+        grid=(groups,),
+        in_specs=[pl.BlockSpec((1, rest, size), lambda e: (e, first // rest, 0))],
+        out_specs=pl.BlockSpec((1, piece, rest // piece * size), lambda e: (e, 0, 0)),
+        cost_estimate=pl.CostEstimate(
+            flops=0, transcendentals=0, bytes_accessed=6 * groups * rest * size
+        ),
+    )(stacked)
+    return in_grad, out_grad.reshape(groups * piece, -1)
+
+
+def kvup_columns_kernel(x_ref, out_ref, *, skip, height):
+    groups, rows, _ = x_ref.shape
+    for e in range(groups):
+        runs = [
+            x_ref[e, c * height : (c + 1) * height, skip:].astype(f32)
+            for c in range(rows // height)
+        ]
+        whole = jnp.concatenate(runs, 1)
+        count = whole.shape[1]
+        out_ref[:, e * count : (e + 1) * count] = whole
+
+
+def kvup_columns(stacked, start, height):
     groups, rows, count = stacked.shape
-    size = min(128, rows)
+    tile = start // 128
+    width = (count - start) * (rows // height)
     return pl.pallas_call(
-        functools.partial(columns_kernel, runs=runs, piece=count // runs),
-        out_shape=jax.ShapeDtypeStruct((rows, groups * count), f32),
-        grid=(rows // size,),
-        in_specs=[pl.BlockSpec((groups, size, count), lambda i: (0, i, 0))],
-        out_specs=pl.BlockSpec((size, groups * count), lambda i: (i, 0)),
+        functools.partial(kvup_columns_kernel, skip=start - 128 * tile, height=height),
+        out_shape=jax.ShapeDtypeStruct((height, groups * width), f32),
+        grid=(1,),
+        in_specs=[pl.BlockSpec((groups, rows, count - 128 * tile), lambda i: (0, 0, tile))],
+        out_specs=pl.BlockSpec((height, groups * width), lambda i: (0, 0)),
         cost_estimate=pl.CostEstimate(
-            flops=0, transcendentals=0, bytes_accessed=6 * stacked.size
+            flops=0, transcendentals=0, bytes_accessed=8 * groups * height * width
         ),
     )(stacked)
 
@@ -414,6 +462,9 @@
     def swap(x):
         return lax.all_to_all(x, "expert", split_axis=0, concat_axis=0, tiled=True)
 
+    def broadcast(x):
+        return swap(jnp.broadcast_to(x[None], (groups,) + x.shape))
+
     def collect(x):
         return lax.psum_scatter(x, "expert", scatter_dimension=0, tiled=True)
 
@@ -481,7 +532,6 @@
 
     ff = w_shared_in.shape[1] // 2
     run = ff // (parts * groups)
-    wout_in = wout[1][0]
     wsi_own = jnp.concatenate(
         [
             lax.dynamic_slice_in_dim(w_shared_in, c * (ff // parts) + me * run, run, 1)
@@ -490,10 +540,10 @@
         1,
     )
     wso_own = lax.dynamic_slice_in_dim(w_shared_out, me * run, run, 0)
-    wsi_me = jnp.concatenate([wsi_own] + others(after(wsi_own, wout_in)), 0)
-    wso_me = lay_out(wso_own, others(after(wso_own, wout_in)))
-    wei_others = others(after(w_expert_in[0], wout_in))
-    weo_others = others(after(w_expert_out[0], wout_in))
+    wsi_me = jnp.concatenate([wsi_own] + others(wsi_own), 0)
+    wso_me = lay_out(wso_own, others(wso_own))
+    wei_others = others(w_expert_in[0])
+    weo_others = others(w_expert_out[0])
     wq = pieces(w_query, wei_others[0], weo_others[0])
     wkvup = pieces(w_kv_up, wei_others[0], weo_others[0])
 
@@ -530,13 +580,17 @@
     sact = swiglu(spre).astype(bf16)
     dsact = dot_nt(dy_all, wso_me)
     dspre = swiglu_back(spre, dsact).astype(bf16)
-    g_si = dot_tn(hid_all, dspre)
     size = width // parts
-    g_si = exchanged(g_si[:size], lambda r: g_si[r * size : (r + 1) * size].astype(bf16))
+    g_si = dot_tn(dspre, hid_all)
     g_so = dot_tn(sact, dy_all)
-    g_so = exchanged(block_of(g_so, part), lambda r: block_of(g_so, part + r).astype(bf16))
-    g_si = stack(row_major(g_si.astype(bf16)))
-    g_so = stack(row_major(g_so.astype(bf16)))
+
+    def shared_grads(r):
+        rows_of = block_of(g_so, part + r)
+        return jnp.concatenate(
+            [g_si[:, r * size : (r + 1) * size]] + jnp.split(rows_of, parts, 1), 0
+        )
+
+    g_shared = exchanged(shared_grads(0), lambda r: shared_grads(r).astype(bf16)).astype(bf16)
 
     arrived = dispatch(hid_all).astype(bf16)
     dyexp = (gate_slots * dispatch(dy_all)).astype(bf16)
@@ -548,7 +602,8 @@
     depre = swiglu_back(epre, deact).astype(bf16)
     dhid_rows = dot_nt(depre, wei).astype(bf16)
     dhid_part = put_back(place, dhid_rows, dspre, wsi_me, dot_nt)
-    dhid_sum = collect(after(dhid_part, g_si, g_so))
+    dhid_sum = collect(dhid_part)
+    g_shared = stack(after(g_shared, dhid_sum))
 
     arrived, depre, eact, dyexp = lax.optimization_barrier(
         (arrived, depre, eact, dyexp, dhid_part)
@@ -569,7 +624,6 @@
     dhid_sum = after(dhid_sum, out_part, *sent_in, *sent_out)
     got_in = [send(x, r).astype(f32) for r, x in enumerate(sent_in, 1)]
     got_out = [send(x, r).astype(f32) for r, x in enumerate(sent_out, 1)]
-    out_sum = collect(after(out_part, dhid_sum))
     dhid = natural(dhid_sum, 1).astype(f32)
 
     dy = dy_own.astype(f32)
@@ -597,9 +651,6 @@
         many = size // x.shape[0]
         return jnp.concatenate(jnp.split(x, many, 1), 0)
 
-    def unfold(x, height):
-        return jnp.concatenate(jnp.split(x, x.shape[1] // height, 1), 2)
-
     def attn_grads(r):
         return jnp.concatenate(
             [
@@ -611,7 +662,9 @@
         )
 
     g_attn = exchanged(attn_grads(0), lambda r: attn_grads(r).astype(bf16))
-    g_attn = stack(row_major(g_attn.astype(bf16)))
+    g_attn = g_attn.astype(bf16)
+    out_sum = collect(after(out_part, g_attn))
+    g_attn = stack(row_major(g_attn))
 
     dq_own = back_of(moved, 0, qk)
     dkvup_own = back_of(moved, 256, 512)
@@ -623,7 +676,7 @@
     dlatent_raw, g_kv_gain = normed_back(latent_own, gain_kv, dlatent)
     dkvfull = jnp.concatenate([dlatent_raw, rotate_back(dkrope_own, cos_own, sin_own)], -1)
     dkvfull = dkvfull.astype(bf16)
-    dkv_all = spread(dkvfull)
+    dkv_all = broadcast(dkvfull).reshape(total, LATENT + ROPE)
     dact = dot_pieces_t(dq_own, wq) + natural(dot_nt(dkvfull, w_down), 1)
     dx_norm, g_attn_gain = normed_back(x_own.astype(f32), gain_attn, dact)
     input_grad = dx1 + dx_norm
@@ -644,7 +697,7 @@
         return jnp.concatenate([g_down[r * step : (r + 1) * step], gains], 0)
 
     last = exchanged(last_grads(0), lambda r: last_grads(r).astype(bf16))
-    last = stack(last.astype(bf16))
+    last = broadcast(last.astype(bf16))
     g_down = last[:, :step].astype(f32).reshape(size, LATENT + ROPE)
     gains = jnp.sum(last[:, step:].astype(f32), 0).reshape(-1)
     gains = jnp.split(gains, cuts)
@@ -653,8 +706,8 @@
     g_ein = sum(got_in, expert_in_grad(0))
     g_eout = sum(got_out, expert_out_grad(0))
     out_grad, query_grad = attn_columns(g_attn, width // groups, qk)
-    kvup_grad = unfold(g_attn[..., width // groups + qk :], LATENT // parts)
-    kvup_grad = kvup_grad.swapaxes(0, 1).reshape(LATENT // parts, -1).astype(f32)
+    kvup_grad = kvup_columns(g_attn, width // groups + qk, LATENT // parts)
+    shared_in_grad, shared_out_grad = shared_rows(g_shared, 2 * parts, run)
     return (
         mixed.reshape(micro, 1, rows, width),
         input_grad.reshape(micro, 1, rows, width),
@@ -665,8 +718,8 @@
         kvup_grad,
         out_grad,
         gains[2],
-        run_columns(g_si, 2 * parts),
-        g_so.astype(f32).reshape(ff // parts, width),
+        shared_in_grad,
+        shared_out_grad,
         g_ein[None],
         g_eout[None],
     )

time: 1300 us -> 1240 us (0.954)
  waiting for transfers between devices: 791 us -> 724 us
  Pallas kernels: 70.1 us -> 88.5 us
  local copies, waits for them, and re-layouts: 86.6 us -> 71.4 us
    all_to_all x5 -> x7, waiting for transfers between devices: 32 us -> 123 us  [swap(): return lax.all_to_all(x, 'expert', split_axis=0, concat_axis=0, tiled=True)]
    ppermute x6 -> x5, waiting for transfers between devices: 228 us -> 157 us  [send(): lax.ppermute(x, 'dp', [(i, (i + step) % parts) for i in range(parts)])]
    ppermute x10, waiting for transfers between devices: 343 us -> 277 us  [shift(): lax.ppermute(x, 'dp', [((i + step) % parts, i) for i in range(parts)])]
    all_to_all x5 -> x7, starting transfers between devices: 35.3 us -> 59.6 us  [swap(): return lax.all_to_all(x, 'expert', split_axis=0, concat_axis=0, tiled=True)]
    all_gather x4 -> x2, waiting for transfers between devices: 19.8 us -> 0.01 us  [stack(): return lax.all_gather(x, 'expert', axis=0, tiled=False)]
    pallas_call x1 -> x3, Pallas kernels: 15.7 us -> 34 us  [the longest x1 17.3 us: shared_rows(): pl.pallas_call(functools.partial(shared_in_kernel, runs=runs, piece=piece...]
    all_gather x5 -> x4, waiting for transfers between devices: 109 us -> 109 us  [spread(): return lax.all_gather(x, 'expert', axis=0, tiled=True)]
  transfers between devices with their start and end apart: 35 -> 33, of which waited for: 19 -> 17; matrix products, arithmetic and copies ran while one was open for 22% -> 20% of each run, Pallas kernels for 4% -> 4%
where the time goes in v2:
time: 1240 us; the launch traced here: 1230 us
  waiting for transfers between devices  724 us (58%)
  matrix products  193 us (16%)
  Pallas kernels  88.5 us (7%)
  starting transfers between devices  78.7 us (6%)
  local copies, waits for them, and re-layouts  71.4 us (6%)
  other arithmetic  57.4 us (5%)
  between operations  15.9 us (1%)
    ppermute x10, waiting for transfers between devices, shift(): lax.ppermute(x, 'dp', [((i + step) % parts, i) for i in range(parts)])  277 us
    ppermute x5, waiting for transfers between devices, send(): lax.ppermute(x, 'dp', [(i, (i + step) % parts) for i in range(parts)])  157 us
    all_to_all x7, waiting for transfers between devices, swap(): return lax.all_to_all(x, 'expert', split_axis=0, concat_axis=0, tiled=True)  123 us
    all_gather x4, waiting for transfers between devices, spread(): return lax.all_gather(x, 'expert', axis=0, tiled=True)  109 us
    dot_general x10, matrix products, dot_tn(): lax.dot_general(left, right, (((0,), (0,)), ((), ())), preferred_element_...  72 us
    dot_general x13, matrix products, dot_nt(): lax.dot_general(left, right, (((1,), (1,)), ((), ())), preferred_element_...  61.2 us
    all_to_all x7, starting transfers between devices, swap(): return lax.all_to_all(x, 'expert', split_axis=0, concat_axis=0, tiled=True)  59.6 us
    reduce_scatter x2, waiting for transfers between devices, collect(): return lax.psum_scatter(x, 'expert', scatter_dimension=0, tiled=True)  56.7 us
  transfers between devices with their start and end apart: 33, of which 17 were waited for; matrix products, arithmetic and copies ran while one was open for 20% of the time, Pallas kernels for 4%

profile of v2, /device:TPU:1, one launch (start us, length us, event | category | flops | bytes accessed | tf_op | source)
XLA Modules:
  0.0 1228.8 jit_solution(16063950565131843787)
XLA Ops:
  16.9 77.0 %all-gather.9.cloned.1.call-done = bf16[2048,2048]{1,0:T(8,128)(2,1)} async-done(((bf16[128,2048]{1,0:T(8,128)(2,1)}), bf16[2048,2048]{1,0:T(8,128)(2,1)}) %all-gather.9.cloned.1.call-update) | async-done | bytes 8388624 | tf_op jit(solution)/shard_map/all_gather | solution.py:457
  98.8 4.5 all-to-all-start
  104.6 3.2 constant_dynamic-slice_fusion.12
  120.0 15.6 %collective-permute-done.2 = bf16[256,256]{1,0:T(8,128)(2,1)} collective-permute-done((bf16[256,256]{1,0:T(8,128)(2,1)S(1)}, bf16[256,256]{1,0:T(8,128)(2,1)}, u32[]{:S(2)}, u32[]{:S(2)}) %collective-permute-start.2) | collective-permute-done | bytes 131104 | tf_op jit(solution)/shard_map/ppermute | solution.py:387
  138.6 42.0 %collective-permute-done.3 = bf16[512,2048]{1,0:T(8,128)(2,1)} collective-permute-done((bf16[512,2048]{1,0:T(8,128)(2,1)}, bf16[512,2048]{1,0:T(8,128)(2,1)}, u32[]{:S(2)}, u32[]{:S(2)}) %collective-permute-start.3) | collective-permute-done | bytes 2097184 | tf_op jit(solution)/shard_map/ppermute | solution.py:387
  181.7 9.3 fusion.83
  197.5 7.7 shard_map.255
  207.3 3.5 all-to-all-start.1
  210.8 13.9 %all-to-all-done.1 = bf16[16,128,128]{1,2,0:T(8,128)(2,1)S(1)} async-done(((bf16[16,128,128]{1,2,0:T(8,128)(2,1)}), bf16[16,128,128]{1,2,0:T(8,128)(2,1)S(1)}, u32[]{:S(2)}, u32[]{:S(2)}) %all-to-all-start.1) | async-done | bytes 524320 | tf_op jit(solution)/shard_map/all_to_all | solution.py:463
  224.7 3.1 fusion.53
  240.7 3.3 broadcast_in_dim.113
  248.1 195.6 %collective-permute-done.7 = bf16[88,2048]{1,0:T(8,128)(2,1)} collective-permute-done((bf16[88,2048]{1,0:T(8,128)(2,1)}, bf16[88,2048]{1,0:T(8,128)(2,1)}, u32[]{:S(2)}, u32[]{:S(2)}) %collective-permute-start.7) | collective-permute-done | bytes 360480 | tf_op jit(solution)/shard_map/ppermute | solution.py:387
  446.8 4.3 constant_dynamic-update-slice_fusion.3
  451.2 4.6 fusion.47
  458.3 7.9 fusion.84
  466.2 8.0 multiply_convert_fusion.7
  479.2 17.2 %fusion.2 = f32[1024,2816]{1,0:T(8,128)} fusion(bf16[1024,2048]{1,0:T(8,128)(2,1)S(1)} %bitcast.178, bf16[1024,2816]{1,0:T(8,128)(2,1)} %collective-permute-done.6, bf16[1024,2816]{1,0:T(8,128)(2,1)S(1)} %bitcast.219), kind=kOutput, calls=%fused_computation.6 | convolution fusion | flops 11834228736 | bytes 27262976 | tf_op jit(solution)/shard_map/dot_general | solution.py:75
  496.4 14.7 %multiply_convert_fusion.3 = (bf16[1024,1408]{1,0:T(8,128)(2,1)S(1)}, bf16[1024,1408]{1,0:T(8,128)(2,1)}, bf16[1024,1408]{1,0:T(8,128)(2,1)}) fusion(f32[1024,2816]{1,0:T(8,128)} %fusion.2, bf16[1024,2048]{1,0:T(8,128)(2,1)S(1)} %copy-done.7, bf16[1408,2048]{1,0:T(8,128)(2,1)} %constant_dynamic-update-slice_fusion.3), kind=kOutput, calls=%fused_computation.11 | convolution fusion | flops 5928648704 | bytes 30146560 | tf_op jit(solution)/shard_map/dot_general | solution.py:83
  511.1 17.6 %fusion.3.rows_ref = bf16[1024,2048]{1,0:T(8,128)(2,1)} fusion(bf16[1024,2816]{1,0:T(8,128)(2,1)} %collective-permute-done.6, bf16[1024,2816]{1,0:T(8,128)(2,1)} %bitcast.216, bf16[1024,1408]{1,0:T(8,128)(2,1)} %get-tuple-element.140, bf16[1024,1408]{1,0:T(8,128)(2,1)S(1)} %get-tuple-element.139), kind=kOutput, calls=%fused_computation.16 | convolution fusion | flops 11847860224 | bytes 21495808 | tf_op jit(solution)/shard_map/dot_general | solution.py:83
  528.7 12.5 %shard_map.256 = bf16[2048,2048]{1,0:T(8,128)(2,1)} custom-call(bf16[32,64,32]{2,1,0:T(8,128)(2,1)} %fusion.37.place_ref, bf16[1024,2048]{1,0:T(8,128)(2,1)} %fusion.3.rows_ref, bf16[2048,352]{1,0:T(8,128)(2,1)} %pad_maximum_fusion.9.units_ref, bf16[2048,352]{1,0:T(8,128)(2,1)} %copy-done.18), custom_call_target="tpu_custom_call" | custom-call | flops 3221225472 | bytes 15466496 | tf_op jit(solution)/shard_map/pallas_call | solution.py:230
  541.8 4.9 pad_maximum_fusion.3
  546.7 11.5 multiply_convert_fusion.rows_ref
  558.3 11.1 shard_map.257
  569.3 7.4 convolution_convert_fusion.2
  576.7 11.3 convolution_convert_fusion
  588.0 56.7 %reduce-scatter.3.cloned.1.call-done = bf16[128,2048]{1,0:T(8,128)(2,1)} async-done(((bf16[2048,2048]{1,0:T(8,128)(2,1)}), bf16[128,2048]{1,0:T(8,128)(2,1)}) %reduce-scatter.3.cloned.1.call-update) | async-done | bytes 524304 | tf_op jit(solution)/shard_map/reduce_scatter | solution.py:469
  653.1 5.3 all-to-all-start.2
  662.6 16.4 %all-to-all-done.2 = bf16[16,128,128]{2,1,0:T(8,128)(2,1)S(1)} async-done(((bf16[16,128,128]{2,1,0:T(8,128)(2,1)}), bf16[16,128,128]{2,1,0:T(8,128)(2,1)S(1)}, u32[]{:S(2)}, u32[]{:S(2)}) %all-to-all-start.2) | async-done | bytes 524320 | tf_op jit(solution)/shard_map/all_to_all | solution.py:463
  680.0 9.5 all-to-all-start.3
  689.5 10.1 shard_map.258
  699.6 5.5 fusion.32
  706.5 3.7 fusion.30
  712.2 32.1 %all-gather.15.cloned.1.call-done = bf16[2048,2048]{0,1:T(8,128)(2,1)} async-done(((bf16[128,2048]{0,1:T(8,128)(2,1)}), bf16[2048,2048]{0,1:T(8,128)(2,1)}) %all-gather.15.cloned.1.call-update) | async-done | bytes 8388624 | tf_op jit(solution)/shard_map/all_gather | solution.py:457
  744.3 5.9 fusion.85
  755.4 15.2 %collective-permute-done.9 = bf16[1024,384]{1,0:T(8,128)(2,1)} collective-permute-done((bf16[1024,384]{1,0:T(8,128)(2,1)}, bf16[1024,384]{1,0:T(8,128)(2,1)}, u32[]{:S(2)}, u32[]{:S(2)}) %collective-permute-start.9) | collective-permute-done | bytes 786464 | tf_op jit(solution)/shard_map/ppermute | solution.py:390
  774.4 5.9 fusion.86
  780.4 6.8 fusion.87
  792.1 21.9 %collective-permute-done.15 = bf16[528,1024]{1,0:T(8,128)(2,1)} collective-permute-done((bf16[528,1024]{1,0:T(8,128)(2,1)}, bf16[528,1024]{1,0:T(8,128)(2,1)}, u32[]{:S(2)}, u32[]{:S(2)}) %collective-permute-start.15) | collective-permute-done | bytes 1081376 | tf_op jit(solution)/shard_map/ppermute | solution.py:390
  814.0 2.6 fusion.10
  816.7 3.9 copy.198
  820.6 6.4 all-to-all-start.4
  830.5 3.8 constant_dynamic-slice_fusion.5
  836.4 17.8 %collective-permute-done.12 = bf16[128,4096]{1,0:T(8,128)(2,1)} collective-permute-done((bf16[128,4096]{1,0:T(8,128)(2,1)}, bf16[128,4096]{1,0:T(8,128)(2,1)}, u32[]{:S(2)}, u32[]{:S(2)}) %collective-permute-start.12) | collective-permute-done | bytes 1048608 | tf_op jit(solution)/shard_map/ppermute | solution.py:387
  856.9 22.3 %all-to-all-done.4 = bf16[16,128,512]{1,2,0:T(8,128)(2,1)S(1)} async-done(((bf16[16,128,512]{1,2,0:T(8,128)(2,1)}), bf16[16,128,512]{1,2,0:T(8,128)(2,1)S(1)}, u32[]{:S(2)}, u32[]{:S(2)}) %all-to-all-start.4) | async-done | bytes 2097184 | tf_op jit(solution)/shard_map/all_to_all | solution.py:463
  888.4 2.8 broadcast_in_dim.116
  891.1 23.6 %all-to-all-start.5 = ((bf16[16,128,576]{1,2,0:T(8,128)(2,1)}), bf16[16,128,576]{1,2,0:T(8,128)(2,1)}, u32[]{:S(2)}, u32[]{:S(2)}) async-start(bf16[16,128,576]{1,2,0:T(8,128)(2,1)} %broadcast_in_dim.116), calls=%async_computation.7 | async-start | bytes 4718592 | tf_op jit(solution)/shard_map/all_to_all | solution.py:463
  915.5 6.2 collective-permute-done.10
  924.4 2.7 constant_dynamic-slice_fusion.2
  928.0 5.0 convolution_dynamic-update-slice_fusion.1
  933.1 3.1 convolution_dynamic-update-slice_fusion.3
  936.2 3.2 convolution_dynamic-update-slice_fusion.2
  941.1 44.4 %all-to-all-done.5 = bf16[16,128,576]{1,2,0:T(8,128)(2,1)} async-done(((bf16[16,128,576]{1,2,0:T(8,128)(2,1)}), bf16[16,128,576]{1,2,0:T(8,128)(2,1)}, u32[]{:S(2)}, u32[]{:S(2)}) %all-to-all-start.5) | async-done | bytes 2359328 | tf_op jit(solution)/shard_map/all_to_all | solution.py:463
  985.5 3.2 fusion.5
  990.1 120.1 %collective-permute-done.14 = bf16[68,576]{0,1:T(8,128)(2,1)S(1)} collective-permute-done((bf16[68,576]{0,1:T(8,128)(2,1)S(1)}, bf16[68,576]{0,1:T(8,128)(2,1)S(1)}, u32[]{:S(2)}, u32[]{:S(2)}) %collective-permute-start.14) | collective-permute-done | bytes 78368 | tf_op jit(solution)/shard_map/ppermute | solution.py:390
  1111.7 6.9 all-to-all-start.6
  1118.6 9.9 add_bitcast_fusion.1
  1128.5 12.6 %add_bitcast_fusion = f32[1,1024,2816]{2,1,0:T(8,128)} fusion(bf16[1024,2816]{1,0:T(8,128)(2,1)} %collective-permute-done.16, bf16[1024,2816]{1,0:T(8,128)(2,1)} %pad_maximum_fusion.3, bf16[1024,2048]{1,0:T(8,128)(2,1)S(1)} %bitcast.180), kind=kOutput, calls=%fused_computation.1 | convolution fusion | flops 5911347200 | bytes 25165824 | tf_op jit(solution)/shard_map/dot_general | solution.py:79
  1141.1 23.7 %all-to-all-done.6 = bf16[16,68,576]{2,1,0:T(8,128)(2,1)S(1)} async-done(((bf16[16,68,576]{2,1,0:T(8,128)(2,1)}), bf16[16,68,576]{2,1,0:T(8,128)(2,1)S(1)}, u32[]{:S(2)}, u32[]{:S(2)}) %all-to-all-start.6) | async-done | bytes 1253408 | tf_op jit(solution)/shard_map/all_to_all | solution.py:463
  1166.9 3.2 copy.210
  1171.3 3.0 multiply_add_fusion
  1174.3 13.2 %shard_map.259 = (f32[1024,2048]{1,0:T(8,128)}, f32[1024,3072]{1,0:T(8,128)}) custom-call(bf16[16,1024,384]{2,1,0:T(8,128)(2,1)} %bitcast.165), custom_call_target="tpu_custom_call" | custom-call | bytes 37748736 | tf_op jit(solution)/shard_map/pallas_call | solution.py:337
  1187.5 4.9 shard_map.260
  1192.4 17.3 %shard_map.261 = f32[1024,5632]{1,0:T(8,128)} custom-call(bf16[16,528,1024]{2,1,0:T(8,128)(2,1)} %bitcast.163), custom_call_target="tpu_custom_call" | custom-call | bytes 34603008 | tf_op jit(solution)/shard_map/pallas_call | solution.py:274
  1209.8 11.7 shard_map.262
  (341 shorter events, 128.8 us)
Async XLA Ops:
  7.2 88.3 %copy-start = (bf16[1024,576]{0,1:T(8,128)(2,1)S(1)}, bf16[1024,576]{0,1:T(8,128)(2,1)}, u32[]{:S(2)}) copy-start(bf16[1024,576]{0,1:T(8,128)(2,1)} %param.23) | copy-start | bytes 3538948
  7.2 86.7 %all-gather.9.cloned.1.call-start = ((), (), s32[]{:S(2)}) async-start(), calls=%async_computation.9 | async-start | bytes 8912896 | tf_op jit(solution)/shard_map/all_gather | solution.py:457
  9.7 3.5 collective-permute-start
  13.1 80.8 %copy-start.57 = (f32[128]{0:T(128)}, f32[128]{0:T(128)S(1)}, u32[]{:S(2)}) copy-start(f32[128]{0:T(128)S(1)} %rsqrt.38) | copy-start | bytes 1540
  16.8 81.1 %copy-start.55 = (f32[2,1,64,6]{2,1,3,0:T(1,128)S(1)}, f32[2,1,64,6]{2,1,3,0:T(1,128)}, u32[]{:S(2)}) copy-start(f32[2,1,64,6]{2,1,3,0:T(1,128)} %param.20) | copy-start | bytes 9220
  16.8 81.2 %copy-start.56 = (s32[2,1,64,6]{2,1,3,0:T(1,128)S(1)}, s32[2,1,64,6]{2,1,3,0:T(1,128)}, u32[]{:S(2)}) copy-start(s32[2,1,64,6]{2,1,3,0:T(1,128)} %param.19) | copy-start | bytes 9220
  16.9 434.3 %all-gather.13.cloned.1.call-start = ((), (), s32[]{:S(2)}) async-start(), calls=%async_computation.11 | async-start | bytes 8912896 | tf_op jit(solution)/shard_map/all_gather | solution.py:457
  96.8 39.7 %collective-permute-start.1 = (bf16[1024,768]{0,1:T(8,128)(2,1)}, bf16[1024,768]{0,1:T(8,128)(2,1)S(1)}, u32[]{:S(2)}, u32[]{:S(2)}) collective-permute-start(bf16[1024,768]{0,1:T(8,128)(2,1)} %pad_maximum_fusion.7), channel_id=1, source_target_pairs={{16,0},{0,16},{17,1},{1,17},{18,2},{2,18},{19,3},{3,19},{20,4},{4,... | collective-permute-start | bytes 4718600 | tf_op jit(solution)/shard_map/ppermute | solution.py:387
  98.8 18.0 %all-to-all-start = ((f32[16,1,128]{2,1,0:T(1,128)}), f32[16,1,128]{2,1,0:T(1,128)}, u32[]{:S(2)}, u32[]{:S(2)}) async-start(f32[16,1,128]{2,1,0:T(1,128)} %bitcast.2), calls=%async_computation | async-start | bytes 16384 | tf_op jit(solution)/shard_map/all_to_all | solution.py:463
  104.3 31.3 %collective-permute-start.2 = (bf16[256,256]{1,0:T(8,128)(2,1)S(1)}, bf16[256,256]{1,0:T(8,128)(2,1)}, u32[]{:S(2)}, u32[]{:S(2)}) collective-permute-start(bf16[256,256]{1,0:T(8,128)(2,1)S(1)} %get-tuple-element.138), channel_id=1, source_target_pairs={{16,0},{0,16},{17,1},{1,17},{18,2},{2,18},{19,3},{3,19},{20,4},{4,... | collective-permute-start | bytes 393224 | tf_op jit(solution)/shard_map/ppermute | solution.py:387
  107.8 72.8 %collective-permute-start.3 = (bf16[512,2048]{1,0:T(8,128)(2,1)}, bf16[512,2048]{1,0:T(8,128)(2,1)}, u32[]{:S(2)}, u32[]{:S(2)}) collective-permute-start(bf16[512,2048]{1,0:T(8,128)(2,1)} %constant_dynamic-slice_fusion.12), channel_id=1, source_target_pairs={{16,0},{0,16},{17,1},{1,17},{18,2},{2,18},{19,3},{3,19},{20,4},{4,... | collective-permute-start | bytes 6291464 | tf_op jit(solution)/shard_map/ppermute | solution.py:387
  138.4 43.3 %slice-start.3 = ((s8[8388608]{0:T(1024)(128)(4,1)}), s8[4194304]{0:T(1024)(128)(4,1)S(1)}, s32[]{:S(2)}) async-start(s8[8388608]{0:T(1024)(128)(4,1)} %bitcast.209), calls=%async_computation.20 | async-start | bytes 8388608
  138.5 43.2 %slice-start.4 = ((s8[8388608]{0:T(1024)(128)(4,1)}), s8[4194304]{0:T(1024)(128)(4,1)S(1)}, s32[]{:S(2)}) async-start(s8[8388608]{0:T(1024)(128)(4,1)} %bitcast.209), calls=%async_computation.21 | async-start | bytes 8388608
  138.5 53.3 %copy-start.34 = (f32[16,64,128]{2,1,0:T(8,128)S(1)}, f32[16,64,128]{2,1,0:T(8,128)}, u32[]{:S(2)}) copy-start(f32[16,64,128]{2,1,0:T(8,128)} %get-tuple-element.179) | copy-start | bytes 1572868
  138.6 53.3 %copy-start.35 = (f32[16,64,128]{2,1,0:T(8,128)S(1)}, f32[16,64,128]{2,1,0:T(8,128)}, u32[]{:S(2)}) copy-start(f32[16,64,128]{2,1,0:T(8,128)} %get-tuple-element.180) | copy-start | bytes 1572868
  180.5 49.4 %collective-permute-start.4 = (bf16[512,2048]{1,0:T(8,128)(2,1)}, bf16[512,2048]{1,0:T(8,128)(2,1)S(1)}, u32[]{:S(2)}, u32[]{:S(2)}) collective-permute-start(bf16[512,2048]{1,0:T(8,128)(2,1)} %collective-permute-done.3), channel_id=1, source_target_pairs={{0,1},{1,0},{2,3},{3,2},{4,5},{5,4},{6,7},{7,6},{8,9},{9,8},{10,11... | collective-permute-start | bytes 6291464 | tf_op jit(solution)/shard_map/ppermute | solution.py:437
  195.8 9.5 copy-start.50
  197.5 13.3 %copy-start.52 = (f32[1,8,2,128]{3,2,1,0:T(2,128)S(1)}, f32[1,8,2,128]{3,2,1,0:T(2,128)}, u32[]{:S(2)}) copy-start(f32[1,8,2,128]{3,2,1,0:T(2,128)} %get-tuple-element.171) | copy-start | bytes 24580
  207.3 17.4 %all-to-all-start.1 = ((bf16[16,128,128]{1,2,0:T(8,128)(2,1)}), bf16[16,128,128]{1,2,0:T(8,128)(2,1)S(1)}, u32[]{:S(2)}, u32[]{:S(2)}) async-start(bf16[16,128,128]{1,2,0:T(8,128)(2,1)} %copy.182), calls=%async_computation.1 | async-start | bytes 1048576 | tf_op jit(solution)/shard_map/all_to_all | solution.py:463
  210.7 247.5 %all-gather.11.cloned.1.call-start = ((), (), s32[]{:S(2)}) async-start(), calls=%async_computation.10 | async-start | bytes 8912896 | tf_op jit(solution)/shard_map/all_gather | solution.py:457
  210.8 19.8 %copy-start.44 = (f32[1,8,2,128]{3,1,2,0:T(8,128)}, f32[1,8,2,128]{3,1,2,0:T(8,128)S(1)}, u32[]{:S(2)}) copy-start(f32[1,8,2,128]{3,1,2,0:T(8,128)S(1)} %copy.234) | copy-start | bytes 24580
  232.9 411.7 %reduce-scatter.3.cloned.1.call-start = ((), (), s32[]{:S(2)}) async-start(), calls=%async_computation.13 | async-start | bytes 8912896 | tf_op jit(solution)/shard_map/reduce_scatter | solution.py:469
  233.0 213.8 %collective-permute-start.5 = (bf16[704,2048]{1,0:T(8,128)(2,1)}, bf16[704,2048]{1,0:T(8,128)(2,1)}, u32[]{:S(2)}, u32[]{:S(2)}) collective-permute-start(bf16[704,2048]{1,0:T(8,128)(2,1)} %bitcast.188), channel_id=1, source_target_pairs={{16,0},{0,16},{17,1},{1,17},{18,2},{2,18},{19,3},{3,19},{20,4},{4,... | collective-permute-start | bytes 8650760 | tf_op jit(solution)/shard_map/ppermute | solution.py:387
  234.2 243.0 %collective-permute-start.6 = (bf16[1024,2816]{1,0:T(8,128)(2,1)}, bf16[1024,2816]{1,0:T(8,128)(2,1)}, u32[]{:S(2)}, u32[]{:S(2)}) collective-permute-start(bf16[1024,2816]{1,0:T(8,128)(2,1)} %bitcast.215), channel_id=1, source_target_pairs={{16,0},{0,16},{17,1},{1,17},{18,2},{2,18},{19,3},{3,19},{20,4},{4,... | collective-permute-start | bytes 17301512 | tf_op jit(solution)/shard_map/ppermute | solution.py:387
  236.4 7.5 copy-start.31
  236.5 7.5 copy-start.32
  236.5 7.5 copy-start.33
  237.3 207.5 %collective-permute-start.8 = (bf16[1024,352]{0,1:T(8,128)(2,1)S(1)}, bf16[1024,352]{0,1:T(8,128)(2,1)S(1)}, u32[]{:S(2)}, u32[]{:S(2)}) collective-permute-start(bf16[1024,352]{0,1:T(8,128)(2,1)S(1)} %copy.183), channel_id=1, source_target_pairs={{16,0},{0,16},{17,1},{1,17},{18,2},{2,18},{19,3},{3,19},{20,4},{4,... | collective-permute-start | bytes 2162696 | tf_op jit(solution)/shard_map/ppermute | solution.py:387
  240.4 203.4 %collective-permute-start.7 = (bf16[88,2048]{1,0:T(8,128)(2,1)}, bf16[88,2048]{1,0:T(8,128)(2,1)}, u32[]{:S(2)}, u32[]{:S(2)}) collective-permute-start(bf16[88,2048]{1,0:T(8,128)(2,1)} %get-tuple-element.134), channel_id=1, source_target_pairs={{16,0},{0,16},{17,1},{1,17},{18,2},{2,18},{19,3},{3,19},{20,4},{4,... | collective-permute-start | bytes 1081352 | tf_op jit(solution)/shard_map/ppermute | solution.py:387
  444.8 21.4 %copy-start.29 = (bf16[176,2048]{1,0:T(8,128)(2,1)}, bf16[176,2048]{1,0:T(8,128)(2,1)S(1)}, u32[]{:S(2)}) copy-start(bf16[176,2048]{1,0:T(8,128)(2,1)S(1)} %constant_dynamic-update-slice_fusion.1.weight_ref) | copy-start | bytes 2162692
  446.8 11.5 copy-start.18
  458.3 17.7 %slice-start = ((s8[8388608]{0:T(1024)(128)(4,1)}), s8[4194304]{0:T(1024)(128)(4,1)S(1)}, s32[]{:S(2)}) async-start(s8[8388608]{0:T(1024)(128)(4,1)} %bitcast.167), calls=%async_computation.17 | async-start | bytes 8388608
  466.2 9.8 slice-start.1
  479.2 17.2 %copy-start.7 = (bf16[1024,2048]{1,0:T(8,128)(2,1)S(1)}, bf16[1024,2048]{1,0:T(8,128)(2,1)}, u32[]{:S(2)}) copy-start(bf16[1024,2048]{1,0:T(8,128)(2,1)} %fusion) | copy-start | bytes 12582916
  541.2 203.1 %all-gather.15.cloned.1.call-start = ((), (), s32[]{:S(2)}) async-start(), calls=%async_computation.12 | async-start | bytes 8912896 | tf_op jit(solution)/shard_map/all_gather | solution.py:457
  558.3 11.1 copy-start.38
  569.3 7.4 copy-start.12
  576.7 68.0 %copy-start.3 = (f32[128,2048]{1,0:T(8,128)S(1)}, f32[128,2048]{1,0:T(8,128)}, u32[]{:S(2)}) copy-start(f32[128,2048]{1,0:T(8,128)} %copy-done.2) | copy-start | bytes 3145732
  576.7 68.0 %copy-start.45 = (f32[1,8,2,128]{3,1,2,0:T(8,128)S(1)}, f32[1,8,2,128]{3,1,2,0:T(8,128)}, u32[]{:S(2)}) copy-start(f32[1,8,2,128]{3,1,2,0:T(8,128)} %copy-done.44) | copy-start | bytes 24580
  576.7 68.0 %copy-start.54 = (f32[128]{0:T(128)S(1)}, f32[128]{0:T(128)}, u32[]{:S(2)}) copy-start(f32[128]{0:T(128)} %copy-done.53) | copy-start | bytes 1540
  576.7 69.7 %copy-start.22 = (bf16[2,1,64,2048]{3,2,1,0:T(8,128)(2,1)S(1)}, bf16[2,1,64,2048]{3,2,1,0:T(8,128)(2,1)}, u32[]{:S(2)}) copy-start(bf16[2,1,64,2048]{3,2,1,0:T(8,128)(2,1)} %param.17) | copy-start | bytes 1572868
  653.1 26.0 %all-to-all-start.2 = ((bf16[16,128,128]{2,1,0:T(8,128)(2,1)}), bf16[16,128,128]{2,1,0:T(8,128)(2,1)S(1)}, u32[]{:S(2)}, u32[]{:S(2)}) async-start(bf16[16,128,128]{2,1,0:T(8,128)(2,1)} %bitcast_bitcast_fusion.1), calls=%async_computation.3 | async-start | bytes 1048576 | tf_op jit(solution)/shard_map/all_to_all | solution.py:463
  679.0 10.5 copy-start.40
  680.0 32.2 %all-to-all-start.3 = ((bf16[16,128,128]{2,1,0:T(8,128)(2,1)}), bf16[16,128,128]{2,1,0:T(8,128)(2,1)S(1)}, u32[]{:S(2)}, u32[]{:S(2)}) async-start(bf16[16,128,128]{2,1,0:T(8,128)(2,1)} %bitcast_bitcast_fusion), calls=%async_computation.4 | async-start | bytes 1048576 | tf_op jit(solution)/shard_map/all_to_all | solution.py:463
  689.5 481.8 %reduce-scatter.5.cloned.1.call-start = ((), (), s32[]{:S(2)}) async-start(), calls=%async_computation.14 | async-start | bytes 8912896 | tf_op jit(solution)/shard_map/reduce_scatter | solution.py:469
  712.2 32.1 %copy-start.41 = (bf16[16,128,128]{2,1,0:T(8,128)(2,1)}, bf16[16,128,128]{2,1,0:T(8,128)(2,1)S(1)}, u32[]{:S(2)}) copy-start(bf16[16,128,128]{2,1,0:T(8,128)(2,1)S(1)} %all-to-all-done.3) | copy-start | bytes 1572868
  751.4 19.1 %collective-permute-start.9 = (bf16[1024,384]{1,0:T(8,128)(2,1)}, bf16[1024,384]{1,0:T(8,128)(2,1)}, u32[]{:S(2)}, u32[]{:S(2)}) collective-permute-start(bf16[1024,384]{1,0:T(8,128)(2,1)} %maximum_maximum_fusion), channel_id=1, source_target_pairs={{0,16},{16,0},{1,17},{17,1},{2,18},{18,2},{3,19},{19,3},{4,20},{20... | collective-permute-start | bytes 2359304 | tf_op jit(solution)/shard_map/ppermute | solution.py:390
  773.0 401.3 %all-gather.17.cloned.1.call-start = ((), (), s32[]{:S(2)}) async-start(), calls=%async_computation.15 | async-start | bytes 13369344 | tf_op jit(solution)/shard_map/all_gather | solution.py:460
  773.8 418.6 %all-gather.19.cloned.1.call-start = ((), (), s32[]{:S(2)}) async-start(), calls=%async_computation.16 | async-start | bytes 18382848 | tf_op jit(solution)/shard_map/all_gather | solution.py:460
  788.4 25.7 %slice-start.2 = ((f32[352,2048]{1,0:T(8,128)}), f32[352,1024]{1,0:T(8,128)S(1)}, s32[]{:S(2)}) async-start(f32[352,2048]{1,0:T(8,128)} %copy-done.14), calls=%async_computation.19 | async-start | bytes 2883584 | tf_op jit(solution)/shard_map/slice | solution.py:590
  789.4 24.6 %collective-permute-start.15 = (bf16[528,1024]{1,0:T(8,128)(2,1)}, bf16[528,1024]{1,0:T(8,128)(2,1)}, u32[]{:S(2)}, u32[]{:S(2)}) collective-permute-start(bf16[528,1024]{1,0:T(8,128)(2,1)} %pad_maximum_fusion.10), channel_id=1, source_target_pairs={{0,16},{16,0},{1,17},{17,1},{2,18},{18,2},{3,19},{19,3},{4,20},{20... | collective-permute-start | bytes 3244040 | tf_op jit(solution)/shard_map/ppermute | solution.py:390
  820.6 58.6 %all-to-all-start.4 = ((bf16[16,128,512]{1,2,0:T(8,128)(2,1)}), bf16[16,128,512]{1,2,0:T(8,128)(2,1)S(1)}, u32[]{:S(2)}, u32[]{:S(2)}) async-start(bf16[16,128,512]{1,2,0:T(8,128)(2,1)} %copy.198), calls=%async_computation.6 | async-start | bytes 4194304 | tf_op jit(solution)/shard_map/all_to_all | solution.py:463
  829.3 24.9 %collective-permute-start.12 = (bf16[128,4096]{1,0:T(8,128)(2,1)}, bf16[128,4096]{1,0:T(8,128)(2,1)}, u32[]{:S(2)}, u32[]{:S(2)}) collective-permute-start(bf16[128,4096]{1,0:T(8,128)(2,1)} %constant_dynamic-slice_fusion.4), channel_id=1, source_target_pairs={{16,0},{0,16},{17,1},{1,17},{18,2},{2,18},{19,3},{3,19},{20,4},{4,... | collective-permute-start | bytes 3145736 | tf_op jit(solution)/shard_map/ppermute | solution.py:387
  834.3 87.3 %collective-permute-start.10 = (bf16[512,3072]{1,0:T(8,128)(2,1)}, bf16[512,3072]{1,0:T(8,128)(2,1)}, u32[]{:S(2)}, u32[]{:S(2)}) collective-permute-start(bf16[512,3072]{1,0:T(8,128)(2,1)} %constant_dynamic-slice_fusion.5), channel_id=1, source_target_pairs={{16,0},{0,16},{17,1},{1,17},{18,2},{2,18},{19,3},{3,19},{20,4},{4,... | collective-permute-start | bytes 9437192 | tf_op jit(solution)/shard_map/ppermute | solution.py:387
  854.2 29.3 %collective-permute-start.13 = (bf16[128,4096]{1,0:T(8,128)(2,1)}, bf16[128,4096]{1,0:T(8,128)(2,1)}, u32[]{:S(2)}, u32[]{:S(2)}) collective-permute-start(bf16[128,4096]{1,0:T(8,128)(2,1)} %collective-permute-done.12), channel_id=1, source_target_pairs={{0,1},{1,0},{2,3},{3,2},{4,5},{5,4},{6,7},{7,6},{8,9},{9,8},{10,11... | collective-permute-start | bytes 3145736 | tf_op jit(solution)/shard_map/ppermute | solution.py:437
  891.1 94.4 %all-to-all-start.5 = ((bf16[16,128,576]{1,2,0:T(8,128)(2,1)}), bf16[16,128,576]{1,2,0:T(8,128)(2,1)}, u32[]{:S(2)}, u32[]{:S(2)}) async-start(bf16[16,128,576]{1,2,0:T(8,128)(2,1)} %broadcast_in_dim.116), calls=%async_computation.7 | async-start | bytes 4718592 | tf_op jit(solution)/shard_map/all_to_all | solution.py:463
  914.7 213.8 %collective-permute-start.16 = (bf16[1024,2816]{1,0:T(8,128)(2,1)}, bf16[1024,2816]{1,0:T(8,128)(2,1)}, u32[]{:S(2)}, u32[]{:S(2)}) collective-permute-start(bf16[1024,2816]{1,0:T(8,128)(2,1)} %convolution_convert_fusion), channel_id=1, source_target_pairs={{0,16},{16,0},{1,17},{17,1},{2,18},{18,2},{3,19},{19,3},{4,20},{20... | collective-permute-start | bytes 17301512 | tf_op jit(solution)/shard_map/ppermute | solution.py:390
  921.7 14.6 %collective-permute-start.11 = (bf16[512,3072]{1,0:T(8,128)(2,1)}, bf16[512,3072]{1,0:T(8,128)(2,1)}, u32[]{:S(2)}, u32[]{:S(2)}) collective-permute-start(bf16[512,3072]{1,0:T(8,128)(2,1)} %collective-permute-done.10), channel_id=1, source_target_pairs={{0,1},{1,0},{2,3},{3,2},{4,5},{5,4},{6,7},{7,6},{8,9},{9,8},{10,11... | collective-permute-start | bytes 9437192 | tf_op jit(solution)/shard_map/ppermute | solution.py:437
  923.2 195.4 %collective-permute-start.17 = (bf16[704,2048]{1,0:T(8,128)(2,1)}, bf16[704,2048]{1,0:T(8,128)(2,1)}, u32[]{:S(2)}, u32[]{:S(2)}) collective-permute-start(bf16[704,2048]{1,0:T(8,128)(2,1)} %convolution_convert_fusion.2), channel_id=1, source_target_pairs={{0,16},{16,0},{1,17},{17,1},{2,18},{18,2},{3,19},{19,3},{4,20},{20... | collective-permute-start | bytes 8650760 | tf_op jit(solution)/shard_map/ppermute | solution.py:390
  936.2 49.3 %copy-start.42 = (bf16[2048,64]{1,0:T(8,128)(2,1)S(1)}, bf16[2048,64]{1,0:T(8,128)(2,1)}, u32[]{:S(2)}) copy-start(bf16[2048,64]{1,0:T(8,128)(2,1)} %get-tuple-element.146) | copy-start | bytes 786436
  936.2 49.3 %copy-start.43 = (bf16[2048,64]{1,0:T(8,128)(2,1)S(1)}, bf16[2048,64]{1,0:T(8,128)(2,1)}, u32[]{:S(2)}) copy-start(bf16[2048,64]{1,0:T(8,128)(2,1)} %get-tuple-element.147) | copy-start | bytes 786436
  989.0 121.2 %collective-permute-start.14 = (bf16[68,576]{0,1:T(8,128)(2,1)S(1)}, bf16[68,576]{0,1:T(8,128)(2,1)S(1)}, u32[]{:S(2)}, u32[]{:S(2)}) collective-permute-start(bf16[68,576]{0,1:T(8,128)(2,1)S(1)} %pad_maximum_fusion.15), channel_id=1, source_target_pairs={{0,16},{16,0},{1,17},{17,1},{2,18},{18,2},{3,19},{19,3},{4,20},{20... | collective-permute-start | bytes 235016 | tf_op jit(solution)/shard_map/ppermute | solution.py:390
  1111.7 53.1 %all-to-all-start.6 = ((bf16[16,68,576]{2,1,0:T(8,128)(2,1)}), bf16[16,68,576]{2,1,0:T(8,128)(2,1)S(1)}, u32[]{:S(2)}, u32[]{:S(2)}) async-start(bf16[16,68,576]{2,1,0:T(8,128)(2,1)} %broadcast_in_dim.117), calls=%async_computation.8 | async-start | bytes 2949120 | tf_op jit(solution)/shard_map/all_to_all | solution.py:463
  1118.6 9.9 copy-start.13
  (37 other events, 119.6 us)
Sparse Core Ops, SparseCore 0:
  17.0 76.8 all-gather.8
  96.1 72.8 all-gather.12
  233.1 73.8 all-gather.10
  541.3 103.2 reduce-scatter.2
  646.7 97.5 all-gather.14
  773.1 131.6 reduce-scatter.4
  907.1 141.1 all-gather.16
  1049.9 114.1 all-gather.18

commit v3 on v2

--- a/solution.py
+++ b/solution.py
@@ -306,8 +306,8 @@
         out_ref[:, e * count : (e + 1) * count] = whole
 
 
-def kvup_columns(stacked, start, height):
-    groups, rows, count = stacked.shape
+def kvup_columns(stacked, rows, start, height):
+    groups, _, count = stacked.shape
     tile = start // 128
     width = (count - start) * (rows // height)
     return pl.pallas_call(
@@ -331,8 +331,8 @@
         )
 
 
-def attn_columns(stacked, a, b):
-    groups, rows, count = stacked.shape
+def attn_columns(stacked, rows, a, b):
+    groups, _, count = stacked.shape
     size = min(128, rows)
     return pl.pallas_call(
         functools.partial(attn_columns_kernel, a=a, b=b),
@@ -462,9 +462,6 @@
     def swap(x):
         return lax.all_to_all(x, "expert", split_axis=0, concat_axis=0, tiled=True)
 
-    def broadcast(x):
-        return swap(jnp.broadcast_to(x[None], (groups,) + x.shape))
-
     def collect(x):
         return lax.psum_scatter(x, "expert", scatter_dimension=0, tiled=True)
 
@@ -624,6 +621,7 @@
     dhid_sum = after(dhid_sum, out_part, *sent_in, *sent_out)
     got_in = [send(x, r).astype(f32) for r, x in enumerate(sent_in, 1)]
     got_out = [send(x, r).astype(f32) for r, x in enumerate(sent_out, 1)]
+    out_sum = collect(after(out_part, dhid_sum))
     dhid = natural(dhid_sum, 1).astype(f32)
 
     dy = dy_own.astype(f32)
@@ -662,9 +660,6 @@
         )
 
     g_attn = exchanged(attn_grads(0), lambda r: attn_grads(r).astype(bf16))
-    g_attn = g_attn.astype(bf16)
-    out_sum = collect(after(out_part, g_attn))
-    g_attn = stack(row_major(g_attn))
 
     dq_own = back_of(moved, 0, qk)
     dkvup_own = back_of(moved, 256, 512)
@@ -676,37 +671,38 @@
     dlatent_raw, g_kv_gain = normed_back(latent_own, gain_kv, dlatent)
     dkvfull = jnp.concatenate([dlatent_raw, rotate_back(dkrope_own, cos_own, sin_own)], -1)
     dkvfull = dkvfull.astype(bf16)
-    dkv_all = broadcast(dkvfull).reshape(total, LATENT + ROPE)
     dact = dot_pieces_t(dq_own, wq) + natural(dot_nt(dkvfull, w_down), 1)
     dx_norm, g_attn_gain = normed_back(x_own.astype(f32), gain_attn, dact)
     input_grad = dx1 + dx_norm
 
-    step = width // (parts * groups)
-    act_rows = jnp.concatenate(
-        [
-            lax.dynamic_slice_in_dim(act, c * size + me * step, step, 1)
-            for c in range(parts)
-        ],
-        1,
-    )
-    g_down = dot_tn(act_rows, dkv_all)
-
-    def last_grads(r):
+    g_down = dot_tn(act_own, dkvfull)
+    down = LATENT + ROPE
+    gain_count = sum(gain_sizes)
+
+    def rest_grads(r):
         gains = [block_of(g, part + r) for g in (g_attn_gain, g_kv_gain, g_ffn_gain)]
-        gains = jnp.concatenate(gains).reshape(-1, LATENT + ROPE)
-        return jnp.concatenate([g_down[r * step : (r + 1) * step], gains], 0)
-
-    last = exchanged(last_grads(0), lambda r: last_grads(r).astype(bf16))
-    last = broadcast(last.astype(bf16))
-    g_down = last[:, :step].astype(f32).reshape(size, LATENT + ROPE)
-    gains = jnp.sum(last[:, step:].astype(f32), 0).reshape(-1)
+        gains = jnp.concatenate(gains).reshape(groups, 1, gain_count // groups)
+        gains = jnp.pad(gains, ((0, 0), (0, 0), (0, down - gain_count // groups)))
+        rows_of = block_of(g_down, part + r).reshape(groups, size // groups, down)
+        return jnp.concatenate([rows_of, gains], 1)
+
+    rest = exchanged(rest_grads(0), lambda r: rest_grads(r).astype(bf16))
+    rest = jnp.sum(swap(rest.astype(bf16)).astype(f32), 0).astype(bf16)
+    count = g_attn.shape[1]
+    extra = rest[:-1].reshape(-1, count)
+    extra_rows = extra.shape[0]
+    extra = jnp.concatenate([extra, jnp.pad(rest[-1:], ((0, 15), (0, 0)))[:, :count]], 0)
+    g_attn = jnp.concatenate([g_attn.astype(bf16), extra], 0)
+    g_attn = stack(row_major(g_attn))
+    g_down = g_attn[:, size : size + extra_rows].astype(f32).reshape(size, down)
+    gains = g_attn[:, size + extra_rows, : gain_count // groups].astype(f32).reshape(-1)
     gains = jnp.split(gains, cuts)
 
     mixed = (x1 + out_sum.astype(f32)).astype(bf16)
     g_ein = sum(got_in, expert_in_grad(0))
     g_eout = sum(got_out, expert_out_grad(0))
-    out_grad, query_grad = attn_columns(g_attn, width // groups, qk)
-    kvup_grad = kvup_columns(g_attn, width // groups + qk, LATENT // parts)
+    out_grad, query_grad = attn_columns(g_attn, size, width // groups, qk)
+    kvup_grad = kvup_columns(g_attn, size, width // groups + qk, LATENT // parts)
     shared_in_grad, shared_out_grad = shared_rows(g_shared, 2 * parts, run)
     return (
         mixed.reshape(micro, 1, rows, width),

time: 1240 us -> 1260 us (1.016)
  waiting for transfers between devices: 724 us -> 760 us
  starting transfers between devices: 78.7 us -> 52.6 us
    ppermute x5, waiting for transfers between devices: 157 us -> 229 us  [send(): lax.ppermute(x, 'dp', [(i, (i + step) % parts) for i in range(parts)])]
    all_to_all x7 -> x6, waiting for transfers between devices: 123 us -> 52.4 us  [swap(): return lax.all_to_all(x, 'expert', split_axis=0, concat_axis=0, tiled=True)]
    ppermute x10, waiting for transfers between devices: 277 us -> 342 us  [shift(): lax.ppermute(x, 'dp', [((i + step) % parts, i) for i in range(parts)])]
    all_gather x4, waiting for transfers between devices: 109 us -> 77 us  [spread(): return lax.all_gather(x, 'expert', axis=0, tiled=True)]
    all_to_all x7 -> x6, starting transfers between devices: 59.6 us -> 35.4 us  [swap(): return lax.all_to_all(x, 'expert', split_axis=0, concat_axis=0, tiled=True)]
  transfers between devices with their start and end apart: 33 -> 32, of which waited for: 17 -> 13; matrix products, arithmetic and copies ran while one was open for 20% -> 21% of each run, Pallas kernels for 4% -> 5%
where the time goes in v3:
time: 1260 us; the launch traced here: 1250 us
  waiting for transfers between devices  760 us (60%)
  matrix products  187 us (15%)
  Pallas kernels  88.3 us (7%)
  local copies, waits for them, and re-layouts  81.6 us (6%)
  other arithmetic  65.3 us (5%)
  starting transfers between devices  52.6 us (4%)
  between operations  15.8 us (1%)
    ppermute x10, waiting for transfers between devices, shift(): lax.ppermute(x, 'dp', [((i + step) % parts, i) for i in range(parts)])  342 us
    ppermute x5, waiting for transfers between devices, send(): lax.ppermute(x, 'dp', [(i, (i + step) % parts) for i in range(parts)])  229 us
    all_gather x4, waiting for transfers between devices, spread(): return lax.all_gather(x, 'expert', axis=0, tiled=True)  77 us
    dot_general x10, matrix products, dot_tn(): lax.dot_general(left, right, (((0,), (0,)), ((), ())), preferred_element_...  65.7 us
    dot_general x13, matrix products, dot_nt(): lax.dot_general(left, right, (((1,), (1,)), ((), ())), preferred_element_...  61.7 us
    reduce_scatter x2, waiting for transfers between devices, collect(): return lax.psum_scatter(x, 'expert', scatter_dimension=0, tiled=True)  59.3 us
    dot_general x8, matrix products, dot(): return jnp.dot(left, right, preferred_element_type=f32)  54 us
    all_to_all x6, waiting for transfers between devices, swap(): return lax.all_to_all(x, 'expert', split_axis=0, concat_axis=0, tiled=True)  52.4 us
  transfers between devices with their start and end apart: 32, of which 13 were waited for; matrix products, arithmetic and copies ran while one was open for 21% of the time, Pallas kernels for 5%

profile of v3, /device:TPU:1, one launch (start us, length us, event | category | flops | bytes accessed | tf_op | source)
XLA Modules:
  0.0 1251.2 jit_solution(16517141563996393140)
XLA Ops:
  17.7 77.0 %all-gather.9.cloned.1.call-done = bf16[2048,2048]{1,0:T(8,128)(2,1)} async-done(((bf16[128,2048]{1,0:T(8,128)(2,1)}), bf16[2048,2048]{1,0:T(8,128)(2,1)}) %all-gather.9.cloned.1.call-update) | async-done | bytes 8388624 | tf_op jit(solution)/shard_map/all_gather | solution.py:457
  99.6 4.6 all-to-all-start
  105.5 3.2 constant_dynamic-slice_fusion.10
  120.8 15.6 %collective-permute-done.2 = bf16[256,256]{1,0:T(8,128)(2,1)} collective-permute-done((bf16[256,256]{1,0:T(8,128)(2,1)S(1)}, bf16[256,256]{1,0:T(8,128)(2,1)}, u32[]{:S(2)}, u32[]{:S(2)}) %collective-permute-start.2) | collective-permute-done | bytes 131104 | tf_op jit(solution)/shard_map/ppermute | solution.py:387
  139.4 41.9 %collective-permute-done.3 = bf16[512,2048]{1,0:T(8,128)(2,1)} collective-permute-done((bf16[512,2048]{1,0:T(8,128)(2,1)}, bf16[512,2048]{1,0:T(8,128)(2,1)}, u32[]{:S(2)}, u32[]{:S(2)}) %collective-permute-start.3) | collective-permute-done | bytes 2097184 | tf_op jit(solution)/shard_map/ppermute | solution.py:387
  182.5 9.5 fusion.83
  194.5 2.4 fusion.78
  198.7 7.7 shard_map.255
  208.4 3.5 all-to-all-start.1
  212.0 13.9 %all-to-all-done.1 = bf16[16,128,128]{1,2,0:T(8,128)(2,1)S(1)} async-done(((bf16[16,128,128]{1,2,0:T(8,128)(2,1)}), bf16[16,128,128]{1,2,0:T(8,128)(2,1)S(1)}, u32[]{:S(2)}, u32[]{:S(2)}) %all-to-all-start.1) | async-done | bytes 524320 | tf_op jit(solution)/shard_map/all_to_all | solution.py:463
  225.9 3.1 fusion.50
  241.8 3.3 broadcast_in_dim.101
  249.0 196.0 %collective-permute-done.7 = bf16[88,2048]{1,0:T(8,128)(2,1)} collective-permute-done((bf16[88,2048]{1,0:T(8,128)(2,1)}, bf16[88,2048]{1,0:T(8,128)(2,1)}, u32[]{:S(2)}, u32[]{:S(2)}) %collective-permute-start.7) | collective-permute-done | bytes 360480 | tf_op jit(solution)/shard_map/ppermute | solution.py:387
  448.0 4.3 constant_dynamic-update-slice_fusion.3
  452.3 4.6 fusion.45
  456.9 2.5 fusion
  459.4 7.9 fusion.84
  467.3 7.9 multiply_convert_fusion.7
  480.3 17.2 %fusion.2 = f32[1024,2816]{1,0:T(8,128)} fusion(bf16[1024,2048]{1,0:T(8,128)(2,1)S(1)} %bitcast.175, bf16[1024,2816]{1,0:T(8,128)(2,1)} %collective-permute-done.6, bf16[1024,2816]{1,0:T(8,128)(2,1)S(1)} %bitcast.216), kind=kOutput, calls=%fused_computation.6 | convolution fusion | flops 11834228736 | bytes 27262976 | tf_op jit(solution)/shard_map/dot_general | solution.py:75
  497.5 14.7 %multiply_convert_fusion.3 = (bf16[1024,1408]{1,0:T(8,128)(2,1)S(1)}, bf16[1024,1408]{1,0:T(8,128)(2,1)}, bf16[1024,1408]{1,0:T(8,128)(2,1)}) fusion(f32[1024,2816]{1,0:T(8,128)} %fusion.2, bf16[1024,2048]{1,0:T(8,128)(2,1)S(1)} %copy-done.8, bf16[1408,2048]{1,0:T(8,128)(2,1)} %constant_dynamic-update-slice_fusion.3), kind=kOutput, calls=%fused_computation.11 | convolution fusion | flops 5928648704 | bytes 30146560 | tf_op jit(solution)/shard_map/dot_general | solution.py:83
  512.2 17.6 %fusion.3.rows_ref = bf16[1024,2048]{1,0:T(8,128)(2,1)} fusion(bf16[1024,2816]{1,0:T(8,128)(2,1)} %collective-permute-done.6, bf16[1024,2816]{1,0:T(8,128)(2,1)} %bitcast.213, bf16[1024,1408]{1,0:T(8,128)(2,1)} %get-tuple-element.127, bf16[1024,1408]{1,0:T(8,128)(2,1)S(1)} %get-tuple-element.126), kind=kOutput, calls=%fused_computation.16 | convolution fusion | flops 11847860224 | bytes 21495808 | tf_op jit(solution)/shard_map/dot_general | solution.py:83
  529.9 12.5 %shard_map.256 = bf16[2048,2048]{1,0:T(8,128)(2,1)} custom-call(bf16[32,64,32]{2,1,0:T(8,128)(2,1)} %fusion.38.place_ref, bf16[1024,2048]{1,0:T(8,128)(2,1)} %fusion.3.rows_ref, bf16[2048,352]{1,0:T(8,128)(2,1)} %pad_maximum_fusion.9.units_ref, bf16[2048,352]{1,0:T(8,128)(2,1)} %copy-done.21), custom_call_target="tpu_custom_call" | custom-call | flops 3221225472 | bytes 15466496 | tf_op jit(solution)/shard_map/pallas_call | solution.py:230
  543.1 4.9 pad_maximum_fusion.3
  548.0 11.7 multiply_convert_fusion.rows_ref
  559.7 11.0 shard_map.257
  570.7 7.8 convolution_convert_fusion.2
  578.5 8.1 convolution_convert_fusion
  586.6 59.2 %reduce-scatter.3.cloned.1.call-done = bf16[128,2048]{1,0:T(8,128)(2,1)} async-done(((bf16[2048,2048]{1,0:T(8,128)(2,1)}), bf16[128,2048]{1,0:T(8,128)(2,1)}) %reduce-scatter.3.cloned.1.call-update) | async-done | bytes 524304 | tf_op jit(solution)/shard_map/reduce_scatter | solution.py:466
  646.0 5.8 fusion.86
  651.9 6.2 fusion.87
  662.9 21.9 %collective-permute-done.15 = bf16[528,1024]{1,0:T(8,128)(2,1)} collective-permute-done((bf16[528,1024]{1,0:T(8,128)(2,1)}, bf16[528,1024]{1,0:T(8,128)(2,1)}, u32[]{:S(2)}, u32[]{:S(2)}) %collective-permute-start.15) | collective-permute-done | bytes 1081376 | tf_op jit(solution)/shard_map/ppermute | solution.py:390
  684.7 2.7 fusion.10
  695.5 6.7 all-to-all-start.2
  705.4 20.0 %all-to-all-done.2 = bf16[16,128,128]{2,1,0:T(8,128)(2,1)S(1)} async-done(((bf16[16,128,128]{2,1,0:T(8,128)(2,1)}), bf16[16,128,128]{2,1,0:T(8,128)(2,1)S(1)}, u32[]{:S(2)}, u32[]{:S(2)}) %all-to-all-start.2) | async-done | bytes 524320 | tf_op jit(solution)/shard_map/all_to_all | solution.py:463
  726.2 9.9 shard_map.258
  736.1 3.9 copy.161
  740.0 7.3 all-to-all-start.3
  747.3 4.1 constant_dynamic-slice_fusion.4
  755.3 88.5 %collective-permute-done.11 = bf16[128,4096]{1,0:T(8,128)(2,1)} collective-permute-done((bf16[128,4096]{1,0:T(8,128)(2,1)}, bf16[128,4096]{1,0:T(8,128)(2,1)}, u32[]{:S(2)}, u32[]{:S(2)}) %collective-permute-start.11) | collective-permute-done | bytes 1048608 | tf_op jit(solution)/shard_map/ppermute | solution.py:387
  848.3 2.5 convolution_dynamic-update-slice_fusion.6
  857.8 5.1 convolution_dynamic-update-slice_fusion.1
  862.9 3.1 convolution_dynamic-update-slice_fusion.3
  866.1 3.2 convolution_dynamic-update-slice_fusion.2
  880.3 6.3 all-to-all-start.4
  886.6 6.7 fusion.33
  893.5 3.4 constant_dynamic-slice_fusion
  896.9 3.2 copy.173
  900.1 8.7 collective-permute-done.14
  908.8 3.4 fusion.5
  912.1 7.0 all-to-all-start.5
  919.6 3.7 fusion.31
  925.1 5.8 fusion.85
  938.1 13.1 %collective-permute-done.13 = bf16[1024,384]{1,0:T(8,128)(2,1)} collective-permute-done((bf16[1024,384]{1,0:T(8,128)(2,1)}, bf16[1024,384]{1,0:T(8,128)(2,1)}, u32[]{:S(2)}, u32[]{:S(2)}) %collective-permute-start.13) | collective-permute-done | bytes 786464 | tf_op jit(solution)/shard_map/ppermute | solution.py:390
  953.6 18.5 %all-to-all-done.5 = bf16[16,65,576]{2,1,0:T(8,128)(2,1)} async-done(((bf16[16,65,576]{2,1,0:T(8,128)(2,1)}), bf16[16,65,576]{2,1,0:T(8,128)(2,1)}, u32[]{:S(2)}, u32[]{:S(2)}) %all-to-all-start.5) | async-done | bytes 1198112 | tf_op jit(solution)/shard_map/all_to_all | solution.py:463
  977.6 185.5 %collective-permute-done.17 = bf16[704,2048]{1,0:T(8,128)(2,1)S(1)} collective-permute-done((bf16[704,2048]{1,0:T(8,128)(2,1)}, bf16[704,2048]{1,0:T(8,128)(2,1)S(1)}, u32[]{:S(2)}, u32[]{:S(2)}) %collective-permute-start.17) | collective-permute-done | bytes 2883616 | tf_op jit(solution)/shard_map/ppermute | solution.py:390
  1163.1 8.7 add_bitcast_fusion.1
  1171.8 12.1 add_bitcast_fusion
  1183.9 3.0 multiply_add_fusion
  1186.9 17.4 %shard_map.261 = f32[1024,5632]{1,0:T(8,128)} custom-call(bf16[16,528,1024]{2,1,0:T(8,128)(2,1)} %bitcast.155), custom_call_target="tpu_custom_call" | custom-call | bytes 34603008 | tf_op jit(solution)/shard_map/pallas_call | solution.py:274
  1204.3 11.7 shard_map.262
  1216.9 13.2 %shard_map.259 = (f32[1024,2048]{1,0:T(8,128)}, f32[1024,3072]{1,0:T(8,128)}) custom-call(bf16[16,1136,384]{2,1,0:T(8,128)(2,1)} %bitcast.158), custom_call_target="tpu_custom_call" | custom-call | bytes 41877504 | tf_op jit(solution)/shard_map/pallas_call | solution.py:337
  1230.1 2.9 slice_convert_fusion.1
  1234.3 5.0 shard_map.260
  1239.2 3.0 reshape.382
  (346 shorter events, 128.9 us)
Async XLA Ops:
  7.2 89.1 %copy-start = (bf16[1024,576]{0,1:T(8,128)(2,1)S(1)}, bf16[1024,576]{0,1:T(8,128)(2,1)}, u32[]{:S(2)}) copy-start(bf16[1024,576]{0,1:T(8,128)(2,1)} %param.23) | copy-start | bytes 3538948
  7.2 87.5 %all-gather.9.cloned.1.call-start = ((), (), s32[]{:S(2)}) async-start(), calls=%async_computation.8 | async-start | bytes 8912896 | tf_op jit(solution)/shard_map/all_gather | solution.py:457
  9.7 3.5 collective-permute-start
  13.1 81.6 %copy-start.57 = (f32[128]{0:T(128)}, f32[128]{0:T(128)S(1)}, u32[]{:S(2)}) copy-start(f32[128]{0:T(128)S(1)} %rsqrt.38) | copy-start | bytes 1540
  17.6 81.1 %copy-start.55 = (f32[2,1,64,6]{2,1,3,0:T(1,128)S(1)}, f32[2,1,64,6]{2,1,3,0:T(1,128)}, u32[]{:S(2)}) copy-start(f32[2,1,64,6]{2,1,3,0:T(1,128)} %param.20) | copy-start | bytes 9220
  17.6 81.2 %copy-start.56 = (s32[2,1,64,6]{2,1,3,0:T(1,128)S(1)}, s32[2,1,64,6]{2,1,3,0:T(1,128)}, u32[]{:S(2)}) copy-start(s32[2,1,64,6]{2,1,3,0:T(1,128)} %param.19) | copy-start | bytes 9220
  17.7 434.6 %all-gather.13.cloned.1.call-start = ((), (), s32[]{:S(2)}) async-start(), calls=%async_computation.10 | async-start | bytes 8912896 | tf_op jit(solution)/shard_map/all_gather | solution.py:457
  97.6 39.7 %collective-permute-start.1 = (bf16[1024,768]{0,1:T(8,128)(2,1)}, bf16[1024,768]{0,1:T(8,128)(2,1)S(1)}, u32[]{:S(2)}, u32[]{:S(2)}) collective-permute-start(bf16[1024,768]{0,1:T(8,128)(2,1)} %pad_maximum_fusion.7), channel_id=1, source_target_pairs={{16,0},{0,16},{17,1},{1,17},{18,2},{2,18},{19,3},{3,19},{20,4},{4,... | collective-permute-start | bytes 4718600 | tf_op jit(solution)/shard_map/ppermute | solution.py:387
  99.6 18.0 %all-to-all-start = ((f32[16,1,128]{2,1,0:T(1,128)}), f32[16,1,128]{2,1,0:T(1,128)}, u32[]{:S(2)}, u32[]{:S(2)}) async-start(f32[16,1,128]{2,1,0:T(1,128)} %bitcast.2), calls=%async_computation | async-start | bytes 16384 | tf_op jit(solution)/shard_map/all_to_all | solution.py:463
  105.2 31.2 %collective-permute-start.2 = (bf16[256,256]{1,0:T(8,128)(2,1)S(1)}, bf16[256,256]{1,0:T(8,128)(2,1)}, u32[]{:S(2)}, u32[]{:S(2)}) collective-permute-start(bf16[256,256]{1,0:T(8,128)(2,1)S(1)} %get-tuple-element.125), channel_id=1, source_target_pairs={{16,0},{0,16},{17,1},{1,17},{18,2},{2,18},{19,3},{3,19},{20,4},{4,... | collective-permute-start | bytes 393224 | tf_op jit(solution)/shard_map/ppermute | solution.py:387
  108.7 72.7 %collective-permute-start.3 = (bf16[512,2048]{1,0:T(8,128)(2,1)}, bf16[512,2048]{1,0:T(8,128)(2,1)}, u32[]{:S(2)}, u32[]{:S(2)}) collective-permute-start(bf16[512,2048]{1,0:T(8,128)(2,1)} %constant_dynamic-slice_fusion.10), channel_id=1, source_target_pairs={{16,0},{0,16},{17,1},{1,17},{18,2},{2,18},{19,3},{3,19},{20,4},{4,... | collective-permute-start | bytes 6291464 | tf_op jit(solution)/shard_map/ppermute | solution.py:387
  139.3 43.2 %slice-start.5 = ((s8[8388608]{0:T(1024)(128)(4,1)}), s8[4194304]{0:T(1024)(128)(4,1)S(1)}, s32[]{:S(2)}) async-start(s8[8388608]{0:T(1024)(128)(4,1)} %bitcast.210), calls=%async_computation.21 | async-start | bytes 8388608
  139.3 43.1 %slice-start.6 = ((s8[8388608]{0:T(1024)(128)(4,1)}), s8[4194304]{0:T(1024)(128)(4,1)S(1)}, s32[]{:S(2)}) async-start(s8[8388608]{0:T(1024)(128)(4,1)} %bitcast.210), calls=%async_computation.22 | async-start | bytes 8388608
  139.4 53.5 %copy-start.34 = (f32[16,64,128]{2,1,0:T(8,128)S(1)}, f32[16,64,128]{2,1,0:T(8,128)}, u32[]{:S(2)}) copy-start(f32[16,64,128]{2,1,0:T(8,128)} %get-tuple-element.164) | copy-start | bytes 1572868
  139.4 53.5 %copy-start.35 = (f32[16,64,128]{2,1,0:T(8,128)S(1)}, f32[16,64,128]{2,1,0:T(8,128)}, u32[]{:S(2)}) copy-start(f32[16,64,128]{2,1,0:T(8,128)} %get-tuple-element.165) | copy-start | bytes 1572868
  181.3 49.8 %collective-permute-start.4 = (bf16[512,2048]{1,0:T(8,128)(2,1)}, bf16[512,2048]{1,0:T(8,128)(2,1)S(1)}, u32[]{:S(2)}, u32[]{:S(2)}) collective-permute-start(bf16[512,2048]{1,0:T(8,128)(2,1)} %collective-permute-done.3), channel_id=1, source_target_pairs={{0,1},{1,0},{2,3},{3,2},{4,5},{5,4},{6,7},{7,6},{8,9},{9,8},{10,11... | collective-permute-start | bytes 6291464 | tf_op jit(solution)/shard_map/ppermute | solution.py:437
  196.9 9.5 copy-start.49
  198.7 13.3 %copy-start.51 = (f32[1,8,2,128]{3,2,1,0:T(2,128)S(1)}, f32[1,8,2,128]{3,2,1,0:T(2,128)}, u32[]{:S(2)}) copy-start(f32[1,8,2,128]{3,2,1,0:T(2,128)} %get-tuple-element.156) | copy-start | bytes 24580
  208.4 17.4 %all-to-all-start.1 = ((bf16[16,128,128]{1,2,0:T(8,128)(2,1)}), bf16[16,128,128]{1,2,0:T(8,128)(2,1)S(1)}, u32[]{:S(2)}, u32[]{:S(2)}) async-start(bf16[16,128,128]{1,2,0:T(8,128)(2,1)} %copy.152), calls=%async_computation.1 | async-start | bytes 1048576 | tf_op jit(solution)/shard_map/all_to_all | solution.py:463
  211.9 247.5 %all-gather.11.cloned.1.call-start = ((), (), s32[]{:S(2)}) async-start(), calls=%async_computation.9 | async-start | bytes 8912896 | tf_op jit(solution)/shard_map/all_gather | solution.py:457
  212.0 19.8 %copy-start.43 = (f32[1,8,2,128]{3,1,2,0:T(8,128)}, f32[1,8,2,128]{3,1,2,0:T(8,128)S(1)}, u32[]{:S(2)}) copy-start(f32[1,8,2,128]{3,1,2,0:T(8,128)S(1)} %copy.201) | copy-start | bytes 24580
  234.1 411.8 %reduce-scatter.3.cloned.1.call-start = ((), (), s32[]{:S(2)}) async-start(), calls=%async_computation.11 | async-start | bytes 8912896 | tf_op jit(solution)/shard_map/reduce_scatter | solution.py:466
  234.1 213.8 %collective-permute-start.5 = (bf16[704,2048]{1,0:T(8,128)(2,1)}, bf16[704,2048]{1,0:T(8,128)(2,1)}, u32[]{:S(2)}, u32[]{:S(2)}) collective-permute-start(bf16[704,2048]{1,0:T(8,128)(2,1)} %bitcast.186), channel_id=1, source_target_pairs={{16,0},{0,16},{17,1},{1,17},{18,2},{2,18},{19,3},{3,19},{20,4},{4,... | collective-permute-start | bytes 8650760 | tf_op jit(solution)/shard_map/ppermute | solution.py:387
  235.4 242.9 %collective-permute-start.6 = (bf16[1024,2816]{1,0:T(8,128)(2,1)}, bf16[1024,2816]{1,0:T(8,128)(2,1)}, u32[]{:S(2)}, u32[]{:S(2)}) collective-permute-start(bf16[1024,2816]{1,0:T(8,128)(2,1)} %bitcast.212), channel_id=1, source_target_pairs={{16,0},{0,16},{17,1},{1,17},{18,2},{2,18},{19,3},{3,19},{20,4},{4,... | collective-permute-start | bytes 17301512 | tf_op jit(solution)/shard_map/ppermute | solution.py:387
  238.4 207.5 %collective-permute-start.8 = (bf16[1024,352]{0,1:T(8,128)(2,1)S(1)}, bf16[1024,352]{0,1:T(8,128)(2,1)S(1)}, u32[]{:S(2)}, u32[]{:S(2)}) collective-permute-start(bf16[1024,352]{0,1:T(8,128)(2,1)S(1)} %copy.153), channel_id=1, source_target_pairs={{16,0},{0,16},{17,1},{1,17},{18,2},{2,18},{19,3},{3,19},{20,4},{4,... | collective-permute-start | bytes 2162696 | tf_op jit(solution)/shard_map/ppermute | solution.py:387
  241.6 203.4 %collective-permute-start.7 = (bf16[88,2048]{1,0:T(8,128)(2,1)}, bf16[88,2048]{1,0:T(8,128)(2,1)}, u32[]{:S(2)}, u32[]{:S(2)}) collective-permute-start(bf16[88,2048]{1,0:T(8,128)(2,1)} %get-tuple-element.121), channel_id=1, source_target_pairs={{16,0},{0,16},{17,1},{1,17},{18,2},{2,18},{19,3},{3,19},{20,4},{4,... | collective-permute-start | bytes 1081352 | tf_op jit(solution)/shard_map/ppermute | solution.py:387
  445.9 21.4 %copy-start.29 = (bf16[176,2048]{1,0:T(8,128)(2,1)}, bf16[176,2048]{1,0:T(8,128)(2,1)S(1)}, u32[]{:S(2)}) copy-start(bf16[176,2048]{1,0:T(8,128)(2,1)S(1)} %constant_dynamic-update-slice_fusion.1.weight_ref) | copy-start | bytes 2162692
  448.0 11.5 copy-start.21
  459.4 17.7 %slice-start = ((s8[8388608]{0:T(1024)(128)(4,1)}), s8[4194304]{0:T(1024)(128)(4,1)S(1)}, s32[]{:S(2)}) async-start(s8[8388608]{0:T(1024)(128)(4,1)} %bitcast.161), calls=%async_computation.16 | async-start | bytes 8388608
  467.3 9.7 slice-start.1
  480.3 17.2 %copy-start.8 = (bf16[1024,2048]{1,0:T(8,128)(2,1)S(1)}, bf16[1024,2048]{1,0:T(8,128)(2,1)}, u32[]{:S(2)}) copy-start(bf16[1024,2048]{1,0:T(8,128)(2,1)} %fusion) | copy-start | bytes 12582916
  542.4 382.6 %all-gather.15.cloned.1.call-start = ((), (), s32[]{:S(2)}) async-start(), calls=%async_computation.13 | async-start | bytes 8912896 | tf_op jit(solution)/shard_map/all_gather | solution.py:457
  543.0 640.9 %reduce-scatter.5.cloned.1.call-start = ((), (), s32[]{:S(2)}) async-start(), calls=%async_computation.12 | async-start | bytes 8912896 | tf_op jit(solution)/shard_map/reduce_scatter | solution.py:466
  559.7 18.8 %slice-start.2 = ((s8[5767168]{0:T(1024)(128)(4,1)}), s8[1572864]{0:T(1024)(128)(4,1)S(1)}, s32[]{:S(2)}) async-start(s8[5767168]{0:T(1024)(128)(4,1)} %bitcast.164), calls=%async_computation.18 | async-start | bytes 3145728
  570.7 7.8 slice-start.3
  570.7 7.9 copy-start.13
  586.6 59.3 %copy-start.7 = (bf16[2048,352]{1,0:T(8,128)(2,1)S(1)}, bf16[2048,352]{1,0:T(8,128)(2,1)}, u32[]{:S(2)}) copy-start(bf16[2048,352]{1,0:T(8,128)(2,1)} %pad_maximum_fusion.9.units_ref) | copy-start | bytes 4325380
  645.9 541.0 %all-gather.19.cloned.1.call-start = ((), (), s32[]{:S(2)}) async-start(), calls=%async_computation.15 | async-start | bytes 18382848 | tf_op jit(solution)/shard_map/all_gather | solution.py:460
  659.2 25.5 %slice-start.4 = ((f32[352,2048]{1,0:T(8,128)}), f32[352,1024]{1,0:T(8,128)S(1)}, s32[]{:S(2)}) async-start(f32[352,2048]{1,0:T(8,128)} %copy-done.15), calls=%async_computation.20 | async-start | bytes 2883584 | tf_op jit(solution)/shard_map/slice | solution.py:587
  660.3 24.5 %collective-permute-start.15 = (bf16[528,1024]{1,0:T(8,128)(2,1)}, bf16[528,1024]{1,0:T(8,128)(2,1)}, u32[]{:S(2)}, u32[]{:S(2)}) collective-permute-start(bf16[528,1024]{1,0:T(8,128)(2,1)} %pad_maximum_fusion.10), channel_id=1, source_target_pairs={{0,16},{16,0},{1,17},{17,1},{2,18},{18,2},{3,19},{19,3},{4,20},{20... | collective-permute-start | bytes 3244040 | tf_op jit(solution)/shard_map/ppermute | solution.py:390
  662.8 24.7 %copy-start.4 = (f32[128,2048]{1,0:T(8,128)S(1)}, f32[128,2048]{1,0:T(8,128)}, u32[]{:S(2)}) copy-start(f32[128,2048]{1,0:T(8,128)} %copy-done.3) | copy-start | bytes 3145732
  662.8 24.7 %copy-start.42 = (bf16[128,2048]{1,0:T(8,128)(2,1)S(1)}, bf16[128,2048]{1,0:T(8,128)(2,1)}, u32[]{:S(2)}) copy-start(bf16[128,2048]{1,0:T(8,128)(2,1)} %reduce-scatter.3.cloned.1.call-done) | copy-start | bytes 1572868
  662.8 24.7 %copy-start.44 = (f32[1,8,2,128]{3,1,2,0:T(8,128)S(1)}, f32[1,8,2,128]{3,1,2,0:T(8,128)}, u32[]{:S(2)}) copy-start(f32[1,8,2,128]{3,1,2,0:T(8,128)} %copy-done.43) | copy-start | bytes 24580
  693.7 8.5 copy-start.60
  695.5 30.0 %all-to-all-start.2 = ((bf16[16,128,128]{2,1,0:T(8,128)(2,1)}), bf16[16,128,128]{2,1,0:T(8,128)(2,1)S(1)}, u32[]{:S(2)}, u32[]{:S(2)}) async-start(bf16[16,128,128]{2,1,0:T(8,128)(2,1)} %bitcast_bitcast_fusion.1), calls=%async_computation.4 | async-start | bytes 1048576 | tf_op jit(solution)/shard_map/all_to_all | solution.py:463
  740.0 105.9 %all-to-all-start.3 = ((bf16[16,128,512]{1,2,0:T(8,128)(2,1)}), bf16[16,128,512]{1,2,0:T(8,128)(2,1)}, u32[]{:S(2)}, u32[]{:S(2)}) async-start(bf16[16,128,512]{1,2,0:T(8,128)(2,1)} %copy.161), calls=%async_computation.5 | async-start | bytes 4194304 | tf_op jit(solution)/shard_map/all_to_all | solution.py:463
  751.4 93.3 %collective-permute-start.9 = (bf16[512,3072]{1,0:T(8,128)(2,1)}, bf16[512,3072]{1,0:T(8,128)(2,1)}, u32[]{:S(2)}, u32[]{:S(2)}) collective-permute-start(bf16[512,3072]{1,0:T(8,128)(2,1)} %constant_dynamic-slice_fusion.4), channel_id=1, source_target_pairs={{16,0},{0,16},{17,1},{1,17},{18,2},{2,18},{19,3},{3,19},{20,4},{4,... | collective-permute-start | bytes 9437192 | tf_op jit(solution)/shard_map/ppermute | solution.py:387
  755.0 88.8 %collective-permute-start.11 = (bf16[128,4096]{1,0:T(8,128)(2,1)}, bf16[128,4096]{1,0:T(8,128)(2,1)}, u32[]{:S(2)}, u32[]{:S(2)}) collective-permute-start(bf16[128,4096]{1,0:T(8,128)(2,1)} %constant_dynamic-slice_fusion.3), channel_id=1, source_target_pairs={{16,0},{0,16},{17,1},{1,17},{18,2},{2,18},{19,3},{3,19},{20,4},{4,... | collective-permute-start | bytes 3145736 | tf_op jit(solution)/shard_map/ppermute | solution.py:387
  843.8 8.8 collective-permute-start.12
  844.7 21.4 %collective-permute-start.10 = (bf16[512,3072]{1,0:T(8,128)(2,1)}, bf16[512,3072]{1,0:T(8,128)(2,1)}, u32[]{:S(2)}, u32[]{:S(2)}) collective-permute-start(bf16[512,3072]{1,0:T(8,128)(2,1)} %collective-permute-done.9), channel_id=1, source_target_pairs={{0,1},{1,0},{2,3},{3,2},{4,5},{5,4},{6,7},{7,6},{8,9},{9,8},{10,11... | collective-permute-start | bytes 9437192 | tf_op jit(solution)/shard_map/ppermute | solution.py:437
  878.1 30.7 %collective-permute-start.14 = (bf16[16,65,576]{2,0,1:T(8,128)(2,1)}, bf16[16,65,576]{2,0,1:T(8,128)(2,1)S(1)}, u32[]{:S(2)}, u32[]{:S(2)}) collective-permute-start(bf16[16,65,576]{2,0,1:T(8,128)(2,1)} %copy.177), channel_id=1, source_target_pairs={{0,16},{16,0},{1,17},{17,1},{2,18},{18,2},{3,19},{19,3},{4,20},{20... | collective-permute-start | bytes 3594248 | tf_op jit(solution)/shard_map/ppermute | solution.py:390
  880.3 31.8 %all-to-all-start.4 = ((bf16[16,128,128]{2,1,0:T(8,128)(2,1)}), bf16[16,128,128]{2,1,0:T(8,128)(2,1)S(1)}, u32[]{:S(2)}, u32[]{:S(2)}) async-start(bf16[16,128,128]{2,1,0:T(8,128)(2,1)} %bitcast_bitcast_fusion), calls=%async_computation.6 | async-start | bytes 1048576 | tf_op jit(solution)/shard_map/all_to_all | solution.py:463
  908.8 10.8 copy-start.50
  912.1 11.1 copy-start.40
  912.1 60.0 %all-to-all-start.5 = ((bf16[16,65,576]{2,1,0:T(8,128)(2,1)}), bf16[16,65,576]{2,1,0:T(8,128)(2,1)}, u32[]{:S(2)}, u32[]{:S(2)}) async-start(bf16[16,65,576]{2,1,0:T(8,128)(2,1)} %fusion.5), calls=%async_computation.7 | async-start | bytes 2949120 | tf_op jit(solution)/shard_map/all_to_all | solution.py:463
  919.1 296.9 %all-gather.17.cloned.1.call-start = ((), (), s32[]{:S(2)}) async-start(), calls=%async_computation.14 | async-start | bytes 14831616 | tf_op jit(solution)/shard_map/all_gather | solution.py:460
  923.3 7.6 copy-start.37
  932.1 19.1 %collective-permute-start.13 = (bf16[1024,384]{1,0:T(8,128)(2,1)}, bf16[1024,384]{1,0:T(8,128)(2,1)}, u32[]{:S(2)}, u32[]{:S(2)}) collective-permute-start(bf16[1024,384]{1,0:T(8,128)(2,1)} %maximum_maximum_fusion), channel_id=1, source_target_pairs={{0,16},{16,0},{1,17},{17,1},{2,18},{18,2},{3,19},{19,3},{4,20},{20... | collective-permute-start | bytes 2359304 | tf_op jit(solution)/shard_map/ppermute | solution.py:390
  976.1 195.7 %copy-start.14 = (bf16[32,32,2048]{2,1,0:T(8,128)(2,1)S(1)}, bf16[32,32,2048]{2,1,0:T(8,128)(2,1)}, u32[]{:S(2)}) copy-start(bf16[32,32,2048]{2,1,0:T(8,128)(2,1)} %copy-done.12) | copy-start | bytes 12582916
  976.1 195.7 %collective-permute-start.16 = (bf16[1024,2816]{1,0:T(8,128)(2,1)}, bf16[1024,2816]{1,0:T(8,128)(2,1)S(1)}, u32[]{:S(2)}, u32[]{:S(2)}) collective-permute-start(bf16[1024,2816]{1,0:T(8,128)(2,1)} %convolution_convert_fusion), channel_id=1, source_target_pairs={{0,16},{16,0},{1,17},{17,1},{2,18},{18,2},{3,19},{19,3},{4,20},{20... | collective-permute-start | bytes 17301512 | tf_op jit(solution)/shard_map/ppermute | solution.py:390
  977.3 185.8 %collective-permute-start.17 = (bf16[704,2048]{1,0:T(8,128)(2,1)}, bf16[704,2048]{1,0:T(8,128)(2,1)S(1)}, u32[]{:S(2)}, u32[]{:S(2)}) collective-permute-start(bf16[704,2048]{1,0:T(8,128)(2,1)} %convolution_convert_fusion.2), channel_id=1, source_target_pairs={{0,16},{16,0},{1,17},{17,1},{2,18},{18,2},{3,19},{19,3},{4,20},{20... | collective-permute-start | bytes 8650760 | tf_op jit(solution)/shard_map/ppermute | solution.py:390
  1171.8 12.1 copy-start.23
  1171.8 12.1 copy-start.26
  1171.8 12.1 copy-start.54
  (38 other events, 131.2 us)
Sparse Core Ops, SparseCore 0:
  17.8 76.8 all-gather.8
  96.9 72.8 all-gather.12
  234.2 73.8 all-gather.10
  542.6 103.2 reduce-scatter.2
  647.9 87.9 all-gather.14
  740.3 127.8 reduce-scatter.4
  869.8 128.4 all-gather.18
  1001.1 114.2 all-gather.16
